TPU v7x, 256 devices: a whole 4x4x8 slice. The times are simulated.
256 devices in a mesh: grid: 16 (over z, y_lo), chan: 16 (over x, y_hi, core).
Axes of the slice: x: 4, y: 4 (y_hi: 2, y_lo: 2; y = y_hi * 2 + y_lo), z: 8, core: 2. Of those that a mesh axis runs over, the one named last changes fastest.
Arguments:
- spectra: bfloat16 [2, 8, 48, 4096], P(None, None, 'grid', 'chan'), may hold values from -90 to 90, as said below
- travel: int32 [65536, 4096], P('grid', 'chan'), may hold values from 0 to 2047
- quality: int32 [4096], P('chan'), may hold values 0 or 1
Outputs:
- beam_power: float32 [48, 65536], P(None, ('grid', 'chan'))
Inputs may be any that keep to these rules, and one draw needn't show every extreme that they name: `spectra`: spectra of the windows; scales differ between channels and between windows.
All inputs are finite; a program needn't handle non-finite values. No bound on the sum of `quality` on one device may be relied on, other than what follows from the above.
Results may differ from a plain program's by a relative error of at most 0.0012.
Values may be sent and summed in bfloat16 or wider, within the bound.
No kernel may reach another device: no remote copies, remote signals or barrier semaphores. Data moves between devices by JAX's collectives and lax.ppermute only.
A program may use at most 64 MiB of HBM per device.

v0:
```python
import math

import jax
import jax.numpy as jnp
from jax import lax
from jax.sharding import PartitionSpec as P

NFFT = 2048


lowest_bin = 37
bin_spacing = 29


def replica_rows(delay_rows, freq_count):
    freq_bins = lowest_bin + bin_spacing * jnp.arange(freq_count, dtype=jnp.int32)
    phase_index = freq_bins[:, None, None] * delay_rows[None, :, :] % NFFT
    angles = phase_index.astype(jnp.float32) * (2.0 * math.pi / NFFT)
    return jnp.concatenate([jnp.cos(angles), jnp.sin(angles)], axis=2).astype(jnp.bfloat16)


def stacked_spectra(masked):
    real_part = masked[0]
    imag_part = masked[1]
    upper_half = jnp.concatenate([real_part, imag_part], axis=1)
    lower_half = jnp.concatenate([-imag_part, real_part], axis=1)
    return jnp.concatenate([upper_half, lower_half], axis=2)


def beams_for(delay_table, spectra_matrix, freq_count):
    total_rows = delay_table.shape[0]
    chan_width = delay_table.shape[1]
    block_rows = math.gcd(total_rows, 1024)

    def one_block(delay_rows):
        replicas = replica_rows(delay_rows, freq_count)
        beam_terms = jnp.einsum(
            "frk,fwk->rfw", replicas, spectra_matrix, preferred_element_type=jnp.float32
        )
        return beam_terms.reshape(block_rows, -1)

    block_terms = lax.map(
        one_block, delay_table.reshape(total_rows // block_rows, block_rows, chan_width)
    )
    return block_terms.reshape(total_rows, -1)


def per_device(spectra, travel, quality):
    freq_count = spectra.shape[1]
    masked = spectra * quality.astype(jnp.bfloat16)
    channel_count = masked.shape[3] * lax.axis_size("chan")
    gathered = lax.all_gather(masked, "grid", axis=2, tiled=True)
    window_count = gathered.shape[2]
    norm_sum = lax.psum(jnp.sum(gathered.astype(jnp.float32) ** 2, axis=(0, 1, 3)), "chan")
    window_norm = norm_sum / (freq_count * channel_count) + 1e-06
    rows_out = travel.shape[0] // lax.axis_size("chan")
    spectra_matrix = stacked_spectra(gathered)
    beam_sums = lax.psum_scatter(
        beams_for(travel, spectra_matrix, freq_count), "chan", scatter_dimension=0, tiled=True
    )
    energies = jnp.sum(beam_sums.reshape(rows_out, 2 * freq_count, window_count) ** 2, axis=1)
    beam_power = energies / (freq_count * channel_count * window_norm[None, :])
    return beam_power.T


def solution(mesh):
    return jax.shard_map(
        per_device,
        mesh=mesh,
        in_specs=(P(None, None, "grid", "chan"), P("grid", "chan"), P("chan")),
        out_specs=P(None, ("grid", "chan")),
        check_vma=False,
    )
```

profile of v0, /device:TPU:1, one launch (start us, length us, event | category | flops | bytes accessed | tf_op | source)
XLA Modules:
  0.0 362.6 jit_solution(12810021472243952818)
XLA Ops:
  8.0 32.6 %all_gather.3 = bf16[2,8,48,256]{3,1,0,2:T(8,128)(2,1)S(1)} all-gather(bf16[2,8,3,256]{3,1,0,2:T(8,128)(2,1)S(1)} %copy_multiply_fusion), channel_id=1, replica_groups=mesh['grid'=16,'chan'=16] {'grid'}, dimensions={2}, use_global_device_ids=true | all-gather | bytes 417792 | tf_op jit(solution)/shard_map/all_gather | solution.py:52
  41.8 177.9 %while.12 = (s32[]{:T(128)}, f32[4,1024,768]{2,1,0:T(8,128)}, s32[4,1024,256]{2,1,0:T(8,128)}, bf16[8,96,512]{2,1,0:T(8,128)(2,1)}, s32[]{:T(128)}) while((s32[]{:T(128)}, f32[4,1024,768]{2,1,0:T(8,128)}, s32[4,1024,256]{2,1,0:T(8,128)}, bf16[8,96,512]{2,1,0:T(8,128)(2,1)}, s32[]{:T(128)}) %tuple.36), condition=%wide.region_1.0_spmd, body=%wide.region_0.0_spmd.sunk | while | flops 855638016 | bytes 36438156 | solution.py:42
  41.8 1.3 dynamic-slice_bitcast_fusion.2
  43.1 33.8 %cosine_convert_fusion.2 = (bf16[8,1024,256]{2,1,0:T(8,128)(2,1)S(1)}, bf16[8,1024,256]{2,1,0:T(8,128)(2,1)S(1)}) fusion(s32[1024,256]{1,0:T(8,128)S(1)} %dynamic-slice_bitcast_fusion.2, s32[8]{0:T(128)S(1)} %multiply_add_fusion.2), kind=kLoop, calls=%fused_computation.13.clone.1 | loop fusion | flops 33554432 | bytes 9437216 | tf_op jit(solution)/shard_map/convert
  76.9 5.1 %fusion.15 = f32[8,1024,96]{1,2,0:T(8,128)} fusion(bf16[8,96,512]{2,1,0:T(8,128)(2,1)} %get-tuple-element.118, bf16[8,1024,256]{2,1,0:T(8,128)(2,1)S(1)} %get-tuple-element.103, bf16[8,1024,256]{2,1,0:T(8,128)(2,1)S(1)} %get-tuple-element.104), kind=kOutput, calls=%fused_computation.8.clone.1 | convolution fusion | flops 822083584 | bytes 12320768 | tf_op jit(solution)/shard_map/while/body/eval_jaxpr/frk,fwk->rfw/dot_general | solution.py:37
  82.0 2.4 copy.20
  84.4 1.9 constant_dynamic-update-slice_fusion.2
  86.3 1.3 dynamic-slice_bitcast_fusion.2
  87.6 33.8 %cosine_convert_fusion.2 = (bf16[8,1024,256]{2,1,0:T(8,128)(2,1)S(1)}, bf16[8,1024,256]{2,1,0:T(8,128)(2,1)S(1)}) fusion(s32[1024,256]{1,0:T(8,128)S(1)} %dynamic-slice_bitcast_fusion.2, s32[8]{0:T(128)S(1)} %multiply_add_fusion.2), kind=kLoop, calls=%fused_computation.13.clone.1 | loop fusion | flops 33554432 | bytes 9437216 | tf_op jit(solution)/shard_map/convert
  121.4 5.1 %fusion.15 = f32[8,1024,96]{1,2,0:T(8,128)} fusion(bf16[8,96,512]{2,1,0:T(8,128)(2,1)} %get-tuple-element.118, bf16[8,1024,256]{2,1,0:T(8,128)(2,1)S(1)} %get-tuple-element.103, bf16[8,1024,256]{2,1,0:T(8,128)(2,1)S(1)} %get-tuple-element.104), kind=kOutput, calls=%fused_computation.8.clone.1 | convolution fusion | flops 822083584 | bytes 12320768 | tf_op jit(solution)/shard_map/while/body/eval_jaxpr/frk,fwk->rfw/dot_general | solution.py:37
  126.5 2.4 copy.20
  128.9 1.9 constant_dynamic-update-slice_fusion.2
  130.8 1.3 dynamic-slice_bitcast_fusion.2
  132.1 33.8 %cosine_convert_fusion.2 = (bf16[8,1024,256]{2,1,0:T(8,128)(2,1)S(1)}, bf16[8,1024,256]{2,1,0:T(8,128)(2,1)S(1)}) fusion(s32[1024,256]{1,0:T(8,128)S(1)} %dynamic-slice_bitcast_fusion.2, s32[8]{0:T(128)S(1)} %multiply_add_fusion.2), kind=kLoop, calls=%fused_computation.13.clone.1 | loop fusion | flops 33554432 | bytes 9437216 | tf_op jit(solution)/shard_map/convert
  165.9 5.1 %fusion.15 = f32[8,1024,96]{1,2,0:T(8,128)} fusion(bf16[8,96,512]{2,1,0:T(8,128)(2,1)} %get-tuple-element.118, bf16[8,1024,256]{2,1,0:T(8,128)(2,1)S(1)} %get-tuple-element.103, bf16[8,1024,256]{2,1,0:T(8,128)(2,1)S(1)} %get-tuple-element.104), kind=kOutput, calls=%fused_computation.8.clone.1 | convolution fusion | flops 822083584 | bytes 12320768 | tf_op jit(solution)/shard_map/while/body/eval_jaxpr/frk,fwk->rfw/dot_general | solution.py:37
  171.0 2.4 copy.20
  173.4 1.9 constant_dynamic-update-slice_fusion.2
  176.6 33.8 %cosine_convert_fusion.2 = (bf16[8,1024,256]{2,1,0:T(8,128)(2,1)S(1)}, bf16[8,1024,256]{2,1,0:T(8,128)(2,1)S(1)}) fusion(s32[1024,256]{1,0:T(8,128)S(1)} %dynamic-slice_bitcast_fusion.2, s32[8]{0:T(128)S(1)} %multiply_add_fusion.2), kind=kLoop, calls=%fused_computation.13.clone.1 | loop fusion | flops 33554432 | bytes 9437216 | tf_op jit(solution)/shard_map/convert
  210.4 5.1 %fusion.15 = f32[8,1024,96]{1,2,0:T(8,128)} fusion(bf16[8,96,512]{2,1,0:T(8,128)(2,1)} %get-tuple-element.118, bf16[8,1024,256]{2,1,0:T(8,128)(2,1)S(1)} %get-tuple-element.103, bf16[8,1024,256]{2,1,0:T(8,128)(2,1)S(1)} %get-tuple-element.104), kind=kOutput, calls=%fused_computation.8.clone.1 | convolution fusion | flops 822083584 | bytes 12320768 | tf_op jit(solution)/shard_map/while/body/eval_jaxpr/frk,fwk->rfw/dot_general | solution.py:37
  215.5 2.4 copy.20
  217.9 1.8 constant_dynamic-update-slice_fusion.2
  220.2 39.9 %psum.7 = f32[48]{0:T(128)S(1)} all-reduce(f32[48]{0:T(128)S(1)} %multiply_reduce_fusion), channel_id=1, replica_groups=mesh['grid'=16,'chan'=16] {'chan'}, use_global_device_ids=true, to_apply=%region_5.6 | all-reduce | flops 48 | bytes 384 | tf_op jit(solution)/shard_map/psum | solution.py:54
  260.1 93.1 %reduce-scatter.2.cloned.1.call-done = f32[256,768]{1,0:T(8,128)} async-done(((f32[4096,768]{1,0:T(8,128)}), f32[256,768]{1,0:T(8,128)}) %reduce-scatter.2.cloned.1.call-update) | async-done | bytes 786448 | tf_op jit(solution)/shard_map/reduce_scatter | solution.py:58
  353.3 1.5 integer_pow.9
  (19 shorter events, 5.5 us)
Async XLA Ops:
  6.5 346.7 %reduce-scatter.2.cloned.1.call-start = ((), (), s32[]{:S(2)}) async-start(), calls=%async_computation.1 | async-start | bytes 13369344 | tf_op jit(solution)/shard_map/reduce_scatter | solution.py:58
Sparse Core Ops, SparseCore 0:
  219.9 133.3 reduce-scatter.1
where the time goes:
time: 363 us
  other arithmetic  139 us (38%)
  waiting for transfers between devices  93.2 us (26%)
  blocking collectives  72.5 us (20%)
  local copies, waits for them, and re-layouts  23.6 us (7%)
  matrix products  20.4 us (6%)
  between operations  13.4 us (4%)
    another operation x4, other arithmetic  135 us
    reduce_scatter x1, waiting for transfers between devices, per_device(): lax.psum_scatter(beams_for(travel, spectra_matrix, freq_count), 'chan', s...  93.1 us
    psum x1, blocking collectives, per_device(): lax.psum(jnp.sum(gathered.astype(jnp.float32) ** 2, axis=(0, 1, 3)), 'chan')  39.9 us
    all_gather x1, blocking collectives, per_device(): gathered = lax.all_gather(masked, 'grid', axis=2, tiled=True)  32.6 us
    dot_general x4, matrix products, one_block(): jnp.einsum('frk,fwk->rfw', replicas, spectra_matrix, preferred_element_ty...  20.4 us
    dynamic_update_slice x8, local copies, waits for them, and re-layouts, beams_for(): lax.map(one_block, delay_table.reshape(total_rows // block_rows, block_ro...  17 us
  transfers between devices with their start and end apart: 1, of which 1 were waited for; matrix products, arithmetic and copies ran while one was open for 0% of the time, Pallas kernels for 0%

commit v1 on v0

v1 whole, which is shorter than its diff:
```python
import functools

import jax
import jax.numpy as jnp
import numpy as np
from jax import lax
from jax.experimental import pallas as pl
from jax.experimental.pallas import tpu as pltpu
from jax.sharding import Mesh, PartitionSpec as P

NFFT = 2048
lowest_bin = 37
bin_spacing = 29
f32 = jnp.float32
bf16 = jnp.bfloat16

NF = 8
ROWS = 256
CH = 256
PIECES = 4
COLS = 96
FSTEP = 4
TILE = 16


def series_coefficients():
    nodes = np.cos(np.linspace(0, np.pi, 4002)) / 8
    squares = nodes**2
    angles = 2 * np.pi * nodes
    sine = np.linalg.lstsq(squares[:, None] ** np.arange(4), np.sin(angles) / nodes, rcond=None)[0]
    cosine = np.linalg.lstsq(squares[:, None] ** np.arange(5), np.cos(angles), rcond=None)[0]
    return [np.float32(v) for v in sine], [np.float32(v) for v in cosine]


SINE, COSINE = series_coefficients()


def horner(coefficients, value):
    total = coefficients[-1]
    for coefficient in coefficients[-2::-1]:
        total = coefficient + value * total
    return total


def unit_circle(turns_times, multiple):
    turns = turns_times * np.float32(multiple / NFFT)
    magic = np.float32(1.5 * 2**23)
    part = turns - ((turns + magic) - magic)
    quarter = part * np.float32(0.25)
    square = quarter * quarter
    sine = quarter * horner(SINE, square)
    cosine = horner(COSINE, square)
    for _ in range(2):
        twice = sine + sine
        sine, cosine = twice * cosine, np.float32(1.0) - twice * sine
    return cosine, sine


def replica_tiles(tau):
    delay = tau.astype(f32)
    c0, s0 = unit_circle(delay, lowest_bin)
    cd, sd = unit_circle(delay, bin_spacing)
    cosines = [c0, c0 * cd - s0 * sd]
    sines = [s0, s0 * cd + c0 * sd]
    twice = cd + cd
    for _ in range(2, NF):
        cosines.append(twice * cosines[-1] - cosines[-2])
        sines.append(twice * sines[-1] - sines[-2])
    return cosines, sines


def beams_kernel(place, t0, t1, t2, t3, w_ref, norm_ref, out_ref, rep_a, rep_b, total, *, with_norm):
    pieces = [t0, t1, t2, t3]
    reps = [rep_a, rep_b]
    steps = NF // FSTEP
    chunk = ROWS // steps

    def fill(piece, step, rep):
        for half in range(CH // 128):
            for tile in range(chunk // TILE):
                rows = pl.ds(pl.multiple_of(step * chunk + tile * TILE, TILE), TILE)
                tau = pieces[piece][0, rows, half * 128 : (half + 1) * 128].astype(jnp.int32)
                cosines, sines = replica_tiles(tau)
                for f in range(NF):
                    rep[f, rows, half * 128 : (half + 1) * 128] = cosines[f].astype(bf16)
                    rep[f, rows, CH + half * 128 : CH + (half + 1) * 128] = sines[f].astype(bf16)

    def multiply(piece, step, rep):
        for q in range(FSTEP):
            f = step * FSTEP + q
            part = lax.dot_general(
                rep[f], w_ref[f, piece], (((1,), (1,)), ((), ())), preferred_element_type=f32
            )
            total[f] = part if piece == 0 else total[f] + part

    def loop(body):
        lax.fori_loop(0, steps, lambda step, carry: (body(step), carry)[1], 0)

    loop(lambda step: fill(0, step, reps[0]))
    for piece in range(PIECES):
        def body(step, piece=piece):
            multiply(piece, step, reps[piece % 2])
            if piece < PIECES - 1:
                fill(piece + 1, step, reps[(piece + 1) % 2])
        loop(body)
    for part in range(ROWS // 128):
        rows = slice(part * 128, (part + 1) * 128)
        joined = jnp.concatenate([total[f, rows] for f in range(NF)], axis=1)
        out_ref[rows] = joined.astype(out_ref.dtype)
    if with_norm:
        out_ref[ROWS : ROWS + 16] = norm_ref[...]


def beams_block(place, pieces, weights, norm_rows, shift, out_dtype):
    with_norm = shift != 0
    out_rows = ROWS + 16 if with_norm else ROWS
    piece = pl.BlockSpec((1, ROWS, CH), lambda i, p: ((p[0] + shift) % 4, 0, 0))
    vmem = pl.BlockSpec(memory_space=pltpu.VMEM)
    return pl.pallas_call(
        functools.partial(beams_kernel, with_norm=with_norm),
        grid_spec=pltpu.PrefetchScalarGridSpec(
            num_scalar_prefetch=1,
            grid=(1,),
            in_specs=[piece, piece, piece, piece, vmem, pl.BlockSpec((16, NF * COLS), lambda i, p: (0, 0))],
            out_specs=pl.BlockSpec((out_rows, NF * COLS), lambda i, p: (0, 0)),
            scratch_shapes=[
                pltpu.VMEM((NF, ROWS, 2 * CH), bf16),
                pltpu.VMEM((NF, ROWS, 2 * CH), bf16),
                pltpu.VMEM((NF, ROWS, COLS), f32),
            ],
        ),
        out_shape=jax.ShapeDtypeStruct((out_rows, NF * COLS), out_dtype),
        cost_estimate=pl.CostEstimate(flops=6_000_000_000, bytes_accessed=4_000_000, transcendentals=0),
        compiler_params=pltpu.CompilerParams(vmem_limit_bytes=24 << 20),
        name=f"beams_{shift}",
    )(place, *pieces, weights, norm_rows)


def prepare_kernel(place, own_ref, other_ref, w_ref, norm_ref, wide):
    squares = jnp.zeros((COLS, CH), f32)
    for piece in range(PIECES):
        source = own_ref if piece % 2 == 0 else other_ref
        block = place[1] ^ (piece // 2)
        for g in range(16):
            for half in range(CH // 128):
                lanes = slice(half * 128, (half + 1) * 128)
                wide[half, g * 48 : (g + 1) * 48, :] = source[g, block, :, lanes].astype(f32)
        for f in range(NF):
            parts = [
                [
                    jnp.concatenate(
                        [
                            wide[half, pl.ds(p * 24 + f * 3 + i, 16, stride=48), :]
                            for half in range(CH // 128)
                        ],
                        axis=1,
                    )
                    for i in range(3)
                ]
                for p in range(2)
            ]
            real = jnp.concatenate(parts[0], axis=0)
            imag = jnp.concatenate(parts[1], axis=0)
            both = jnp.concatenate([real, imag], axis=0)
            squares = squares + both * both
            w_ref[f, piece, :, 0:CH] = both.astype(bf16)
            w_ref[f, piece, :, CH : 2 * CH] = jnp.concatenate([-imag, real], axis=0).astype(bf16)
    sums = lax.dot_general(
        jnp.ones((16, CH), f32), squares, (((1,), (1,)), ((), ())),
        preferred_element_type=f32, precision=lax.Precision.HIGHEST,
    )
    high = sums.astype(bf16).astype(f32)
    middle = (sums - high).astype(bf16).astype(f32)
    low = sums - high - middle
    row = lax.broadcasted_iota(jnp.int32, sums.shape, 0)
    zero = jnp.zeros_like(sums)
    split = jnp.where(row == 0, high, jnp.where(row == 1, middle, jnp.where(row == 2, low, zero)))
    norm_ref[...] = jnp.concatenate([split] + [zero] * (NF - 1), axis=1).astype(bf16)


def prepare(place, own, other):
    whole = pl.BlockSpec(own.shape, lambda i, p: (0, 0, 0, 0))
    return pl.pallas_call(
        prepare_kernel,
        grid_spec=pltpu.PrefetchScalarGridSpec(
            num_scalar_prefetch=1,
            grid=(1,),
            in_specs=[whole, whole],
            out_specs=[
                pl.BlockSpec(memory_space=pltpu.VMEM),
                pl.BlockSpec((16, NF * COLS), lambda i, p: (0, 0)),
            ],
            scratch_shapes=[pltpu.VMEM((CH // 128, 768, 128), f32)],
        ),
        out_shape=[
            jax.ShapeDtypeStruct((NF, PIECES, COLS, 2 * CH), bf16),
            jax.ShapeDtypeStruct((16, NF * COLS), bf16),
        ],
        compiler_params=pltpu.CompilerParams(vmem_limit_bytes=24 << 20),
        name="prepare",
    )(place, own, other)


def selection():
    column = np.arange(NF * COLS)
    slot = column % 48
    window = 3 * (slot % 16) + slot // 16
    return (np.arange(48)[:, None] == window[None, :]).astype(np.float32)


def finish_kernel(r1, r2, r3, own_ref, norm_ref, pick_ref, out_ref, *, count):
    def total_of(rows):
        return r1[rows].astype(f32) + r2[rows].astype(f32) + r3[rows].astype(f32)

    def pick(values):
        return lax.dot_general(
            pick_ref[...], values, (((1,), (1,)), ((), ())),
            preferred_element_type=f32, precision=lax.Precision.HIGHEST,
        )

    beams = own_ref[...] + total_of(slice(0, ROWS))
    norm_rows = norm_ref[...].astype(f32) + total_of(slice(ROWS, ROWS + 16))
    norm_sum = jnp.sum(pick(norm_rows), axis=1, keepdims=True)
    window_norm = norm_sum / count + 1e-06
    out_ref[...] = pick(beams * beams) / (count * window_norm)


def finish(received, own, norm_rows, count):
    pick = jnp.asarray(selection())
    return pl.pallas_call(
        functools.partial(finish_kernel, count=count),
        out_shape=jax.ShapeDtypeStruct((48, ROWS), f32),
        compiler_params=pltpu.CompilerParams(vmem_limit_bytes=24 << 20),
        name="finish",
    )(*received, own, norm_rows, pick)


def per_device(spectra, travel, quality):
    masked = (spectra * quality.astype(bf16)).reshape(48, CH)
    place = jnp.stack([lax.axis_index("x"), lax.axis_index("yh"), lax.axis_index("c")]).astype(jnp.int32)
    yh, core = place[1], place[2]
    blocks = travel.reshape(4, 2, 2, ROWS, CH)

    def travel_for(flip_y, flip_c):
        return lax.dynamic_slice(
            blocks, (0, yh ^ flip_y, core ^ flip_c, 0, 0), (4, 1, 1, ROWS, CH)
        ).reshape(4, ROWS, CH).astype(jnp.int16)

    parts = [travel_for(flip // 2, flip % 2) for flip in range(4)]
    copies = jnp.broadcast_to(masked[None], (32, 48, CH))
    copies, *parts = lax.optimization_barrier((copies, *parts))
    pieces = parts[:1] + [
        lax.ppermute(parts[flip], ("yh", "c"), [(i, i ^ flip) for i in range(4)])
        for flip in (1, 2, 3)
    ]
    own = lax.all_to_all(copies, ("z", "yl", "yh"), 0, 0, tiled=True).reshape(16, 2, 48, CH)
    own, pieces[2], pieces[3] = lax.optimization_barrier((own, pieces[2], pieces[3]))
    other = lax.ppermute(own, "c", [(0, 1), (1, 0)])
    weights, norm_rows = prepare(place, own, other)
    received = []
    for shift in (2, 1, 3):
        beams = beams_block(place, pieces, weights, norm_rows, shift, bf16)
        received.append(lax.ppermute(beams, "x", [(i, (i + shift) % 4) for i in range(4)]))
    mine = beams_block(place, pieces, weights, norm_rows, 0, f32)
    return finish(received, mine, norm_rows, float(NF * CH * 16))


def solution(mesh):
    fine = Mesh(mesh.devices.reshape(8, 2, 4, 2, 2), ("z", "yl", "x", "yh", "c"))
    return jax.shard_map(
        per_device,
        mesh=fine,
        in_specs=(
            P(None, None, ("z", "yl"), ("x", "yh", "c")),
            P(("z", "yl"), ("x", "yh", "c")),
            P(("x", "yh", "c")),
        ),
        out_specs=P(None, ("z", "yl", "x", "yh", "c")),
        check_vma=False,
    )
```

time: 363 us -> 101 us (0.28)
  other arithmetic: 139 us -> 4.75 us
  blocking collectives: 72.5 us -> 0 us
  waiting for transfers between devices: 93.2 us -> 34.2 us
  Pallas kernels: 0 us -> 37 us
  local copies, waits for them, and re-layouts: 23.6 us -> 0.99 us
  starting transfers between devices: 0.01 us -> 22.6 us
  matrix products: 20.4 us -> 0 us
  between operations: 13.4 us -> 0.11 us
    another operation x4 -> x1, other arithmetic: 135 us -> 0.08 us  [per_device(): jnp.stack([lax.axis_index('x'), lax.axis_index('yh'), lax.axis_index('c')])]
    reduce_scatter x1 -> x0, waiting for transfers between devices: 93.1 us -> none  [per_device(): lax.psum_scatter(beams_for(travel, spectra_matrix, freq_count), 'chan', s...]
    psum x1 -> x0, blocking collectives: 39.9 us -> none  [per_device(): lax.psum(jnp.sum(gathered.astype(jnp.float32) ** 2, axis=(0, 1, 3)), 'chan')]
    pallas_call x0 -> x6, Pallas kernels: none -> 37 us  [the longest x4 33.5 us: beams_block(): pl.pallas_call(functools.partial(beams_kernel, with_norm=with_norm), grid...]
    ppermute x0 -> x7, waiting for transfers between devices: none -> 34.2 us  [the longest x3 31.7 us: per_device(): lax.ppermute(parts[flip], ('yh', 'c'), [(i, i ^ flip) for i in range(4)])]
    all_gather x1 -> x0, blocking collectives: 32.6 us -> none  [per_device(): gathered = lax.all_gather(masked, 'grid', axis=2, tiled=True)]
    dot_general x4 -> x0, matrix products: 20.4 us -> none  [one_block(): jnp.einsum('frk,fwk->rfw', replicas, spectra_matrix, preferred_element_ty...]
    dynamic_update_slice x8 -> x0, local copies, waits for them, and re-layouts: 17 us -> none  [beams_for(): lax.map(one_block, delay_table.reshape(total_rows // block_rows, block_ro...]
  transfers between devices with their start and end apart: 1 -> 8, of which waited for: 1 -> 3; matrix products, arithmetic and copies ran while one was open for 0% -> 0% of each run, Pallas kernels for 0% -> 27%
where the time goes in v1:
time: 101 us; the launch traced here: 99.6 us
  Pallas kernels  37 us (37%)
  waiting for transfers between devices  34.2 us (34%)
  starting transfers between devices  22.6 us (22%)
  other arithmetic  4.75 us (5%)
    pallas_call x4, Pallas kernels, beams_block(): pl.pallas_call(functools.partial(beams_kernel, with_norm=with_norm), grid...  33.5 us
    ppermute x3, waiting for transfers between devices, per_device(): lax.ppermute(parts[flip], ('yh', 'c'), [(i, i ^ flip) for i in range(4)])  31.7 us
    all_to_all x1, starting transfers between devices, per_device(): lax.all_to_all(copies, ('z', 'yl', 'yh'), 0, 0, tiled=True)  12 us
    ppermute x3, starting transfers between devices, per_device(): lax.ppermute(beams, 'x', [(i, (i + shift) % 4) for i in range(4)])  5.85 us
    ppermute x3, starting transfers between devices, per_device(): lax.ppermute(parts[flip], ('yh', 'c'), [(i, i ^ flip) for i in range(4)])  4.69 us
    convert_element_type x1, other arithmetic, travel_for(): return lax.dynamic_slice(blocks, (0, yh ^ flip_y, core ^ flip_c, 0, 0), (...  3.25 us
    ppermute x1, waiting for transfers between devices, per_device(): other = lax.ppermute(own, 'c', [(0, 1), (1, 0)])  2.45 us
  transfers between devices with their start and end apart: 8, of which 3 were waited for; matrix products, arithmetic and copies ran while one was open for 0% of the time, Pallas kernels for 27%

profile of v1, /device:TPU:1, one launch (start us, length us, event | category | flops | bytes accessed | tf_op | source)
XLA Modules:
  0.0 99.6 jit_solution(2270923546585948756)
XLA Ops:
  0.0 0.7 convert_element_type.27
  0.7 0.7 broadcast_multiply_fusion
  1.5 3.3 %fusion.3 = (s16[4,256,256]{2,1,0:T(8,128)(2,1)S(1)}, s16[4,256,256]{2,1,0:T(8,128)(2,1)S(1)}, s16[4,256,256]{2,1,0:T(8,128)(2,1)}, s16[4,256,256]{2,1,0:T(8,128)(2,1)S(1)}) fusion(s32[4,2,2,256,256]{4,3,2,1,0:T(8,128)} %bitcast.31, s32[]{:T(128)S(6)} %select_n.19, s32[]{:T(128)S(6)} %select_n.18, s32[]{:T(128)S(6)} %select_n.17, s32[]{:T(128)S(6)} %select_n.16), kind=kLoop, calls=%fused_computation.7 | loop fusion | flops 1048576 | bytes 6291472 | tf_op jit(solution)/shard_map/convert_element_type | solution.py:247
  4.7 0.9 broadcast_in_dim.9
  5.7 12.0 %all-to-all-start = ((bf16[32,48,256]{2,1,0:T(8,128)(2,1)}), bf16[32,48,256]{2,1,0:T(8,128)(2,1)S(1)}, u32[]{:S(2)}, u32[]{:S(2)}) async-start(bf16[32,48,256]{2,1,0:T(8,128)(2,1)} %broadcast_in_dim.9), calls=%async_computation | async-start | bytes 1572864 | tf_op jit(solution)/shard_map/all_to_all | solution.py:256
  17.7 2.8 %collective-permute-start.1 = (s16[4,256,256]{2,1,0:T(8,128)(2,1)S(1)}, s16[4,256,256]{2,1,0:T(8,128)(2,1)S(1)}, u32[]{:S(2)}, u32[]{:S(2)}) collective-permute-start(s16[4,256,256]{2,1,0:T(8,128)(2,1)S(1)} %get-tuple-element.18), channel_id=1, source_target_pairs={{0,2},{1,3},{2,0},{3,1},{4,6},{5,7},{6,4},{7,5},{8,10},{9,11},{10,... | collective-permute-start | bytes 1572872 | tf_op jit(solution)/shard_map/ppermute | solution.py:253
  20.5 1.4 %collective-permute-start.2 = (s16[4,256,256]{2,1,0:T(8,128)(2,1)S(1)}, s16[4,256,256]{2,1,0:T(8,128)(2,1)S(1)}, u32[]{:S(2)}, u32[]{:S(2)}) collective-permute-start(s16[4,256,256]{2,1,0:T(8,128)(2,1)S(1)} %get-tuple-element.19), channel_id=1, source_target_pairs={{0,3},{1,2},{2,1},{3,0},{4,7},{5,6},{6,5},{7,4},{8,11},{9,10},{10,... | collective-permute-start | bytes 1572872 | tf_op jit(solution)/shard_map/ppermute | solution.py:253
  21.9 18.9 %collective-permute-done.1.t2 = s16[4,256,256]{2,1,0:T(8,128)(2,1)S(1)} collective-permute-done((s16[4,256,256]{2,1,0:T(8,128)(2,1)S(1)}, s16[4,256,256]{2,1,0:T(8,128)(2,1)S(1)}, u32[]{:S(2)}, u32[]{:S(2)}) %collective-permute-start.1) | collective-permute-done | bytes 524320 | tf_op jit(solution)/shard_map/ppermute | solution.py:253
  40.8 12.8 %collective-permute-done.2.t3 = s16[4,256,256]{2,1,0:T(8,128)(2,1)S(1)} collective-permute-done((s16[4,256,256]{2,1,0:T(8,128)(2,1)S(1)}, s16[4,256,256]{2,1,0:T(8,128)(2,1)S(1)}, u32[]{:S(2)}, u32[]{:S(2)}) %collective-permute-start.2) | collective-permute-done | bytes 524320 | tf_op jit(solution)/shard_map/ppermute | solution.py:253
  53.6 0.0 all-to-all-done
  53.6 0.5 collective-permute-start
  54.1 0.1 pad_add_fusion.place
  54.2 2.4 %collective-permute-done.3.other_ref = bf16[16,2,48,256]{3,2,1,0:T(8,128)(2,1)S(1)} collective-permute-done((bf16[16,2,48,256]{3,2,1,0:T(8,128)(2,1)S(1)}, bf16[16,2,48,256]{3,2,1,0:T(8,128)(2,1)S(1)}, u32[]{:S(2)}, u32[]{:S(2)}) %collective-permute-start.3) | collective-permute-done | bytes 786464 | tf_op jit(solution)/shard_map/ppermute | solution.py:258
  56.6 1.9 %prepare.1 = (bf16[8,4,96,512]{3,2,1,0:T(8,128)(2,1)S(1)}, bf16[16,768]{1,0:T(8,128)(2,1)S(1)}) custom-call(s32[3]{0:T(128)S(1)} %pad_add_fusion.place, bf16[16,2,48,256]{3,2,1,0:T(8,128)(2,1)S(1)} %bitcast.30, bf16[16,2,48,256]{3,2,1,0:T(8,128)(2,1)S(1)} %collective-permute-done.3.other_ref), custom_call_target="tpu_custom_call" | custom-call | tf_op jit(solution)/shard_map/prepare/pallas_call | solution.py:183
  58.5 0.0 collective-permute-done.t1
  58.6 8.3 %beams_2.1 = bf16[272,768]{1,0:T(8,128)(2,1)S(1)} custom-call(s32[3]{0:T(128)S(1)} %pad_add_fusion.place, s16[4,256,256]{2,1,0:T(8,128)(2,1)S(1)} %get-tuple-element.15.t0, s16[4,256,256]{2,1,0:T(8,128)(2,1)} %collective-permute-done.t1, s16[4,256,256]{2,1,0:T(8,128)(2,1)S(1)} %collective-permute-done.1.t2, ...), custom_call_target="tpu_custom_call" | custom-call | flops 6000000000 | bytes 4000000 | tf_op jit(solution)/shard_map/beams_2/pallas_call | solution.py:119
  66.9 2.8 %collective-permute-start.4 = (bf16[272,768]{1,0:T(8,128)(2,1)S(1)}, bf16[272,768]{1,0:T(8,128)(2,1)S(1)}, u32[]{:S(2)}, u32[]{:S(2)}) collective-permute-start(bf16[272,768]{1,0:T(8,128)(2,1)S(1)} %beams_2.1), channel_id=1, source_target_pairs={{0,8},{4,12},{8,0},{12,4},{1,9},{5,13},{9,1},{13,5},{2,10},{6,14},... | collective-permute-start | bytes 1253384 | tf_op jit(solution)/shard_map/ppermute | solution.py:263
  69.8 8.3 %beams_1.1 = bf16[272,768]{1,0:T(8,128)(2,1)S(1)} custom-call(s32[3]{0:T(128)S(1)} %pad_add_fusion.place, s16[4,256,256]{2,1,0:T(8,128)(2,1)S(1)} %get-tuple-element.15.t0, s16[4,256,256]{2,1,0:T(8,128)(2,1)} %collective-permute-done.t1, s16[4,256,256]{2,1,0:T(8,128)(2,1)S(1)} %collective-permute-done.1.t2, ...), custom_call_target="tpu_custom_call" | custom-call | flops 6000000000 | bytes 4000000 | tf_op jit(solution)/shard_map/beams_1/pallas_call | solution.py:119
  78.1 0.6 collective-permute-start.5
  78.7 8.3 %beams_3.1 = bf16[272,768]{1,0:T(8,128)(2,1)S(1)} custom-call(s32[3]{0:T(128)S(1)} %pad_add_fusion.place, s16[4,256,256]{2,1,0:T(8,128)(2,1)S(1)} %get-tuple-element.15.t0, s16[4,256,256]{2,1,0:T(8,128)(2,1)} %collective-permute-done.t1, s16[4,256,256]{2,1,0:T(8,128)(2,1)S(1)} %collective-permute-done.1.t2, ...), custom_call_target="tpu_custom_call" | custom-call | flops 6000000000 | bytes 4000000 | tf_op jit(solution)/shard_map/beams_3/pallas_call | solution.py:119
  87.0 0.0 copy-start
  87.0 2.4 %collective-permute-start.6 = (bf16[272,768]{1,0:T(8,128)(2,1)S(1)}, bf16[272,768]{1,0:T(8,128)(2,1)S(1)}, u32[]{:S(2)}, u32[]{:S(2)}) collective-permute-start(bf16[272,768]{1,0:T(8,128)(2,1)S(1)} %beams_3.1), channel_id=1, source_target_pairs={{0,12},{4,0},{8,4},{12,8},{1,13},{5,1},{9,5},{13,9},{2,14},{6,2},{... | collective-permute-start | bytes 1253384 | tf_op jit(solution)/shard_map/ppermute | solution.py:263
  89.5 8.4 %beams_0.1.own_ref = f32[256,768]{1,0:T(8,128)S(1)} custom-call(s32[3]{0:T(128)S(1)} %pad_add_fusion.place, s16[4,256,256]{2,1,0:T(8,128)(2,1)S(1)} %get-tuple-element.15.t0, s16[4,256,256]{2,1,0:T(8,128)(2,1)} %collective-permute-done.t1, s16[4,256,256]{2,1,0:T(8,128)(2,1)S(1)} %collective-permute-done.1.t2, ...), custom_call_target="tpu_custom_call" | custom-call | flops 6000000000 | bytes 4000000 | tf_op jit(solution)/shard_map/beams_0/pallas_call | solution.py:119
  98.0 1.7 %finish.1 = f32[48,256]{1,0:T(8,128)} custom-call(bf16[272,768]{1,0:T(8,128)(2,1)S(1)} %collective-permute-done.4.r1, bf16[272,768]{1,0:T(8,128)(2,1)S(1)} %collective-permute-done.5.r2, bf16[272,768]{1,0:T(8,128)(2,1)S(1)} %collective-permute-done.6.r3, f32[256,768]{1,0:T(8,128)S(1)} %beams_0.1.own_ref, bf16[16,768]{1,0:T(8,128)(2,1)S(1)} %get-tuple-element.24.norm_ref, ...), custom_call_target="tpu_custom_call" | custom-call | tf_op jit(solution)/shard_map/finish/pallas_call | solution.py:230
  (7 shorter events, 0.1 us)
Async XLA Ops:
  5.7 47.9 %all-to-all-start = ((bf16[32,48,256]{2,1,0:T(8,128)(2,1)}), bf16[32,48,256]{2,1,0:T(8,128)(2,1)S(1)}, u32[]{:S(2)}, u32[]{:S(2)}) async-start(bf16[32,48,256]{2,1,0:T(8,128)(2,1)} %broadcast_in_dim.9), calls=%async_computation | async-start | bytes 1572864 | tf_op jit(solution)/shard_map/all_to_all | solution.py:256
  17.7 23.1 %collective-permute-start.1 = (s16[4,256,256]{2,1,0:T(8,128)(2,1)S(1)}, s16[4,256,256]{2,1,0:T(8,128)(2,1)S(1)}, u32[]{:S(2)}, u32[]{:S(2)}) collective-permute-start(s16[4,256,256]{2,1,0:T(8,128)(2,1)S(1)} %get-tuple-element.18), channel_id=1, source_target_pairs={{0,2},{1,3},{2,0},{3,1},{4,6},{5,7},{6,4},{7,5},{8,10},{9,11},{10,... | collective-permute-start | bytes 1572872 | tf_op jit(solution)/shard_map/ppermute | solution.py:253
  20.5 33.0 %collective-permute-start.2 = (s16[4,256,256]{2,1,0:T(8,128)(2,1)S(1)}, s16[4,256,256]{2,1,0:T(8,128)(2,1)S(1)}, u32[]{:S(2)}, u32[]{:S(2)}) collective-permute-start(s16[4,256,256]{2,1,0:T(8,128)(2,1)S(1)} %get-tuple-element.19), channel_id=1, source_target_pairs={{0,3},{1,2},{2,1},{3,0},{4,7},{5,6},{6,5},{7,4},{8,11},{9,10},{10,... | collective-permute-start | bytes 1572872 | tf_op jit(solution)/shard_map/ppermute | solution.py:253
  53.6 3.0 %collective-permute-start.3 = (bf16[16,2,48,256]{3,2,1,0:T(8,128)(2,1)S(1)}, bf16[16,2,48,256]{3,2,1,0:T(8,128)(2,1)S(1)}, u32[]{:S(2)}, u32[]{:S(2)}) collective-permute-start(bf16[16,2,48,256]{3,2,1,0:T(8,128)(2,1)S(1)} %bitcast.29), channel_id=1, source_target_pairs={{0,1},{1,0},{2,3},{3,2},{4,5},{5,4},{6,7},{7,6},{8,9},{9,8},{10,11... | collective-permute-start | bytes 2359304 | tf_op jit(solution)/shard_map/ppermute | solution.py:258
  53.6 5.0 %collective-permute-start = (s16[4,256,256]{2,1,0:T(8,128)(2,1)}, s16[4,256,256]{2,1,0:T(8,128)(2,1)}, u32[]{:S(2)}, u32[]{:S(2)}) collective-permute-start(s16[4,256,256]{2,1,0:T(8,128)(2,1)} %get-tuple-element.16), channel_id=1, source_target_pairs={{0,1},{1,0},{2,3},{3,2},{4,5},{5,4},{6,7},{7,6},{8,9},{9,8},{10,11... | collective-permute-start | bytes 1572872 | tf_op jit(solution)/shard_map/ppermute | solution.py:253
  66.9 31.0 %collective-permute-start.4 = (bf16[272,768]{1,0:T(8,128)(2,1)S(1)}, bf16[272,768]{1,0:T(8,128)(2,1)S(1)}, u32[]{:S(2)}, u32[]{:S(2)}) collective-permute-start(bf16[272,768]{1,0:T(8,128)(2,1)S(1)} %beams_2.1), channel_id=1, source_target_pairs={{0,8},{4,12},{8,0},{12,4},{1,9},{5,13},{9,1},{13,5},{2,10},{6,14},... | collective-permute-start | bytes 1253384 | tf_op jit(solution)/shard_map/ppermute | solution.py:263
  78.1 19.8 %collective-permute-start.5 = (bf16[272,768]{1,0:T(8,128)(2,1)S(1)}, bf16[272,768]{1,0:T(8,128)(2,1)S(1)}, u32[]{:S(2)}, u32[]{:S(2)}) collective-permute-start(bf16[272,768]{1,0:T(8,128)(2,1)S(1)} %beams_1.1), channel_id=1, source_target_pairs={{0,4},{4,8},{8,12},{12,0},{1,5},{5,9},{9,13},{13,1},{2,6},{6,10},{... | collective-permute-start | bytes 1253384 | tf_op jit(solution)/shard_map/ppermute | solution.py:263
  87.0 10.9 %copy-start = (f32[48,768]{1,0:T(8,128)S(1)}, f32[48,768]{1,0:T(8,128)}, u32[]{:S(2)}) copy-start(f32[48,768]{1,0:T(8,128)} %constant.19.clone.pick_ref) | copy-start | bytes 442372
  87.0 10.9 %collective-permute-start.6 = (bf16[272,768]{1,0:T(8,128)(2,1)S(1)}, bf16[272,768]{1,0:T(8,128)(2,1)S(1)}, u32[]{:S(2)}, u32[]{:S(2)}) collective-permute-start(bf16[272,768]{1,0:T(8,128)(2,1)S(1)} %beams_3.1), channel_id=1, source_target_pairs={{0,12},{4,0},{8,4},{12,8},{1,13},{5,1},{9,5},{13,9},{2,14},{6,2},{... | collective-permute-start | bytes 1253384 | tf_op jit(solution)/shard_map/ppermute | solution.py:263

commit v2 on v0

v2 whole, which is shorter than its diff:
```python
import functools

import jax
import jax.numpy as jnp
import numpy as np
from jax import lax
from jax.experimental import pallas as pl
from jax.experimental.pallas import tpu as pltpu
from jax.sharding import Mesh, PartitionSpec as P

NFFT = 2048
lowest_bin = 37
bin_spacing = 29
f32 = jnp.float32
bf16 = jnp.bfloat16

NF = 8
ROWS = 256
CH = 256
COLS = 96
TILE = 32
NORM_ROWS = 8


def series_coefficients():
    nodes = np.cos(np.linspace(0, np.pi, 4002)) / 8
    squares = nodes**2
    angles = 2 * np.pi * nodes
    sine = np.linalg.lstsq(squares[:, None] ** np.arange(4), np.sin(angles) / nodes, rcond=None)[0]
    cosine = np.linalg.lstsq(squares[:, None] ** np.arange(5), np.cos(angles), rcond=None)[0]
    return [np.float32(v) for v in sine], [np.float32(v) for v in cosine]


SINE, COSINE = series_coefficients()


def horner(coefficients, value):
    total = coefficients[-1]
    for coefficient in coefficients[-2::-1]:
        total = coefficient + value * total
    return total


def unit_circle(turns_times, multiple):
    turns = turns_times * np.float32(multiple / NFFT)
    magic = np.float32(1.5 * 2**23)
    part = turns - ((turns + magic) - magic)
    quarter = part * np.float32(0.25)
    square = quarter * quarter
    sine = quarter * horner(SINE, square)
    cosine = horner(COSINE, square)
    for _ in range(2):
        twice = sine + sine
        sine, cosine = twice * cosine, np.float32(1.0) - twice * sine
    return cosine, sine


def replica_tiles(tau):
    delay = tau.astype(f32)
    c0, s0 = unit_circle(delay, lowest_bin)
    cd, sd = unit_circle(delay, bin_spacing)
    cosines = [c0, c0 * cd - s0 * sd]
    sines = [s0, s0 * cd + c0 * sd]
    twice = cd + cd
    for _ in range(2, NF):
        cosines.append(twice * cosines[-1] - cosines[-2])
        sines.append(twice * sines[-1] - sines[-2])
    return cosines, sines


VMEM = pl.BlockSpec(memory_space=pltpu.VMEM)
BY_COLUMNS = (((1,), (1,)), ((), ()))


def product(left, right):
    return lax.dot_general(left, right, BY_COLUMNS, preferred_element_type=f32)


def thirds(values):
    high = values.astype(bf16)
    rest = values - high.astype(f32)
    middle = rest.astype(bf16)
    low = (rest - middle.astype(f32)).astype(bf16)
    return high, middle, low


def exact_product(ones, values):
    high, middle, low = thirds(values)
    return product(ones, high) + (product(ones, middle) + product(ones, low))


def replicas_kernel(place, travel_ref, after_ref, rep_ref, token_ref):
    block = pl.program_id(0)
    token_ref[...] = jnp.zeros_like(token_ref)

    def body(step, carry):
        rows = pl.ds(pl.multiple_of(step * TILE, TILE), TILE)
        for half in range(CH // 128):
            lanes = slice(half * 128, (half + 1) * 128)
            cosines, sines = replica_tiles(travel_ref[0, 0, rows, lanes].astype(jnp.int32))
            for f in range(NF):
                rep_ref[block, f, rows, lanes] = cosines[f].astype(bf16)
                rep_ref[block, f, rows, CH + half * 128 : CH + (half + 1) * 128] = sines[f].astype(bf16)
        return carry

    lax.fori_loop(0, ROWS // TILE, body, 0)


def replicas(place, travel, after, first, own):
    def index(i, p):
        return (p[first + i], p[8] if own else 0, 0, 0)

    return pl.pallas_call(
        replicas_kernel,
        grid_spec=pltpu.PrefetchScalarGridSpec(
            num_scalar_prefetch=1,
            grid=(4,),
            in_specs=[pl.BlockSpec((1, 1, ROWS, CH), index), VMEM],
            out_specs=[VMEM, VMEM],
        ),
        out_shape=[
            jax.ShapeDtypeStruct((4, NF, ROWS, 2 * CH), bf16),
            jax.ShapeDtypeStruct((8, 128), jnp.int32),
        ],
        cost_estimate=pl.CostEstimate(flops=4_500_000_000, bytes_accessed=1_000_000, transcendentals=0),
        compiler_params=pltpu.CompilerParams(vmem_limit_bytes=4 << 20),
        name=f"replicas_{int(own)}_{first}",
    )(place, travel, after)


def join_kernel(a_ref, b_ref, token_ref, out_ref):
    half = a_ref.shape[0]
    out_ref[0:half] = a_ref[...]
    out_ref[half : 2 * half] = b_ref[...]


def join(a, b, token):
    return pl.pallas_call(
        join_kernel,
        in_specs=[VMEM] * 3,
        out_specs=VMEM,
        out_shape=jax.ShapeDtypeStruct((2 * a.shape[0],) + a.shape[1:], a.dtype),
        cost_estimate=pl.CostEstimate(flops=0, bytes_accessed=100_000, transcendentals=0),
        compiler_params=pltpu.CompilerParams(vmem_limit_bytes=2 << 20),
        name=f"join_{a.shape[0]}",
    )(a, b, token)


def beams_kernel(a_ref, b_ref, wa_ref, wb_ref, na_ref, nb_ref, out_ref, *, slot):
    columns = [
        product(a_ref[slot, f], wa_ref[f]) + product(b_ref[slot, f], wb_ref[f]) for f in range(NF)
    ]
    out_ref[0:ROWS] = jnp.concatenate(columns, axis=1).astype(out_ref.dtype)
    if out_ref.shape[0] > ROWS:
        out_ref[ROWS : ROWS + NORM_ROWS] = na_ref[...] + nb_ref[...]


def beams_block(reps, weights, norms, step):
    own = STEPS[step] == (0, 0)
    rows = ROWS if own else ROWS + NORM_ROWS
    return pl.pallas_call(
        functools.partial(beams_kernel, slot=step % 4),
        in_specs=[VMEM] * 6,
        out_specs=VMEM,
        out_shape=jax.ShapeDtypeStruct((rows, NF * COLS), f32 if own else bf16),
        cost_estimate=pl.CostEstimate(flops=3_000_000_000, bytes_accessed=1_000_000, transcendentals=0),
        compiler_params=pltpu.CompilerParams(vmem_limit_bytes=4 << 20),
        name=f"beams_{step}",
    )(*reps, *weights, *norms)


def prepare_kernel(low_ref, high_ref, token_ref, w_ref, norm_ref, wide, *, first_row):
    for g in range(16):
        source = (low_ref, high_ref)[g // 8]
        for half in range(CH // 128):
            lanes = slice(half * 128, (half + 1) * 128)
            wide[half, g * 48 : (g + 1) * 48, :] = source[g % 8, :, lanes].astype(f32)
    squares = jnp.zeros((COLS, CH), f32)
    for f in range(NF):
        real, imag = [
            jnp.concatenate(
                [
                    jnp.concatenate(
                        [
                            wide[half, pl.ds(p * 24 + f * 3 + i, 16, stride=48), :]
                            for half in range(CH // 128)
                        ],
                        axis=1,
                    )
                    for i in range(3)
                ],
                axis=0,
            )
            for p in range(2)
        ]
        both = jnp.concatenate([real, imag], axis=0)
        squares = squares + both * both
        w_ref[f, :, 0:CH] = both.astype(bf16)
        w_ref[f, :, CH : 2 * CH] = jnp.concatenate([-imag, real], axis=0).astype(bf16)
    sums = exact_product(jnp.ones((NORM_ROWS, CH), bf16), squares)
    row = lax.broadcasted_iota(jnp.int32, sums.shape, 0) - first_row
    zero = jnp.zeros_like(sums)
    split = zero
    for index, part in enumerate(thirds(sums)):
        split = jnp.where(row == index, part.astype(f32), split)
    norm_ref[...] = jnp.concatenate([split] + [zero] * (NF - 1), axis=1).astype(bf16)


def prepare(low, high, token, first_row):
    return pl.pallas_call(
        functools.partial(prepare_kernel, first_row=first_row),
        in_specs=[VMEM] * 3,
        out_specs=[VMEM, VMEM],
        scratch_shapes=[pltpu.VMEM((CH // 128, 768, 128), f32)],
        out_shape=[
            jax.ShapeDtypeStruct((NF, COLS, 2 * CH), bf16),
            jax.ShapeDtypeStruct((NORM_ROWS, NF * COLS), bf16),
        ],
        cost_estimate=pl.CostEstimate(flops=1_000_000_000, bytes_accessed=1_000_000, transcendentals=0),
        compiler_params=pltpu.CompilerParams(vmem_limit_bytes=6 << 20),
        name=f"prepare_{first_row}",
    )(low, high, token)


def column_tables():
    slot = np.arange(NF * COLS) % 48
    place = slot % 16
    relative = sum(((place >> bit) & 1) << (3 - bit) for bit in range(4))
    return np.stack([relative, slot // 16]).astype(np.int32)


def finish_kernel(place, *refs, count):
    *received, own_ref, na_ref, nb_ref, table_ref, out_ref = refs
    window = lax.broadcasted_iota(jnp.int32, (48, NF * COLS), 0)
    source = table_ref[0:1, :] ^ place[9]
    pick = jnp.where(window == 3 * source + table_ref[1:2, :], 1.0, 0.0).astype(bf16)
    beams = own_ref[...]
    norm_rows = na_ref[...].astype(f32) + nb_ref[...].astype(f32)
    for ref in received:
        beams = beams + ref[0:ROWS].astype(f32)
        norm_rows = norm_rows + ref[ROWS : ROWS + NORM_ROWS].astype(f32)
    norm_sum = jnp.sum(exact_product(pick, norm_rows), axis=1, keepdims=True)
    window_norm = norm_sum / count + 1e-06
    out_ref[...] = exact_product(pick, beams * beams) / (count * window_norm)


def finish(place, received, own, norms, count):
    return pl.pallas_call(
        functools.partial(finish_kernel, count=count),
        in_specs=[pl.BlockSpec(memory_space=pltpu.SMEM)] + [VMEM] * 11,
        out_specs=VMEM,
        out_shape=jax.ShapeDtypeStruct((48, ROWS), f32),
        compiler_params=pltpu.CompilerParams(vmem_limit_bytes=8 << 20),
        name="finish",
    )(place, *received, own, *norms, jnp.asarray(column_tables()))


LAG = 3
STEPS = ((2, 1), (1, 1), (3, 1), (2, 0), (0, 1), (1, 0), (3, 0), (0, 0))
SWAP = [(0, 1), (1, 0)]


def tie(*values):
    return lax.optimization_barrier(values)


def per_device(spectra, travel, quality):
    x, yh, core = lax.axis_index("x"), lax.axis_index("yh"), lax.axis_index("c")
    order = [((x + dx) % 4) * 2 + (yh ^ dy) for dx, dy in STEPS]
    place = jnp.stack(order + [core, lax.axis_index("z") * 2 + lax.axis_index("yl")]).astype(jnp.int32)
    blocks = travel.reshape(8, 2, ROWS, CH)
    sent = lax.dynamic_slice(blocks, (0, 1 - core, 0, 0), (8, 1, ROWS, CH)).astype(jnp.int16)
    block = (spectra * quality.astype(bf16)).reshape(1, 48, CH)
    block, sent, place = tie(block, sent, place)

    def partner(mask):
        return [(i, i ^ mask) for i in range(16)]

    arrived = lax.ppermute(sent, "c", SWAP)
    held = block
    reps = []
    for stage, mask in enumerate((8, 4, 2, 1)):
        other = lax.ppermute(held, ("z", "yl"), partner(mask))
        if stage == 3:
            held_swapped = lax.ppermute(held, "c", SWAP)
        rep, token = replicas(place, blocks if stage < 2 else arrived, held, 4 * (stage % 2), stage < 2)
        reps.append(rep)
        if stage < 3:
            held = join(held, other, token)
    other_swapped = lax.ppermute(other, "c", SWAP)
    w_a, n_a = prepare(held, other, token, 0)
    w_b, n_b = prepare(held_swapped, other_swapped, token, 3)
    weights, norms = (w_a, w_b), (n_a, n_b)
    received = []
    for step, (dx, dy) in enumerate(STEPS):
        if step >= LAG:
            n_a, received[step - LAG] = tie(n_a, received[step - LAG])
        beams = beams_block((reps[step // 4], reps[2 + step // 4]), weights, (n_a, n_b), step)
        if (dx, dy) == (0, 0):
            kept = beams
        else:
            pairs = [(i, ((i // 2 + dx) % 4) * 2 + ((i % 2) ^ dy)) for i in range(8)]
            received.append(lax.ppermute(beams, ("x", "yh"), pairs))
    return finish(place, received, kept, (n_a, n_b), float(NF * CH * 16))


def solution(mesh):
    fine = Mesh(mesh.devices.reshape(8, 2, 4, 2, 2), ("z", "yl", "x", "yh", "c"))
    return jax.shard_map(
        per_device,
        mesh=fine,
        in_specs=(
            P(None, None, ("z", "yl"), ("x", "yh", "c")),
            P(("z", "yl"), ("x", "yh", "c")),
            P(("x", "yh", "c")),
        ),
        out_specs=P(None, ("z", "yl", "x", "yh", "c")),
        check_vma=False,
    )
```

time: 363 us -> 105 us (0.29)
  other arithmetic: 139 us -> 3.14 us
  blocking collectives: 72.5 us -> 0 us
  waiting for transfers between devices: 93.2 us -> 32.4 us
  starting transfers between devices: 0.01 us -> 35.1 us
  Pallas kernels: 0 us -> 31.5 us
  local copies, waits for them, and re-layouts: 23.6 us -> 2.33 us
  matrix products: 20.4 us -> 0 us
  between operations: 13.4 us -> 0.21 us
    another operation x4 -> x0, other arithmetic: 135 us -> none
    reduce_scatter x1 -> x0, waiting for transfers between devices: 93.1 us -> none  [per_device(): lax.psum_scatter(beams_for(travel, spectra_matrix, freq_count), 'chan', s...]
    psum x1 -> x0, blocking collectives: 39.9 us -> none  [per_device(): lax.psum(jnp.sum(gathered.astype(jnp.float32) ** 2, axis=(0, 1, 3)), 'chan')]
    ppermute x0 -> x14, starting transfers between devices: none -> 35.1 us  [the longest x7 20.1 us: per_device(): received.append(lax.ppermute(beams, ('x', 'yh'), pairs))]
    all_gather x1 -> x0, blocking collectives: 32.6 us -> none  [per_device(): gathered = lax.all_gather(masked, 'grid', axis=2, tiled=True)]
    ppermute x0 -> x14, waiting for transfers between devices: none -> 32.4 us  [the longest x7 29.4 us: per_device(): received.append(lax.ppermute(beams, ('x', 'yh'), pairs))]
    pallas_call x0 -> x18, Pallas kernels: none -> 31.5 us  [the longest x4 18.1 us: replicas(): pl.pallas_call(replicas_kernel, grid_spec=pltpu.PrefetchScalarGridSpec(nu...]
    dot_general x4 -> x0, matrix products: 20.4 us -> none  [one_block(): jnp.einsum('frk,fwk->rfw', replicas, spectra_matrix, preferred_element_ty...]
  transfers between devices with their start and end apart: 1 -> 14, of which waited for: 1 -> 6; matrix products, arithmetic and copies ran while one was open for 0% -> 0% of each run, Pallas kernels for 0% -> 26%
where the time goes in v2:
time: 105 us
  starting transfers between devices  35.1 us (33%)
  waiting for transfers between devices  32.4 us (31%)
  Pallas kernels  31.5 us (30%)
  other arithmetic  3.14 us (3%)
  local copies, waits for them, and re-layouts  2.33 us (2%)
    ppermute x7, waiting for transfers between devices, per_device(): received.append(lax.ppermute(beams, ('x', 'yh'), pairs))  29.4 us
    ppermute x7, starting transfers between devices, per_device(): received.append(lax.ppermute(beams, ('x', 'yh'), pairs))  20.1 us
    pallas_call x4, Pallas kernels, replicas(): pl.pallas_call(replicas_kernel, grid_spec=pltpu.PrefetchScalarGridSpec(nu...  18.1 us
    pallas_call x8, Pallas kernels, beams_block(): pl.pallas_call(functools.partial(beams_kernel, slot=step % 4), in_specs=[...  10.5 us
    ppermute x4, starting transfers between devices, per_device(): other = lax.ppermute(held, ('z', 'yl'), partner(mask))  8.68 us
    ppermute x1, starting transfers between devices, per_device(): arrived = lax.ppermute(sent, 'c', SWAP)  3.29 us
    ppermute x4, waiting for transfers between devices, per_device(): other = lax.ppermute(held, ('z', 'yl'), partner(mask))  3 us
    unnamed x6, local copies, waits for them, and re-layouts  2.2 us
  transfers between devices with their start and end apart: 14, of which 6 were waited for; matrix products, arithmetic and copies ran while one was open for 0% of the time, Pallas kernels for 26%

profile of v2, /device:TPU:1, one launch (start us, length us, event | category | flops | bytes accessed | tf_op | source)
XLA Modules:
  0.0 104.7 jit_solution(15033968088884196624)
XLA Ops:
  1.5 1.7 %dynamic-slice_convert_fusion = s16[8,1,256,256]{3,2,1,0:T(8,128)(2,1)S(1)} fusion(s32[8,2,256,256]{3,2,1,0:T(8,128)} %bitcast.11, s32[]{:T(128)S(6)} %select_n.30), kind=kLoop, calls=%fused_computation | loop fusion | flops 524288 | bytes 3145732 | tf_op jit(solution)/shard_map/convert_element_type | solution.py:272
  3.3 3.3 %collective-permute-start.3 = (s16[8,1,256,256]{3,2,1,0:T(8,128)(2,1)S(1)}, s16[8,1,256,256]{3,2,1,0:T(8,128)(2,1)S(1)}, u32[]{:S(2)}, u32[]{:S(2)}) collective-permute-start(s16[8,1,256,256]{3,2,1,0:T(8,128)(2,1)S(1)} %dynamic-slice_convert_fusion), channel_id=1, source_target_pairs={{0,1},{1,0},{2,3},{3,2},{4,5},{5,4},{6,7},{7,6},{8,9},{9,8},{10,11... | collective-permute-start | bytes 3145736 | tf_op jit(solution)/shard_map/ppermute | solution.py:279
  6.6 5.2 %collective-permute-start = (bf16[1,48,256]{2,1,0:T(8,128)(2,1)S(1)}, bf16[1,48,256]{2,1,0:T(8,128)(2,1)S(1)}, u32[]{:S(2)}, u32[]{:S(2)}) collective-permute-start(bf16[1,48,256]{2,1,0:T(8,128)(2,1)S(1)} %reshape.7.after_ref.a_ref), channel_id=1, source_target_pairs={{0,128},{16,144},{32,160},{48,176},{64,192},{80,208},{96,224},{112... | collective-permute-start | bytes 73736 | tf_op jit(solution)/shard_map/ppermute | solution.py:283
  11.8 2.2 %copy-done = s32[4096,256]{1,0:T(8,128)S(1)} copy-done((s32[4096,256]{1,0:T(8,128)S(1)}, s32[4096,256]{1,0:T(8,128)}, u32[]{:S(2)}) %copy-start) | copy-done | bytes 4194328
  14.0 4.5 %replicas_1_0.1 = (bf16[4,8,256,512]{3,2,1,0:T(8,128)(2,1)S(1)}, s32[8,128]{1,0:T(8,128)S(1)}) custom-call(s32[10]{0:T(128)S(1)} %stack.43.place, s32[8,2,256,256]{3,2,1,0:T(8,128)S(1)} %bitcast.12, bf16[1,48,256]{2,1,0:T(8,128)(2,1)S(1)} %reshape.7.after_ref.a_ref), custom_call_target="tpu_custom_call" | custom-call | flops 4499999744 | bytes 1000000 | tf_op jit(solution)/shard_map/replicas_1_0/pallas_call | solution.py:113
  19.8 4.5 %replicas_1_4.1 = (bf16[4,8,256,512]{3,2,1,0:T(8,128)(2,1)S(1)}, s32[8,128]{1,0:T(8,128)S(1)}) custom-call(s32[10]{0:T(128)S(1)} %stack.43.place, s32[8,2,256,256]{3,2,1,0:T(8,128)S(1)} %bitcast.13, bf16[2,48,256]{2,1,0:T(8,128)(2,1)S(1)} %join_1.1.after_ref.a_ref), custom_call_target="tpu_custom_call" | custom-call | flops 4499999744 | bytes 1000000 | tf_op jit(solution)/shard_map/replicas_1_4/pallas_call | solution.py:113
  25.2 4.5 %replicas_0_0.1 = (bf16[4,8,256,512]{3,2,1,0:T(8,128)(2,1)S(1)}, s32[8,128]{1,0:T(8,128)S(1)}) custom-call(s32[10]{0:T(128)S(1)} %stack.43.place, s16[8,1,256,256]{3,2,1,0:T(8,128)(2,1)S(1)} %collective-permute-done.3.travel_ref, bf16[4,48,256]{2,1,0:T(8,128)(2,1)S(1)} %join_2.1.after_ref.a_ref), custom_call_target="tpu_custom_call" | custom-call | flops 4499999744 | bytes 1000000 | tf_op jit(solution)/shard_map/replicas_0_0/pallas_call | solution.py:113
  29.8 1.4 %collective-permute-start.4 = (bf16[8,48,256]{2,1,0:T(8,128)(2,1)S(1)}, bf16[8,48,256]{2,1,0:T(8,128)(2,1)S(1)}, u32[]{:S(2)}, u32[]{:S(2)}) collective-permute-start(bf16[8,48,256]{2,1,0:T(8,128)(2,1)S(1)} %join_4.1.after_ref.low_ref), channel_id=1, source_target_pairs={{0,16},{16,0},{32,48},{48,32},{64,80},{80,64},{96,112},{112,96},{1... | collective-permute-start | bytes 589832 | tf_op jit(solution)/shard_map/ppermute | solution.py:283
  32.4 3.0 %collective-permute-done.4.high_ref = bf16[8,48,256]{2,1,0:T(8,128)(2,1)S(1)} collective-permute-done((bf16[8,48,256]{2,1,0:T(8,128)(2,1)S(1)}, bf16[8,48,256]{2,1,0:T(8,128)(2,1)S(1)}, u32[]{:S(2)}, u32[]{:S(2)}) %collective-permute-start.4) | collective-permute-done | bytes 196640 | tf_op jit(solution)/shard_map/ppermute | solution.py:283
  35.3 1.8 %collective-permute-start.6 = (bf16[8,48,256]{2,1,0:T(8,128)(2,1)S(1)}, bf16[8,48,256]{2,1,0:T(8,128)(2,1)S(1)}, u32[]{:S(2)}, u32[]{:S(2)}) collective-permute-start(bf16[8,48,256]{2,1,0:T(8,128)(2,1)S(1)} %collective-permute-done.4.high_ref), channel_id=1, source_target_pairs={{0,1},{1,0},{2,3},{3,2},{4,5},{5,4},{6,7},{7,6},{8,9},{9,8},{10,11... | collective-permute-start | bytes 589832 | tf_op jit(solution)/shard_map/ppermute | solution.py:290
  37.2 4.5 %replicas_0_4.1 = (bf16[4,8,256,512]{3,2,1,0:T(8,128)(2,1)S(1)}, s32[8,128]{1,0:T(8,128)S(1)}) custom-call(s32[10]{0:T(128)S(1)} %stack.43.place, s16[8,1,256,256]{3,2,1,0:T(8,128)(2,1)S(1)} %collective-permute-done.3.travel_ref, bf16[8,48,256]{2,1,0:T(8,128)(2,1)S(1)} %join_4.1.after_ref.low_ref), custom_call_target="tpu_custom_call" | custom-call | flops 4499999744 | bytes 1000000 | tf_op jit(solution)/shard_map/replicas_0_4/pallas_call | solution.py:113
  42.6 1.3 %beams_0.1 = bf16[264,768]{1,0:T(8,128)(2,1)S(1)} custom-call(bf16[4,8,256,512]{3,2,1,0:T(8,128)(2,1)S(1)} %get-tuple-element.38.a_ref, bf16[4,8,256,512]{3,2,1,0:T(8,128)(2,1)S(1)} %get-tuple-element.39.b_ref, bf16[8,96,512]{2,1,0:T(8,128)(2,1)S(1)} %get-tuple-element.40.wa_ref, bf16[8,96,512]{2,1,0:T(8,128)(2,1)S(1)} %get-tuple-element.41.wb_ref, ...), custom_call_target="tpu_custom_call" | custom-call | flops 3000000000 | bytes 1000000 | tf_op jit(solution)/shard_map/beams_0/pallas_call | solution.py:161
  43.9 5.5 %collective-permute-start.7 = (bf16[264,768]{1,0:T(8,128)(2,1)S(1)}, bf16[264,768]{1,0:T(8,128)(2,1)S(1)}, u32[]{:S(2)}, u32[]{:S(2)}) collective-permute-start(bf16[264,768]{1,0:T(8,128)(2,1)S(1)} %beams_0.1), channel_id=1, source_target_pairs={{0,10},{2,8},{4,14},{6,12},{8,2},{10,0},{12,6},{14,4},{1,11},{3,9}... | collective-permute-start | bytes 1216520 | tf_op jit(solution)/shard_map/ppermute | solution.py:303
  52.2 5.1 %collective-permute-start.9 = (bf16[264,768]{1,0:T(8,128)(2,1)S(1)}, bf16[264,768]{1,0:T(8,128)(2,1)S(1)}, u32[]{:S(2)}, u32[]{:S(2)}) collective-permute-start(bf16[264,768]{1,0:T(8,128)(2,1)S(1)} %beams_2.1), channel_id=1, source_target_pairs={{0,14},{2,12},{4,2},{6,0},{8,6},{10,4},{12,10},{14,8},{1,15},{3,13... | collective-permute-start | bytes 1216520 | tf_op jit(solution)/shard_map/ppermute | solution.py:303
  57.3 1.7 %collective-permute-done.7.refs_0_ = bf16[264,768]{1,0:T(8,128)(2,1)S(1)} collective-permute-done((bf16[264,768]{1,0:T(8,128)(2,1)S(1)}, bf16[264,768]{1,0:T(8,128)(2,1)S(1)}, u32[]{:S(2)}, u32[]{:S(2)}) %collective-permute-start.7) | collective-permute-done | bytes 405536 | tf_op jit(solution)/shard_map/ppermute | solution.py:303
  59.0 1.3 %beams_3.1 = bf16[264,768]{1,0:T(8,128)(2,1)S(1)} custom-call(bf16[4,8,256,512]{3,2,1,0:T(8,128)(2,1)S(1)} %get-tuple-element.38.a_ref, bf16[4,8,256,512]{3,2,1,0:T(8,128)(2,1)S(1)} %get-tuple-element.39.b_ref, bf16[8,96,512]{2,1,0:T(8,128)(2,1)S(1)} %get-tuple-element.40.wa_ref, bf16[8,96,512]{2,1,0:T(8,128)(2,1)S(1)} %get-tuple-element.41.wb_ref, ...), custom_call_target="tpu_custom_call" | custom-call | flops 3000000000 | bytes 1000000 | tf_op jit(solution)/shard_map/beams_3/pallas_call | solution.py:161
  60.3 3.3 %collective-permute-start.10 = (bf16[264,768]{1,0:T(8,128)(2,1)S(1)}, bf16[264,768]{1,0:T(8,128)(2,1)S(1)}, u32[]{:S(2)}, u32[]{:S(2)}) collective-permute-start(bf16[264,768]{1,0:T(8,128)(2,1)S(1)} %beams_3.1), channel_id=1, source_target_pairs={{0,8},{2,10},{4,12},{6,14},{8,0},{10,2},{12,4},{14,6},{1,9},{3,11}... | collective-permute-start | bytes 1216520 | tf_op jit(solution)/shard_map/ppermute | solution.py:303
  63.6 10.6 %collective-permute-done.8.refs_1_ = bf16[264,768]{1,0:T(8,128)(2,1)S(1)} collective-permute-done((bf16[264,768]{1,0:T(8,128)(2,1)S(1)}, bf16[264,768]{1,0:T(8,128)(2,1)S(1)}, u32[]{:S(2)}, u32[]{:S(2)}) %collective-permute-start.8) | collective-permute-done | bytes 405536 | tf_op jit(solution)/shard_map/ppermute | solution.py:303
  75.5 2.4 %collective-permute-start.11 = (bf16[264,768]{1,0:T(8,128)(2,1)S(1)}, bf16[264,768]{1,0:T(8,128)(2,1)S(1)}, u32[]{:S(2)}, u32[]{:S(2)}) collective-permute-start(bf16[264,768]{1,0:T(8,128)(2,1)S(1)} %beams_4.1), channel_id=1, source_target_pairs={{0,2},{2,0},{4,6},{6,4},{8,10},{10,8},{12,14},{14,12},{1,3},{3,1},... | collective-permute-start | bytes 1216520 | tf_op jit(solution)/shard_map/ppermute | solution.py:303
  79.2 3.4 %collective-permute-start.12 = (bf16[264,768]{1,0:T(8,128)(2,1)S(1)}, bf16[264,768]{1,0:T(8,128)(2,1)S(1)}, u32[]{:S(2)}, u32[]{:S(2)}) collective-permute-start(bf16[264,768]{1,0:T(8,128)(2,1)S(1)} %beams_5.1), channel_id=1, source_target_pairs={{0,4},{2,6},{4,8},{6,10},{8,12},{10,14},{12,0},{14,2},{1,5},{3,7},... | collective-permute-start | bytes 1216520 | tf_op jit(solution)/shard_map/ppermute | solution.py:303
  82.6 4.7 %collective-permute-done.10.refs_3_ = bf16[264,768]{1,0:T(8,128)(2,1)S(1)} collective-permute-done((bf16[264,768]{1,0:T(8,128)(2,1)S(1)}, bf16[264,768]{1,0:T(8,128)(2,1)S(1)}, u32[]{:S(2)}, u32[]{:S(2)}) %collective-permute-start.10) | collective-permute-done | bytes 405536 | tf_op jit(solution)/shard_map/ppermute | solution.py:303
  90.3 6.0 %collective-permute-done.12.refs_5_ = bf16[264,768]{1,0:T(8,128)(2,1)S(1)} collective-permute-done((bf16[264,768]{1,0:T(8,128)(2,1)S(1)}, bf16[264,768]{1,0:T(8,128)(2,1)S(1)}, u32[]{:S(2)}, u32[]{:S(2)}) %collective-permute-start.12) | collective-permute-done | bytes 405536 | tf_op jit(solution)/shard_map/ppermute | solution.py:303
  96.3 6.4 %collective-permute-done.13.refs_6_ = bf16[264,768]{1,0:T(8,128)(2,1)S(1)} collective-permute-done((bf16[264,768]{1,0:T(8,128)(2,1)S(1)}, bf16[264,768]{1,0:T(8,128)(2,1)S(1)}, u32[]{:S(2)}, u32[]{:S(2)}) %collective-permute-start.13) | collective-permute-done | bytes 405536 | tf_op jit(solution)/shard_map/ppermute | solution.py:303
  102.7 2.1 %finish.1 = f32[48,256]{1,0:T(8,128)} custom-call(s32[10]{0:T(128)S(1)} %stack.43.place, bf16[264,768]{1,0:T(8,128)(2,1)S(1)} %collective-permute-done.7.refs_0_, bf16[264,768]{1,0:T(8,128)(2,1)S(1)} %collective-permute-done.8.refs_1_, bf16[264,768]{1,0:T(8,128)(2,1)S(1)} %collective-permute-done.9.refs_2_, ...), custom_call_target="tpu_custom_call" | custom-call | tf_op jit(solution)/shard_map/finish/pallas_call | solution.py:248
  (34 shorter events, 14.1 us)
Async XLA Ops:
  3.3 21.9 %collective-permute-start.3 = (s16[8,1,256,256]{3,2,1,0:T(8,128)(2,1)S(1)}, s16[8,1,256,256]{3,2,1,0:T(8,128)(2,1)S(1)}, u32[]{:S(2)}, u32[]{:S(2)}) collective-permute-start(s16[8,1,256,256]{3,2,1,0:T(8,128)(2,1)S(1)} %dynamic-slice_convert_fusion), channel_id=1, source_target_pairs={{0,1},{1,0},{2,3},{3,2},{4,5},{5,4},{6,7},{7,6},{8,9},{9,8},{10,11... | collective-permute-start | bytes 3145736 | tf_op jit(solution)/shard_map/ppermute | solution.py:279
  6.6 11.9 %collective-permute-start = (bf16[1,48,256]{2,1,0:T(8,128)(2,1)S(1)}, bf16[1,48,256]{2,1,0:T(8,128)(2,1)S(1)}, u32[]{:S(2)}, u32[]{:S(2)}) collective-permute-start(bf16[1,48,256]{2,1,0:T(8,128)(2,1)S(1)} %reshape.7.after_ref.a_ref), channel_id=1, source_target_pairs={{0,128},{16,144},{32,160},{48,176},{64,192},{80,208},{96,224},{112... | collective-permute-start | bytes 73736 | tf_op jit(solution)/shard_map/ppermute | solution.py:283
  11.8 2.2 %copy-start = (s32[4096,256]{1,0:T(8,128)S(1)}, s32[4096,256]{1,0:T(8,128)}, u32[]{:S(2)}) copy-start(s32[4096,256]{1,0:T(8,128)} %param.5) | copy-start | bytes 12582916
  14.0 5.8 %copy-start.1 = (s32[4096,256]{1,0:T(8,128)S(1)}, s32[4096,256]{1,0:T(8,128)}, u32[]{:S(2)}) copy-start(s32[4096,256]{1,0:T(8,128)} %param.5) | copy-start | bytes 12582916
  18.5 5.8 %collective-permute-start.1 = (bf16[2,48,256]{2,1,0:T(8,128)(2,1)S(1)}, bf16[2,48,256]{2,1,0:T(8,128)(2,1)S(1)}, u32[]{:S(2)}, u32[]{:S(2)}) collective-permute-start(bf16[2,48,256]{2,1,0:T(8,128)(2,1)S(1)} %join_1.1.after_ref.a_ref), channel_id=1, source_target_pairs={{0,64},{16,80},{32,96},{48,112},{64,0},{80,16},{96,32},{112,48},{1... | collective-permute-start | bytes 147464 | tf_op jit(solution)/shard_map/ppermute | solution.py:283
  24.4 5.4 %collective-permute-start.2 = (bf16[4,48,256]{2,1,0:T(8,128)(2,1)S(1)}, bf16[4,48,256]{2,1,0:T(8,128)(2,1)S(1)}, u32[]{:S(2)}, u32[]{:S(2)}) collective-permute-start(bf16[4,48,256]{2,1,0:T(8,128)(2,1)S(1)} %join_2.1.after_ref.a_ref), channel_id=1, source_target_pairs={{0,32},{16,48},{32,0},{48,16},{64,96},{80,112},{96,64},{112,80},{1... | collective-permute-start | bytes 294920 | tf_op jit(solution)/shard_map/ppermute | solution.py:283
  29.8 5.6 %collective-permute-start.4 = (bf16[8,48,256]{2,1,0:T(8,128)(2,1)S(1)}, bf16[8,48,256]{2,1,0:T(8,128)(2,1)S(1)}, u32[]{:S(2)}, u32[]{:S(2)}) collective-permute-start(bf16[8,48,256]{2,1,0:T(8,128)(2,1)S(1)} %join_4.1.after_ref.low_ref), channel_id=1, source_target_pairs={{0,16},{16,0},{32,48},{48,32},{64,80},{80,64},{96,112},{112,96},{1... | collective-permute-start | bytes 589832 | tf_op jit(solution)/shard_map/ppermute | solution.py:283
  31.2 11.0 %collective-permute-start.5 = (bf16[8,48,256]{2,1,0:T(8,128)(2,1)S(1)}, bf16[8,48,256]{2,1,0:T(8,128)(2,1)S(1)}, u32[]{:S(2)}, u32[]{:S(2)}) collective-permute-start(bf16[8,48,256]{2,1,0:T(8,128)(2,1)S(1)} %join_4.1.after_ref.low_ref), channel_id=1, source_target_pairs={{0,1},{1,0},{2,3},{3,2},{4,5},{5,4},{6,7},{7,6},{8,9},{9,8},{10,11... | collective-permute-start | bytes 589832 | tf_op jit(solution)/shard_map/ppermute | solution.py:285
  35.3 6.8 %collective-permute-start.6 = (bf16[8,48,256]{2,1,0:T(8,128)(2,1)S(1)}, bf16[8,48,256]{2,1,0:T(8,128)(2,1)S(1)}, u32[]{:S(2)}, u32[]{:S(2)}) collective-permute-start(bf16[8,48,256]{2,1,0:T(8,128)(2,1)S(1)} %collective-permute-done.4.high_ref), channel_id=1, source_target_pairs={{0,1},{1,0},{2,3},{3,2},{4,5},{5,4},{6,7},{7,6},{8,9},{9,8},{10,11... | collective-permute-start | bytes 589832 | tf_op jit(solution)/shard_map/ppermute | solution.py:290
  43.9 15.1 %collective-permute-start.7 = (bf16[264,768]{1,0:T(8,128)(2,1)S(1)}, bf16[264,768]{1,0:T(8,128)(2,1)S(1)}, u32[]{:S(2)}, u32[]{:S(2)}) collective-permute-start(bf16[264,768]{1,0:T(8,128)(2,1)S(1)} %beams_0.1), channel_id=1, source_target_pairs={{0,10},{2,8},{4,14},{6,12},{8,2},{10,0},{12,6},{14,4},{1,11},{3,9}... | collective-permute-start | bytes 1216520 | tf_op jit(solution)/shard_map/ppermute | solution.py:303
  50.7 23.5 %collective-permute-start.8 = (bf16[264,768]{1,0:T(8,128)(2,1)S(1)}, bf16[264,768]{1,0:T(8,128)(2,1)S(1)}, u32[]{:S(2)}, u32[]{:S(2)}) collective-permute-start(bf16[264,768]{1,0:T(8,128)(2,1)S(1)} %beams_1.1), channel_id=1, source_target_pairs={{0,6},{2,4},{4,10},{6,8},{8,14},{10,12},{12,2},{14,0},{1,7},{3,5},... | collective-permute-start | bytes 1216520 | tf_op jit(solution)/shard_map/ppermute | solution.py:303
  52.2 25.7 %collective-permute-start.9 = (bf16[264,768]{1,0:T(8,128)(2,1)S(1)}, bf16[264,768]{1,0:T(8,128)(2,1)S(1)}, u32[]{:S(2)}, u32[]{:S(2)}) collective-permute-start(bf16[264,768]{1,0:T(8,128)(2,1)S(1)} %beams_2.1), channel_id=1, source_target_pairs={{0,14},{2,12},{4,2},{6,0},{8,6},{10,4},{12,10},{14,8},{1,15},{3,13... | collective-permute-start | bytes 1216520 | tf_op jit(solution)/shard_map/ppermute | solution.py:303
  60.3 27.0 %collective-permute-start.10 = (bf16[264,768]{1,0:T(8,128)(2,1)S(1)}, bf16[264,768]{1,0:T(8,128)(2,1)S(1)}, u32[]{:S(2)}, u32[]{:S(2)}) collective-permute-start(bf16[264,768]{1,0:T(8,128)(2,1)S(1)} %beams_3.1), channel_id=1, source_target_pairs={{0,8},{2,10},{4,12},{6,14},{8,0},{10,2},{12,4},{14,6},{1,9},{3,11}... | collective-permute-start | bytes 1216520 | tf_op jit(solution)/shard_map/ppermute | solution.py:303
  75.5 13.4 %collective-permute-start.11 = (bf16[264,768]{1,0:T(8,128)(2,1)S(1)}, bf16[264,768]{1,0:T(8,128)(2,1)S(1)}, u32[]{:S(2)}, u32[]{:S(2)}) collective-permute-start(bf16[264,768]{1,0:T(8,128)(2,1)S(1)} %beams_4.1), channel_id=1, source_target_pairs={{0,2},{2,0},{4,6},{6,4},{8,10},{10,8},{12,14},{14,12},{1,3},{3,1},... | collective-permute-start | bytes 1216520 | tf_op jit(solution)/shard_map/ppermute | solution.py:303
  79.2 17.0 %collective-permute-start.12 = (bf16[264,768]{1,0:T(8,128)(2,1)S(1)}, bf16[264,768]{1,0:T(8,128)(2,1)S(1)}, u32[]{:S(2)}, u32[]{:S(2)}) collective-permute-start(bf16[264,768]{1,0:T(8,128)(2,1)S(1)} %beams_5.1), channel_id=1, source_target_pairs={{0,4},{2,6},{4,8},{6,10},{8,12},{10,14},{12,0},{14,2},{1,5},{3,7},... | collective-permute-start | bytes 1216520 | tf_op jit(solution)/shard_map/ppermute | solution.py:303
  88.6 14.0 %copy-start.2 = (s32[2,768]{1,0:T(2,128)S(1)}, s32[2,768]{1,0:T(2,128)}, u32[]{:S(2)}) copy-start(s32[2,768]{1,0:T(2,128)} %constant.63.clone.refs_10_) | copy-start | bytes 18436
  88.6 14.0 %collective-permute-start.13 = (bf16[264,768]{1,0:T(8,128)(2,1)S(1)}, bf16[264,768]{1,0:T(8,128)(2,1)S(1)}, u32[]{:S(2)}, u32[]{:S(2)}) collective-permute-start(bf16[264,768]{1,0:T(8,128)(2,1)S(1)} %beams_6.1), channel_id=1, source_target_pairs={{0,12},{2,14},{4,0},{6,2},{8,4},{10,6},{12,8},{14,10},{1,13},{3,15... | collective-permute-start | bytes 1216520 | tf_op jit(solution)/shard_map/ppermute | solution.py:303

commit v3 on v2

--- a/solution.py
+++ b/solution.py
@@ -108,7 +108,7 @@
 
 def replicas(place, travel, after, first, own):
     def index(i, p):
-        return (p[first + i], p[8] if own else 0, 0, 0)
+        return (p[first + i], 0, 0, 0)
 
     return pl.pallas_call(
         replicas_kernel,
@@ -255,7 +255,7 @@
     )(place, *received, own, *norms, jnp.asarray(column_tables()))
 
 
-LAG = 3
+LAG = 4
 STEPS = ((2, 1), (1, 1), (3, 1), (2, 0), (0, 1), (1, 0), (3, 0), (0, 0))
 SWAP = [(0, 1), (1, 0)]
 
@@ -269,33 +269,39 @@
     order = [((x + dx) % 4) * 2 + (yh ^ dy) for dx, dy in STEPS]
     place = jnp.stack(order + [core, lax.axis_index("z") * 2 + lax.axis_index("yl")]).astype(jnp.int32)
     blocks = travel.reshape(8, 2, ROWS, CH)
-    sent = lax.dynamic_slice(blocks, (0, 1 - core, 0, 0), (8, 1, ROWS, CH)).astype(jnp.int16)
     block = (spectra * quality.astype(bf16)).reshape(1, 48, CH)
-    block, sent, place = tie(block, sent, place)
+    kept_travel, sent = [
+        lax.dynamic_slice(blocks, (0, of, 0, 0), (8, 1, ROWS, CH)).astype(jnp.int16)
+        for of in (core, 1 - core)
+    ]
+    block, kept_travel, sent, place = tie(block, kept_travel, sent, place)
 
     def partner(mask):
         return [(i, i ^ mask) for i in range(16)]
 
     arrived = lax.ppermute(sent, "c", SWAP)
     held = block
-    reps = []
+    reps = {}
     for stage, mask in enumerate((8, 4, 2, 1)):
         other = lax.ppermute(held, ("z", "yl"), partner(mask))
         if stage == 3:
             held_swapped = lax.ppermute(held, "c", SWAP)
-        rep, token = replicas(place, blocks if stage < 2 else arrived, held, 4 * (stage % 2), stage < 2)
-        reps.append(rep)
-        if stage < 3:
-            held = join(held, other, token)
+            break
+        own, first = ((True, 0), (False, 0), (True, 4))[stage]
+        reps[own, first], token = replicas(place, kept_travel if own else arrived, held, first, own)
+        held = join(held, other, token)
     other_swapped = lax.ppermute(other, "c", SWAP)
     w_a, n_a = prepare(held, other, token, 0)
     w_b, n_b = prepare(held_swapped, other_swapped, token, 3)
-    weights, norms = (w_a, w_b), (n_a, n_b)
+    weights = (w_a, w_b)
     received = []
     for step, (dx, dy) in enumerate(STEPS):
         if step >= LAG:
             n_a, received[step - LAG] = tie(n_a, received[step - LAG])
-        beams = beams_block((reps[step // 4], reps[2 + step // 4]), weights, (n_a, n_b), step)
+        if step == 4:
+            reps[False, 4], _ = replicas(place, arrived, beams, 4, False)
+        first = step // 4 * 4
+        beams = beams_block((reps[True, first], reps[False, first]), weights, (n_a, n_b), step)
         if (dx, dy) == (0, 0):
             kept = beams
         else:

time: 105 us -> 99.4 us (0.947)
  starting transfers between devices: 35.1 us -> 32.1 us
  waiting for transfers between devices: 32.4 us -> 29.8 us
  local copies, waits for them, and re-layouts: 2.33 us -> 0.14 us
    ppermute x7, waiting for transfers between devices: 29.4 us -> 26.2 us  [per_device(): received.append(lax.ppermute(beams, ('x', 'yh'), pairs))]
    ppermute x7, starting transfers between devices: 20.1 us -> 17.1 us  [per_device(): received.append(lax.ppermute(beams, ('x', 'yh'), pairs))]
    unnamed x6 -> x2, local copies, waits for them, and re-layouts: 2.2 us -> 0.01 us
  transfers between devices with their start and end apart: 14 -> 14, of which waited for: 6 -> 7; matrix products, arithmetic and copies ran while one was open for 0% -> 0% of each run, Pallas kernels for 26% -> 25%
where the time goes in v3:
time: 99.4 us; the launch traced here: 98.3 us
  starting transfers between devices  32.1 us (32%)
  Pallas kernels  32.1 us (32%)
  waiting for transfers between devices  29.8 us (30%)
  other arithmetic  3.87 us (4%)
    ppermute x7, waiting for transfers between devices, per_device(): received.append(lax.ppermute(beams, ('x', 'yh'), pairs))  26.2 us
    pallas_call x4, Pallas kernels, replicas(): pl.pallas_call(replicas_kernel, grid_spec=pltpu.PrefetchScalarGridSpec(nu...  18.7 us
    ppermute x7, starting transfers between devices, per_device(): received.append(lax.ppermute(beams, ('x', 'yh'), pairs))  17.1 us
    pallas_call x8, Pallas kernels, beams_block(): pl.pallas_call(functools.partial(beams_kernel, slot=step % 4), in_specs=[...  10.5 us
    ppermute x4, starting transfers between devices, per_device(): other = lax.ppermute(held, ('z', 'yl'), partner(mask))  8.68 us
    ppermute x1, starting transfers between devices, per_device(): arrived = lax.ppermute(sent, 'c', SWAP)  3.29 us
    ppermute x4, waiting for transfers between devices, per_device(): other = lax.ppermute(held, ('z', 'yl'), partner(mask))  3 us
    convert_element_type x1, other arithmetic, per_device(): lax.dynamic_slice(blocks, (0, of, 0, 0), (8, 1, ROWS, CH)).astype(jnp.int16)  2.44 us
  transfers between devices with their start and end apart: 14, of which 7 were waited for; matrix products, arithmetic and copies ran while one was open for 0% of the time, Pallas kernels for 25%

profile of v3, /device:TPU:1, one launch (start us, length us, event | category | flops | bytes accessed | tf_op | source)
XLA Modules:
  0.0 98.3 jit_solution(16376997548333696024)
XLA Ops:
  1.5 2.4 %dynamic-slice_convert_fusion = (s16[8,1,256,256]{3,2,1,0:T(8,128)(2,1)S(1)}, s16[8,1,256,256]{3,2,1,0:T(8,128)(2,1)S(1)}) fusion(s32[8,2,256,256]{3,2,1,0:T(8,128)} %bitcast.11, s32[]{:T(128)S(6)} %select_n.34, s32[]{:T(128)S(6)} %select_n.33), kind=kLoop, calls=%fused_computation | loop fusion | flops 1048576 | bytes 6291464 | tf_op jit(solution)/shard_map/convert_element_type | solution.py:274
  4.0 3.3 %collective-permute-start.2 = (s16[8,1,256,256]{3,2,1,0:T(8,128)(2,1)S(1)}, s16[8,1,256,256]{3,2,1,0:T(8,128)(2,1)S(1)}, u32[]{:S(2)}, u32[]{:S(2)}) collective-permute-start(s16[8,1,256,256]{3,2,1,0:T(8,128)(2,1)S(1)} %get-tuple-element.32), channel_id=1, source_target_pairs={{0,1},{1,0},{2,3},{3,2},{4,5},{5,4},{6,7},{7,6},{8,9},{9,8},{10,11... | collective-permute-start | bytes 3145736 | tf_op jit(solution)/shard_map/ppermute | solution.py:282
  7.3 5.2 %collective-permute-start = (bf16[1,48,256]{2,1,0:T(8,128)(2,1)S(1)}, bf16[1,48,256]{2,1,0:T(8,128)(2,1)S(1)}, u32[]{:S(2)}, u32[]{:S(2)}) collective-permute-start(bf16[1,48,256]{2,1,0:T(8,128)(2,1)S(1)} %reshape.7.after_ref.a_ref), channel_id=1, source_target_pairs={{0,128},{16,144},{32,160},{48,176},{64,192},{80,208},{96,224},{112... | collective-permute-start | bytes 73736 | tf_op jit(solution)/shard_map/ppermute | solution.py:286
  12.5 4.5 %replicas_1_0.1 = (bf16[4,8,256,512]{3,2,1,0:T(8,128)(2,1)S(1)}, s32[8,128]{1,0:T(8,128)S(1)}) custom-call(s32[10]{0:T(128)S(1)} %stack.43.place, s16[8,1,256,256]{3,2,1,0:T(8,128)(2,1)S(1)} %get-tuple-element.30.travel_ref, bf16[1,48,256]{2,1,0:T(8,128)(2,1)S(1)} %reshape.7.after_ref.a_ref), custom_call_target="tpu_custom_call" | custom-call | flops 4499999744 | bytes 1000000 | tf_op jit(solution)/shard_map/replicas_1_0/pallas_call | solution.py:113
  18.3 4.5 %replicas_0_0.1 = (bf16[4,8,256,512]{3,2,1,0:T(8,128)(2,1)S(1)}, s32[8,128]{1,0:T(8,128)S(1)}) custom-call(s32[10]{0:T(128)S(1)} %stack.43.place, s16[8,1,256,256]{3,2,1,0:T(8,128)(2,1)S(1)} %collective-permute-done.2.travel_ref, bf16[2,48,256]{2,1,0:T(8,128)(2,1)S(1)} %join_1.1.after_ref.a_ref), custom_call_target="tpu_custom_call" | custom-call | flops 4499999744 | bytes 1000000 | tf_op jit(solution)/shard_map/replicas_0_0/pallas_call | solution.py:113
  23.7 4.5 %replicas_1_4.1 = (bf16[4,8,256,512]{3,2,1,0:T(8,128)(2,1)S(1)}, s32[8,128]{1,0:T(8,128)S(1)}) custom-call(s32[10]{0:T(128)S(1)} %stack.43.place, s16[8,1,256,256]{3,2,1,0:T(8,128)(2,1)S(1)} %get-tuple-element.30.travel_ref, bf16[4,48,256]{2,1,0:T(8,128)(2,1)S(1)} %join_2.1.after_ref.a_ref), custom_call_target="tpu_custom_call" | custom-call | flops 4499999744 | bytes 1000000 | tf_op jit(solution)/shard_map/replicas_1_4/pallas_call | solution.py:113
  28.3 1.4 %collective-permute-start.4 = (bf16[8,48,256]{2,1,0:T(8,128)(2,1)S(1)}, bf16[8,48,256]{2,1,0:T(8,128)(2,1)S(1)}, u32[]{:S(2)}, u32[]{:S(2)}) collective-permute-start(bf16[8,48,256]{2,1,0:T(8,128)(2,1)S(1)} %join_4.1.low_ref), channel_id=1, source_target_pairs={{0,16},{16,0},{32,48},{48,32},{64,80},{80,64},{96,112},{112,96},{1... | collective-permute-start | bytes 589832 | tf_op jit(solution)/shard_map/ppermute | solution.py:286
  30.9 3.0 %collective-permute-done.4.high_ref = bf16[8,48,256]{2,1,0:T(8,128)(2,1)S(1)} collective-permute-done((bf16[8,48,256]{2,1,0:T(8,128)(2,1)S(1)}, bf16[8,48,256]{2,1,0:T(8,128)(2,1)S(1)}, u32[]{:S(2)}, u32[]{:S(2)}) %collective-permute-start.4) | collective-permute-done | bytes 196640 | tf_op jit(solution)/shard_map/ppermute | solution.py:286
  33.9 1.8 %collective-permute-start.6 = (bf16[8,48,256]{2,1,0:T(8,128)(2,1)S(1)}, bf16[8,48,256]{2,1,0:T(8,128)(2,1)S(1)}, u32[]{:S(2)}, u32[]{:S(2)}) collective-permute-start(bf16[8,48,256]{2,1,0:T(8,128)(2,1)S(1)} %collective-permute-done.4.high_ref), channel_id=1, source_target_pairs={{0,1},{1,0},{2,3},{3,2},{4,5},{5,4},{6,7},{7,6},{8,9},{9,8},{10,11... | collective-permute-start | bytes 589832 | tf_op jit(solution)/shard_map/ppermute | solution.py:293
  37.2 1.3 %beams_3.1.after_ref = bf16[264,768]{1,0:T(8,128)(2,1)S(1)} custom-call(bf16[4,8,256,512]{3,2,1,0:T(8,128)(2,1)S(1)} %get-tuple-element.36.a_ref, bf16[4,8,256,512]{3,2,1,0:T(8,128)(2,1)S(1)} %get-tuple-element.37.b_ref, bf16[8,96,512]{2,1,0:T(8,128)(2,1)S(1)} %get-tuple-element.38.wa_ref, bf16[8,96,512]{2,1,0:T(8,128)(2,1)S(1)} %get-tuple-element.39.wb_ref, ...), custom_call_target="tpu_custom_call" | custom-call | flops 3000000000 | bytes 1000000 | tf_op jit(solution)/shard_map/beams_3/pallas_call | solution.py:161
  38.5 1.3 %beams_2.1 = bf16[264,768]{1,0:T(8,128)(2,1)S(1)} custom-call(bf16[4,8,256,512]{3,2,1,0:T(8,128)(2,1)S(1)} %get-tuple-element.36.a_ref, bf16[4,8,256,512]{3,2,1,0:T(8,128)(2,1)S(1)} %get-tuple-element.37.b_ref, bf16[8,96,512]{2,1,0:T(8,128)(2,1)S(1)} %get-tuple-element.38.wa_ref, bf16[8,96,512]{2,1,0:T(8,128)(2,1)S(1)} %get-tuple-element.39.wb_ref, ...), custom_call_target="tpu_custom_call" | custom-call | flops 3000000000 | bytes 1000000 | tf_op jit(solution)/shard_map/beams_2/pallas_call | solution.py:161
  39.9 1.3 %beams_1.1 = bf16[264,768]{1,0:T(8,128)(2,1)S(1)} custom-call(bf16[4,8,256,512]{3,2,1,0:T(8,128)(2,1)S(1)} %get-tuple-element.36.a_ref, bf16[4,8,256,512]{3,2,1,0:T(8,128)(2,1)S(1)} %get-tuple-element.37.b_ref, bf16[8,96,512]{2,1,0:T(8,128)(2,1)S(1)} %get-tuple-element.38.wa_ref, bf16[8,96,512]{2,1,0:T(8,128)(2,1)S(1)} %get-tuple-element.39.wb_ref, ...), custom_call_target="tpu_custom_call" | custom-call | flops 3000000000 | bytes 1000000 | tf_op jit(solution)/shard_map/beams_1/pallas_call | solution.py:161
  41.2 1.3 %beams_0.1 = bf16[264,768]{1,0:T(8,128)(2,1)S(1)} custom-call(bf16[4,8,256,512]{3,2,1,0:T(8,128)(2,1)S(1)} %get-tuple-element.36.a_ref, bf16[4,8,256,512]{3,2,1,0:T(8,128)(2,1)S(1)} %get-tuple-element.37.b_ref, bf16[8,96,512]{2,1,0:T(8,128)(2,1)S(1)} %get-tuple-element.38.wa_ref, bf16[8,96,512]{2,1,0:T(8,128)(2,1)S(1)} %get-tuple-element.39.wb_ref, ...), custom_call_target="tpu_custom_call" | custom-call | flops 3000000000 | bytes 1000000 | tf_op jit(solution)/shard_map/beams_0/pallas_call | solution.py:161
  42.5 5.5 %collective-permute-start.7 = (bf16[264,768]{1,0:T(8,128)(2,1)S(1)}, bf16[264,768]{1,0:T(8,128)(2,1)S(1)}, u32[]{:S(2)}, u32[]{:S(2)}) collective-permute-start(bf16[264,768]{1,0:T(8,128)(2,1)S(1)} %beams_0.1), channel_id=1, source_target_pairs={{0,10},{2,8},{4,14},{6,12},{8,2},{10,0},{12,6},{14,4},{1,11},{3,9}... | collective-permute-start | bytes 1216520 | tf_op jit(solution)/shard_map/ppermute | solution.py:309
  48.0 5.0 %collective-permute-start.9 = (bf16[264,768]{1,0:T(8,128)(2,1)S(1)}, bf16[264,768]{1,0:T(8,128)(2,1)S(1)}, u32[]{:S(2)}, u32[]{:S(2)}) collective-permute-start(bf16[264,768]{1,0:T(8,128)(2,1)S(1)} %beams_2.1), channel_id=1, source_target_pairs={{0,14},{2,12},{4,2},{6,0},{8,6},{10,4},{12,10},{14,8},{1,15},{3,13... | collective-permute-start | bytes 1216520 | tf_op jit(solution)/shard_map/ppermute | solution.py:309
  53.0 5.1 %replicas_0_4.1 = (bf16[4,8,256,512]{3,2,1,0:T(8,128)(2,1)S(1)}, s32[8,128]{1,0:T(8,128)}) custom-call(s32[10]{0:T(128)S(1)} %stack.43.place, s16[8,1,256,256]{3,2,1,0:T(8,128)(2,1)S(1)} %collective-permute-done.2.travel_ref, bf16[264,768]{1,0:T(8,128)(2,1)S(1)} %beams_3.1.after_ref), custom_call_target="tpu_custom_call" | custom-call | flops 4499999744 | bytes 1000000 | tf_op jit(solution)/shard_map/replicas_0_4/pallas_call | solution.py:113
  59.5 12.7 %collective-permute-done.8.refs_1_ = bf16[264,768]{1,0:T(8,128)(2,1)S(1)} collective-permute-done((bf16[264,768]{1,0:T(8,128)(2,1)S(1)}, bf16[264,768]{1,0:T(8,128)(2,1)S(1)}, u32[]{:S(2)}, u32[]{:S(2)}) %collective-permute-start.8) | collective-permute-done | bytes 405536 | tf_op jit(solution)/shard_map/ppermute | solution.py:309
  75.7 3.0 %collective-permute-start.11 = (bf16[264,768]{1,0:T(8,128)(2,1)S(1)}, bf16[264,768]{1,0:T(8,128)(2,1)S(1)}, u32[]{:S(2)}, u32[]{:S(2)}) collective-permute-start(bf16[264,768]{1,0:T(8,128)(2,1)S(1)} %beams_4.1), channel_id=1, source_target_pairs={{0,2},{2,0},{4,6},{6,4},{8,10},{10,8},{12,14},{14,12},{1,3},{3,1},... | collective-permute-start | bytes 1216520 | tf_op jit(solution)/shard_map/ppermute | solution.py:309
  78.7 1.6 %collective-permute-start.12 = (bf16[264,768]{1,0:T(8,128)(2,1)S(1)}, bf16[264,768]{1,0:T(8,128)(2,1)S(1)}, u32[]{:S(2)}, u32[]{:S(2)}) collective-permute-start(bf16[264,768]{1,0:T(8,128)(2,1)S(1)} %beams_5.1), channel_id=1, source_target_pairs={{0,4},{2,6},{4,8},{6,10},{8,12},{10,14},{12,0},{14,2},{1,5},{3,7},... | collective-permute-start | bytes 1216520 | tf_op jit(solution)/shard_map/ppermute | solution.py:309
  80.3 2.0 %collective-permute-start.13 = (bf16[264,768]{1,0:T(8,128)(2,1)S(1)}, bf16[264,768]{1,0:T(8,128)(2,1)S(1)}, u32[]{:S(2)}, u32[]{:S(2)}) collective-permute-start(bf16[264,768]{1,0:T(8,128)(2,1)S(1)} %beams_6.1), channel_id=1, source_target_pairs={{0,12},{2,14},{4,0},{6,2},{8,4},{10,6},{12,8},{14,10},{1,13},{3,15... | collective-permute-start | bytes 1216520 | tf_op jit(solution)/shard_map/ppermute | solution.py:309
  82.3 2.6 %collective-permute-done.10.refs_3_ = bf16[264,768]{1,0:T(8,128)(2,1)S(1)} collective-permute-done((bf16[264,768]{1,0:T(8,128)(2,1)S(1)}, bf16[264,768]{1,0:T(8,128)(2,1)S(1)}, u32[]{:S(2)}, u32[]{:S(2)}) %collective-permute-start.10) | collective-permute-done | bytes 405536 | tf_op jit(solution)/shard_map/ppermute | solution.py:309
  86.2 8.1 %collective-permute-done.12.refs_5_ = bf16[264,768]{1,0:T(8,128)(2,1)S(1)} collective-permute-done((bf16[264,768]{1,0:T(8,128)(2,1)S(1)}, bf16[264,768]{1,0:T(8,128)(2,1)S(1)}, u32[]{:S(2)}, u32[]{:S(2)}) %collective-permute-start.12) | collective-permute-done | bytes 405536 | tf_op jit(solution)/shard_map/ppermute | solution.py:309
  94.3 1.9 %collective-permute-done.13.refs_6_ = bf16[264,768]{1,0:T(8,128)(2,1)S(1)} collective-permute-done((bf16[264,768]{1,0:T(8,128)(2,1)S(1)}, bf16[264,768]{1,0:T(8,128)(2,1)S(1)}, u32[]{:S(2)}, u32[]{:S(2)}) %collective-permute-start.13) | collective-permute-done | bytes 405536 | tf_op jit(solution)/shard_map/ppermute | solution.py:309
  96.2 2.1 %finish.1 = f32[48,256]{1,0:T(8,128)} custom-call(s32[10]{0:T(128)S(1)} %stack.43.place, bf16[264,768]{1,0:T(8,128)(2,1)S(1)} %collective-permute-done.7.refs_0_, bf16[264,768]{1,0:T(8,128)(2,1)S(1)} %collective-permute-done.8.refs_1_, bf16[264,768]{1,0:T(8,128)(2,1)S(1)} %collective-permute-done.9.refs_2_, ...), custom_call_target="tpu_custom_call" | custom-call | tf_op jit(solution)/shard_map/finish/pallas_call | solution.py:248
  (30 shorter events, 12.6 us)
Async XLA Ops:
  4.0 14.3 %collective-permute-start.2 = (s16[8,1,256,256]{3,2,1,0:T(8,128)(2,1)S(1)}, s16[8,1,256,256]{3,2,1,0:T(8,128)(2,1)S(1)}, u32[]{:S(2)}, u32[]{:S(2)}) collective-permute-start(s16[8,1,256,256]{3,2,1,0:T(8,128)(2,1)S(1)} %get-tuple-element.32), channel_id=1, source_target_pairs={{0,1},{1,0},{2,3},{3,2},{4,5},{5,4},{6,7},{7,6},{8,9},{9,8},{10,11... | collective-permute-start | bytes 3145736 | tf_op jit(solution)/shard_map/ppermute | solution.py:282
  7.3 9.7 %collective-permute-start = (bf16[1,48,256]{2,1,0:T(8,128)(2,1)S(1)}, bf16[1,48,256]{2,1,0:T(8,128)(2,1)S(1)}, u32[]{:S(2)}, u32[]{:S(2)}) collective-permute-start(bf16[1,48,256]{2,1,0:T(8,128)(2,1)S(1)} %reshape.7.after_ref.a_ref), channel_id=1, source_target_pairs={{0,128},{16,144},{32,160},{48,176},{64,192},{80,208},{96,224},{112... | collective-permute-start | bytes 73736 | tf_op jit(solution)/shard_map/ppermute | solution.py:286
  17.1 5.8 %collective-permute-start.1 = (bf16[2,48,256]{2,1,0:T(8,128)(2,1)S(1)}, bf16[2,48,256]{2,1,0:T(8,128)(2,1)S(1)}, u32[]{:S(2)}, u32[]{:S(2)}) collective-permute-start(bf16[2,48,256]{2,1,0:T(8,128)(2,1)S(1)} %join_1.1.after_ref.a_ref), channel_id=1, source_target_pairs={{0,64},{16,80},{32,96},{48,112},{64,0},{80,16},{96,32},{112,48},{1... | collective-permute-start | bytes 147464 | tf_op jit(solution)/shard_map/ppermute | solution.py:286
  22.9 5.4 %collective-permute-start.3 = (bf16[4,48,256]{2,1,0:T(8,128)(2,1)S(1)}, bf16[4,48,256]{2,1,0:T(8,128)(2,1)S(1)}, u32[]{:S(2)}, u32[]{:S(2)}) collective-permute-start(bf16[4,48,256]{2,1,0:T(8,128)(2,1)S(1)} %join_2.1.after_ref.a_ref), channel_id=1, source_target_pairs={{0,32},{16,48},{32,0},{48,16},{64,96},{80,112},{96,64},{112,80},{1... | collective-permute-start | bytes 294920 | tf_op jit(solution)/shard_map/ppermute | solution.py:286
  28.3 5.6 %collective-permute-start.4 = (bf16[8,48,256]{2,1,0:T(8,128)(2,1)S(1)}, bf16[8,48,256]{2,1,0:T(8,128)(2,1)S(1)}, u32[]{:S(2)}, u32[]{:S(2)}) collective-permute-start(bf16[8,48,256]{2,1,0:T(8,128)(2,1)S(1)} %join_4.1.low_ref), channel_id=1, source_target_pairs={{0,16},{16,0},{32,48},{48,32},{64,80},{80,64},{96,112},{112,96},{1... | collective-permute-start | bytes 589832 | tf_op jit(solution)/shard_map/ppermute | solution.py:286
  29.7 6.5 %collective-permute-start.5 = (bf16[8,48,256]{2,1,0:T(8,128)(2,1)S(1)}, bf16[8,48,256]{2,1,0:T(8,128)(2,1)S(1)}, u32[]{:S(2)}, u32[]{:S(2)}) collective-permute-start(bf16[8,48,256]{2,1,0:T(8,128)(2,1)S(1)} %join_4.1.low_ref), channel_id=1, source_target_pairs={{0,1},{1,0},{2,3},{3,2},{4,5},{5,4},{6,7},{7,6},{8,9},{9,8},{10,11... | collective-permute-start | bytes 589832 | tf_op jit(solution)/shard_map/ppermute | solution.py:288
  33.9 2.9 %collective-permute-start.6 = (bf16[8,48,256]{2,1,0:T(8,128)(2,1)S(1)}, bf16[8,48,256]{2,1,0:T(8,128)(2,1)S(1)}, u32[]{:S(2)}, u32[]{:S(2)}) collective-permute-start(bf16[8,48,256]{2,1,0:T(8,128)(2,1)S(1)} %collective-permute-done.4.high_ref), channel_id=1, source_target_pairs={{0,1},{1,0},{2,3},{3,2},{4,5},{5,4},{6,7},{7,6},{8,9},{9,8},{10,11... | collective-permute-start | bytes 589832 | tf_op jit(solution)/shard_map/ppermute | solution.py:293
  42.5 15.7 %collective-permute-start.7 = (bf16[264,768]{1,0:T(8,128)(2,1)S(1)}, bf16[264,768]{1,0:T(8,128)(2,1)S(1)}, u32[]{:S(2)}, u32[]{:S(2)}) collective-permute-start(bf16[264,768]{1,0:T(8,128)(2,1)S(1)} %beams_0.1), channel_id=1, source_target_pairs={{0,10},{2,8},{4,14},{6,12},{8,2},{10,0},{12,6},{14,4},{1,11},{3,9}... | collective-permute-start | bytes 1216520 | tf_op jit(solution)/shard_map/ppermute | solution.py:309
  48.0 24.2 %collective-permute-start.8 = (bf16[264,768]{1,0:T(8,128)(2,1)S(1)}, bf16[264,768]{1,0:T(8,128)(2,1)S(1)}, u32[]{:S(2)}, u32[]{:S(2)}) collective-permute-start(bf16[264,768]{1,0:T(8,128)(2,1)S(1)} %beams_1.1), channel_id=1, source_target_pairs={{0,6},{2,4},{4,10},{6,8},{8,14},{10,12},{12,2},{14,0},{1,7},{3,5},... | collective-permute-start | bytes 1216520 | tf_op jit(solution)/shard_map/ppermute | solution.py:309
  48.0 26.4 %collective-permute-start.9 = (bf16[264,768]{1,0:T(8,128)(2,1)S(1)}, bf16[264,768]{1,0:T(8,128)(2,1)S(1)}, u32[]{:S(2)}, u32[]{:S(2)}) collective-permute-start(bf16[264,768]{1,0:T(8,128)(2,1)S(1)} %beams_2.1), channel_id=1, source_target_pairs={{0,14},{2,12},{4,2},{6,0},{8,6},{10,4},{12,10},{14,8},{1,15},{3,13... | collective-permute-start | bytes 1216520 | tf_op jit(solution)/shard_map/ppermute | solution.py:309
  53.0 31.9 %collective-permute-start.10 = (bf16[264,768]{1,0:T(8,128)(2,1)S(1)}, bf16[264,768]{1,0:T(8,128)(2,1)S(1)}, u32[]{:S(2)}, u32[]{:S(2)}) collective-permute-start(bf16[264,768]{1,0:T(8,128)(2,1)S(1)} %beams_3.1.after_ref), channel_id=1, source_target_pairs={{0,8},{2,10},{4,12},{6,14},{8,0},{10,2},{12,4},{14,6},{1,9},{3,11}... | collective-permute-start | bytes 1216520 | tf_op jit(solution)/shard_map/ppermute | solution.py:309
  75.7 20.5 %copy-start = (s32[2,768]{1,0:T(2,128)S(1)}, s32[2,768]{1,0:T(2,128)}, u32[]{:S(2)}) copy-start(s32[2,768]{1,0:T(2,128)} %constant.63.clone.refs_10_) | copy-start | bytes 18436
  75.7 10.5 %collective-permute-start.11 = (bf16[264,768]{1,0:T(8,128)(2,1)S(1)}, bf16[264,768]{1,0:T(8,128)(2,1)S(1)}, u32[]{:S(2)}, u32[]{:S(2)}) collective-permute-start(bf16[264,768]{1,0:T(8,128)(2,1)S(1)} %beams_4.1), channel_id=1, source_target_pairs={{0,2},{2,0},{4,6},{6,4},{8,10},{10,8},{12,14},{14,12},{1,3},{3,1},... | collective-permute-start | bytes 1216520 | tf_op jit(solution)/shard_map/ppermute | solution.py:309
  78.7 15.6 %collective-permute-start.12 = (bf16[264,768]{1,0:T(8,128)(2,1)S(1)}, bf16[264,768]{1,0:T(8,128)(2,1)S(1)}, u32[]{:S(2)}, u32[]{:S(2)}) collective-permute-start(bf16[264,768]{1,0:T(8,128)(2,1)S(1)} %beams_5.1), channel_id=1, source_target_pairs={{0,4},{2,6},{4,8},{6,10},{8,12},{10,14},{12,0},{14,2},{1,5},{3,7},... | collective-permute-start | bytes 1216520 | tf_op jit(solution)/shard_map/ppermute | solution.py:309
  80.3 15.9 %collective-permute-start.13 = (bf16[264,768]{1,0:T(8,128)(2,1)S(1)}, bf16[264,768]{1,0:T(8,128)(2,1)S(1)}, u32[]{:S(2)}, u32[]{:S(2)}) collective-permute-start(bf16[264,768]{1,0:T(8,128)(2,1)S(1)} %beams_6.1), channel_id=1, source_target_pairs={{0,12},{2,14},{4,0},{6,2},{8,4},{10,6},{12,8},{14,10},{1,13},{3,15... | collective-permute-start | bytes 1216520 | tf_op jit(solution)/shard_map/ppermute | solution.py:309

commit v4 on v2

--- a/solution.py
+++ b/solution.py
@@ -97,7 +97,7 @@
         rows = pl.ds(pl.multiple_of(step * TILE, TILE), TILE)
         for half in range(CH // 128):
             lanes = slice(half * 128, (half + 1) * 128)
-            cosines, sines = replica_tiles(travel_ref[0, 0, rows, lanes].astype(jnp.int32))
+            cosines, sines = replica_tiles(travel_ref[0, rows, lanes].astype(jnp.int32))
             for f in range(NF):
                 rep_ref[block, f, rows, lanes] = cosines[f].astype(bf16)
                 rep_ref[block, f, rows, CH + half * 128 : CH + (half + 1) * 128] = sines[f].astype(bf16)
@@ -106,25 +106,25 @@
     lax.fori_loop(0, ROWS // TILE, body, 0)
 
 
-def replicas(place, travel, after, first, own):
+def replicas(place, travel, after, name):
     def index(i, p):
-        return (p[first + i], p[8] if own else 0, 0, 0)
+        return (p[i], 0, 0)
 
     return pl.pallas_call(
         replicas_kernel,
         grid_spec=pltpu.PrefetchScalarGridSpec(
             num_scalar_prefetch=1,
             grid=(4,),
-            in_specs=[pl.BlockSpec((1, 1, ROWS, CH), index), VMEM],
+            in_specs=[pl.BlockSpec((1, ROWS, CH), index), VMEM],
             out_specs=[VMEM, VMEM],
         ),
         out_shape=[
             jax.ShapeDtypeStruct((4, NF, ROWS, 2 * CH), bf16),
             jax.ShapeDtypeStruct((8, 128), jnp.int32),
         ],
-        cost_estimate=pl.CostEstimate(flops=4_500_000_000, bytes_accessed=1_000_000, transcendentals=0),
+        cost_estimate=pl.CostEstimate(flops=40_000_000_000, bytes_accessed=1_000_000, transcendentals=0),
         compiler_params=pltpu.CompilerParams(vmem_limit_bytes=4 << 20),
-        name=f"replicas_{int(own)}_{first}",
+        name=f"replicas_{name}",
     )(place, travel, after)
 
 
@@ -146,9 +146,11 @@
     )(a, b, token)
 
 
-def beams_kernel(a_ref, b_ref, wa_ref, wb_ref, na_ref, nb_ref, out_ref, *, slot):
+def beams_kernel(r0, r1, r2, r3, wa_ref, wb_ref, na_ref, nb_ref, out_ref, *, slot):
     columns = [
-        product(a_ref[slot, f], wa_ref[f]) + product(b_ref[slot, f], wb_ref[f]) for f in range(NF)
+        (product(r0[slot, f], wa_ref[0, f]) + product(r1[slot, f], wb_ref[0, f]))
+        + (product(r2[slot, f], wa_ref[1, f]) + product(r3[slot, f], wb_ref[1, f]))
+        for f in range(NF)
     ]
     out_ref[0:ROWS] = jnp.concatenate(columns, axis=1).astype(out_ref.dtype)
     if out_ref.shape[0] > ROWS:
@@ -156,11 +158,11 @@
 
 
 def beams_block(reps, weights, norms, step):
-    own = STEPS[step] == (0, 0)
+    own = STEPS[step] == 0
     rows = ROWS if own else ROWS + NORM_ROWS
     return pl.pallas_call(
-        functools.partial(beams_kernel, slot=step % 4),
-        in_specs=[VMEM] * 6,
+        functools.partial(beams_kernel, slot=step),
+        in_specs=[VMEM] * 8,
         out_specs=VMEM,
         out_shape=jax.ShapeDtypeStruct((rows, NF * COLS), f32 if own else bf16),
         cost_estimate=pl.CostEstimate(flops=3_000_000_000, bytes_accessed=1_000_000, transcendentals=0),
@@ -169,34 +171,35 @@
     )(*reps, *weights, *norms)
 
 
-def prepare_kernel(low_ref, high_ref, token_ref, w_ref, norm_ref, wide, *, first_row):
-    for g in range(16):
-        source = (low_ref, high_ref)[g // 8]
-        for half in range(CH // 128):
-            lanes = slice(half * 128, (half + 1) * 128)
-            wide[half, g * 48 : (g + 1) * 48, :] = source[g % 8, :, lanes].astype(f32)
+def prepare_kernel(low_ref, high_ref, w_ref, norm_ref, wide, *, first_row):
     squares = jnp.zeros((COLS, CH), f32)
-    for f in range(NF):
-        real, imag = [
-            jnp.concatenate(
-                [
-                    jnp.concatenate(
-                        [
-                            wide[half, pl.ds(p * 24 + f * 3 + i, 16, stride=48), :]
-                            for half in range(CH // 128)
-                        ],
-                        axis=1,
-                    )
-                    for i in range(3)
-                ],
-                axis=0,
-            )
-            for p in range(2)
-        ]
-        both = jnp.concatenate([real, imag], axis=0)
-        squares = squares + both * both
-        w_ref[f, :, 0:CH] = both.astype(bf16)
-        w_ref[f, :, CH : 2 * CH] = jnp.concatenate([-imag, real], axis=0).astype(bf16)
+    for flip in range(2):
+        for g in range(16):
+            source = (low_ref, high_ref)[g // 8]
+            for half in range(CH // 128):
+                lanes = slice(half * 128, (half + 1) * 128)
+                wide[half, g * 48 : (g + 1) * 48, :] = source[flip * 8 + g % 8, :, lanes].astype(f32)
+        for f in range(NF):
+            real, imag = [
+                jnp.concatenate(
+                    [
+                        jnp.concatenate(
+                            [
+                                wide[half, pl.ds(p * 24 + f * 3 + i, 16, stride=48), :]
+                                for half in range(CH // 128)
+                            ],
+                            axis=1,
+                        )
+                        for i in range(3)
+                    ],
+                    axis=0,
+                )
+                for p in range(2)
+            ]
+            both = jnp.concatenate([real, imag], axis=0)
+            squares = squares + both * both
+            w_ref[flip, f, :, 0:CH] = both.astype(bf16)
+            w_ref[flip, f, :, CH : 2 * CH] = jnp.concatenate([-imag, real], axis=0).astype(bf16)
     sums = exact_product(jnp.ones((NORM_ROWS, CH), bf16), squares)
     row = lax.broadcasted_iota(jnp.int32, sums.shape, 0) - first_row
     zero = jnp.zeros_like(sums)
@@ -206,33 +209,33 @@
     norm_ref[...] = jnp.concatenate([split] + [zero] * (NF - 1), axis=1).astype(bf16)
 
 
-def prepare(low, high, token, first_row):
+def prepare(low, high, first_row):
     return pl.pallas_call(
         functools.partial(prepare_kernel, first_row=first_row),
-        in_specs=[VMEM] * 3,
+        in_specs=[VMEM] * 2,
         out_specs=[VMEM, VMEM],
         scratch_shapes=[pltpu.VMEM((CH // 128, 768, 128), f32)],
         out_shape=[
-            jax.ShapeDtypeStruct((NF, COLS, 2 * CH), bf16),
+            jax.ShapeDtypeStruct((2, NF, COLS, 2 * CH), bf16),
             jax.ShapeDtypeStruct((NORM_ROWS, NF * COLS), bf16),
         ],
         cost_estimate=pl.CostEstimate(flops=1_000_000_000, bytes_accessed=1_000_000, transcendentals=0),
         compiler_params=pltpu.CompilerParams(vmem_limit_bytes=6 << 20),
         name=f"prepare_{first_row}",
-    )(low, high, token)
+    )(low, high)
 
 
 def column_tables():
     slot = np.arange(NF * COLS) % 48
     place = slot % 16
-    relative = sum(((place >> bit) & 1) << (3 - bit) for bit in range(4))
+    relative = sum(((place >> bit) & 1) * mask for bit, mask in enumerate((8, 4, 1, 2)))
     return np.stack([relative, slot // 16]).astype(np.int32)
 
 
 def finish_kernel(place, *refs, count):
     *received, own_ref, na_ref, nb_ref, table_ref, out_ref = refs
     window = lax.broadcasted_iota(jnp.int32, (48, NF * COLS), 0)
-    source = table_ref[0:1, :] ^ place[9]
+    source = table_ref[0:1, :] ^ place[4]
     pick = jnp.where(window == 3 * source + table_ref[1:2, :], 1.0, 0.0).astype(bf16)
     beams = own_ref[...]
     norm_rows = na_ref[...].astype(f32) + nb_ref[...].astype(f32)
@@ -247,7 +250,7 @@
 def finish(place, received, own, norms, count):
     return pl.pallas_call(
         functools.partial(finish_kernel, count=count),
-        in_specs=[pl.BlockSpec(memory_space=pltpu.SMEM)] + [VMEM] * 11,
+        in_specs=[pl.BlockSpec(memory_space=pltpu.SMEM)] + [VMEM] * 7,
         out_specs=VMEM,
         out_shape=jax.ShapeDtypeStruct((48, ROWS), f32),
         compiler_params=pltpu.CompilerParams(vmem_limit_bytes=8 << 20),
@@ -255,8 +258,7 @@
     )(place, *received, own, *norms, jnp.asarray(column_tables()))
 
 
-LAG = 3
-STEPS = ((2, 1), (1, 1), (3, 1), (2, 0), (0, 1), (1, 0), (3, 0), (0, 0))
+STEPS = (2, 1, 3, 0)
 SWAP = [(0, 1), (1, 0)]
 
 
@@ -266,42 +268,56 @@
 
 def per_device(spectra, travel, quality):
     x, yh, core = lax.axis_index("x"), lax.axis_index("yh"), lax.axis_index("c")
-    order = [((x + dx) % 4) * 2 + (yh ^ dy) for dx, dy in STEPS]
-    place = jnp.stack(order + [core, lax.axis_index("z") * 2 + lax.axis_index("yl")]).astype(jnp.int32)
-    blocks = travel.reshape(8, 2, ROWS, CH)
-    sent = lax.dynamic_slice(blocks, (0, 1 - core, 0, 0), (8, 1, ROWS, CH)).astype(jnp.int16)
+    order = [(x + dx) % 4 for dx in STEPS]
+    place = jnp.stack(order + [lax.axis_index("z") * 2 + lax.axis_index("yl")]).astype(jnp.int32)
+    blocks = travel.reshape(4, 2, 2, ROWS, CH)
+
+    def travel_for(flip_y, flip_c):
+        return lax.dynamic_slice(
+            blocks, (0, yh ^ flip_y, core ^ flip_c, 0, 0), (4, 1, 1, ROWS, CH)
+        ).reshape(4, ROWS, CH).astype(jnp.int16)
+
     block = (spectra * quality.astype(bf16)).reshape(1, 48, CH)
-    block, sent, place = tie(block, sent, place)
-
-    def partner(mask):
-        return [(i, i ^ mask) for i in range(16)]
-
-    arrived = lax.ppermute(sent, "c", SWAP)
+    parts = [travel_for(flip // 2, flip % 2) for flip in range(4)]
+    block, place, *parts = tie(block, place, *parts)
+
+    def moved(flip):
+        return lax.ppermute(parts[flip], ("yh", "c"), [(i, i ^ flip) for i in range(4)])
+
+    def exchange(values, stage):
+        if stage == 3:
+            return lax.ppermute(values, "yh", SWAP)
+        mask = (8, 4, 1, None, 2)[stage]
+        return lax.ppermute(values, ("z", "yl"), [(i, i ^ mask) for i in range(16)])
+
+    far, near, both = moved(2), moved(1), moved(3)
     held = block
-    reps = []
-    for stage, mask in enumerate((8, 4, 2, 1)):
-        other = lax.ppermute(held, ("z", "yl"), partner(mask))
-        if stage == 3:
-            held_swapped = lax.ppermute(held, "c", SWAP)
-        rep, token = replicas(place, blocks if stage < 2 else arrived, held, 4 * (stage % 2), stage < 2)
-        reps.append(rep)
-        if stage < 3:
-            held = join(held, other, token)
+    other = exchange(held, 0)
+    rep_own, token = replicas(place, parts[0], held, "own")
+    held = join(held, other, token)
+    other = exchange(held, 1)
+    rep_near, token = replicas(place, near, held, "near")
+    held = join(held, other, token)
+    for stage in (2, 3):
+        other = exchange(held, stage)
+        held = join(held, other, token)
+    held, far, both = tie(held, far, both)
+    other = exchange(held, 4)
+    held_swapped = lax.ppermute(held, "c", SWAP)
+    rep_far, token = replicas(place, far, held, "far")
     other_swapped = lax.ppermute(other, "c", SWAP)
-    w_a, n_a = prepare(held, other, token, 0)
-    w_b, n_b = prepare(held_swapped, other_swapped, token, 3)
-    weights, norms = (w_a, w_b), (n_a, n_b)
+    rep_both, _ = replicas(place, both, other, "both")
+    w_a, n_a = prepare(held, other, 0)
+    w_b, n_b = prepare(held_swapped, other_swapped, 3)
+    reps = (rep_own, rep_near, rep_far, rep_both)
     received = []
-    for step, (dx, dy) in enumerate(STEPS):
-        if step >= LAG:
-            n_a, received[step - LAG] = tie(n_a, received[step - LAG])
-        beams = beams_block((reps[step // 4], reps[2 + step // 4]), weights, (n_a, n_b), step)
-        if (dx, dy) == (0, 0):
-            kept = beams
-        else:
-            pairs = [(i, ((i // 2 + dx) % 4) * 2 + ((i % 2) ^ dy)) for i in range(8)]
-            received.append(lax.ppermute(beams, ("x", "yh"), pairs))
-    return finish(place, received, kept, (n_a, n_b), float(NF * CH * 16))
+    for step, dx in enumerate(STEPS):
+        if step == 3:
+            n_a, received[0] = tie(n_a, received[0])
+        beams = beams_block(reps, (w_a, w_b), (n_a, n_b), step)
+        if dx:
+            received.append(lax.ppermute(beams, "x", [(i, (i + dx) % 4) for i in range(4)]))
+    return finish(place, received, beams, (n_a, n_b), float(NF * CH * 16))
 
 
 def solution(mesh):

time: 105 us -> 93.6 us (0.89)
  starting transfers between devices: 35.1 us -> 27.4 us
  waiting for transfers between devices: 32.4 us -> 29.4 us
  local copies, waits for them, and re-layouts: 2.33 us -> 0.14 us
    ppermute x12 -> x11, starting transfers between devices: 32.1 us -> 22.8 us  [the longest x4 11.3 us: exchange(): return lax.ppermute(values, ('z', 'yl'), [(i, i ^ mask) for i in range(16)])]
    ppermute x12 -> x11, waiting for transfers between devices: 32.4 us -> 29.4 us  [the longest x4 15 us: exchange(): return lax.ppermute(values, ('z', 'yl'), [(i, i ^ mask) for i in range(16)])]
    unnamed x6 -> x2, local copies, waits for them, and re-layouts: 2.2 us -> 0.01 us
    pallas_call x4, Pallas kernels: 18.1 us -> 19.3 us  [replicas(): pl.pallas_call(replicas_kernel, grid_spec=pltpu.PrefetchScalarGridSpec(nu...]
    pallas_call x8 -> x4, Pallas kernels: 10.5 us -> 9.59 us  [beams_block(): pl.pallas_call(functools.partial(beams_kernel, slot=step), in_specs=[VMEM...]
  transfers between devices with their start and end apart: 14 -> 13, of which waited for: 6 -> 5; matrix products, arithmetic and copies ran while one was open for 0% -> 0% of each run, Pallas kernels for 26% -> 29%
where the time goes in v4:
time: 93.6 us; the launch traced here: 93.5 us
  Pallas kernels  32.5 us (35%)
  waiting for transfers between devices  29.4 us (31%)
  starting transfers between devices  27.4 us (29%)
  other arithmetic  3.86 us (4%)
    pallas_call x4, Pallas kernels, replicas(): pl.pallas_call(replicas_kernel, grid_spec=pltpu.PrefetchScalarGridSpec(nu...  19.3 us
    ppermute x4, waiting for transfers between devices, exchange(): return lax.ppermute(values, ('z', 'yl'), [(i, i ^ mask) for i in range(16)])  15 us
    ppermute x4, starting transfers between devices, exchange(): return lax.ppermute(values, ('z', 'yl'), [(i, i ^ mask) for i in range(16)])  11.3 us
    pallas_call x4, Pallas kernels, beams_block(): pl.pallas_call(functools.partial(beams_kernel, slot=step), in_specs=[VMEM...  9.59 us
    ppermute x3, waiting for transfers between devices, per_device(): lax.ppermute(beams, 'x', [(i, (i + dx) % 4) for i in range(4)])  8.81 us
    ppermute x3, starting transfers between devices, per_device(): lax.ppermute(beams, 'x', [(i, (i + dx) % 4) for i in range(4)])  5.77 us
    ppermute x1, waiting for transfers between devices, exchange(): return lax.ppermute(values, 'yh', SWAP)  5.59 us
    ppermute x3, starting transfers between devices, moved(): lax.ppermute(parts[flip], ('yh', 'c'), [(i, i ^ flip) for i in range(4)])  4.09 us
  transfers between devices with their start and end apart: 13, of which 5 were waited for; matrix products, arithmetic and copies ran while one was open for 0% of the time, Pallas kernels for 29%

profile of v4, /device:TPU:1, one launch (start us, length us, event | category | flops | bytes accessed | tf_op | source)
XLA Modules:
  0.0 93.5 jit_solution(9635549327648527433)
XLA Ops:
  1.6 2.4 %fusion.3 = (s16[4,256,256]{2,1,0:T(8,128)(2,1)S(1)}, s16[4,256,256]{2,1,0:T(8,128)(2,1)S(1)}, s16[4,256,256]{2,1,0:T(8,128)(2,1)S(1)}, s16[4,256,256]{2,1,0:T(8,128)(2,1)S(1)}) fusion(s32[4,2,2,256,256]{4,3,2,1,0:T(8,128)} %bitcast.30, s32[]{:T(128)S(6)} %select_n.42, s32[]{:T(128)S(6)} %select_n.41, s32[]{:T(128)S(6)} %select_n.40, s32[]{:T(128)S(6)} %select_n.39), kind=kLoop, calls=%fused_computation.7 | loop fusion | flops 1048576 | bytes 6291472 | tf_op jit(solution)/shard_map/convert_element_type | solution.py:278
  4.1 7.8 %collective-permute-start = (bf16[1,48,256]{2,1,0:T(8,128)(2,1)S(1)}, bf16[1,48,256]{2,1,0:T(8,128)(2,1)S(1)}, u32[]{:S(2)}, u32[]{:S(2)}) collective-permute-start(bf16[1,48,256]{2,1,0:T(8,128)(2,1)S(1)} %reshape.15.after_ref.a_ref), channel_id=1, source_target_pairs={{0,128},{16,144},{32,160},{48,176},{64,192},{80,208},{96,224},{112... | collective-permute-start | bytes 73736 | tf_op jit(solution)/shard_map/ppermute | solution.py:291
  12.8 2.9 %collective-permute-start.5 = (s16[4,256,256]{2,1,0:T(8,128)(2,1)S(1)}, s16[4,256,256]{2,1,0:T(8,128)(2,1)S(1)}, u32[]{:S(2)}, u32[]{:S(2)}) collective-permute-start(s16[4,256,256]{2,1,0:T(8,128)(2,1)S(1)} %get-tuple-element.32), channel_id=1, source_target_pairs={{0,2},{1,3},{2,0},{3,1},{4,6},{5,7},{6,4},{7,5},{8,10},{9,11},{10,... | collective-permute-start | bytes 1572872 | tf_op jit(solution)/shard_map/ppermute | solution.py:285
  16.0 4.5 %replicas_own.1 = (bf16[4,8,256,512]{3,2,1,0:T(8,128)(2,1)S(1)}, s32[8,128]{1,0:T(8,128)S(1)}) custom-call(s32[5]{0:T(128)S(1)} %stack.23.place, s16[4,256,256]{2,1,0:T(8,128)(2,1)S(1)} %get-tuple-element.28.travel_ref, bf16[1,48,256]{2,1,0:T(8,128)(2,1)S(1)} %reshape.15.after_ref.a_ref), custom_call_target="tpu_custom_call" | custom-call | flops 40000000000 | bytes 1000000 | tf_op jit(solution)/shard_map/replicas_own/pallas_call | solution.py:113
  20.5 1.3 %collective-permute-start.1 = (bf16[2,48,256]{2,1,0:T(8,128)(2,1)S(1)}, bf16[2,48,256]{2,1,0:T(8,128)(2,1)S(1)}, u32[]{:S(2)}, u32[]{:S(2)}) collective-permute-start(bf16[2,48,256]{2,1,0:T(8,128)(2,1)S(1)} %join_1.1.after_ref.a_ref), channel_id=1, source_target_pairs={{0,64},{16,80},{32,96},{48,112},{64,0},{80,16},{96,32},{112,48},{1... | collective-permute-start | bytes 147464 | tf_op jit(solution)/shard_map/ppermute | solution.py:291
  21.8 4.5 %replicas_near.1 = (bf16[4,8,256,512]{3,2,1,0:T(8,128)(2,1)S(1)}, s32[8,128]{1,0:T(8,128)S(1)}) custom-call(s32[5]{0:T(128)S(1)} %stack.23.place, s16[4,256,256]{2,1,0:T(8,128)(2,1)S(1)} %collective-permute-done.2.travel_ref, bf16[2,48,256]{2,1,0:T(8,128)(2,1)S(1)} %join_1.1.after_ref.a_ref), custom_call_target="tpu_custom_call" | custom-call | flops 40000000000 | bytes 1000000 | tf_op jit(solution)/shard_map/replicas_near/pallas_call | solution.py:113
  26.4 1.4 %collective-permute-start.3 = (bf16[4,48,256]{2,1,0:T(8,128)(2,1)S(1)}, bf16[4,48,256]{2,1,0:T(8,128)(2,1)S(1)}, u32[]{:S(2)}, u32[]{:S(2)}) collective-permute-start(bf16[4,48,256]{2,1,0:T(8,128)(2,1)S(1)} %join_2.1.a_ref), channel_id=1, source_target_pairs={{0,16},{16,0},{32,48},{48,32},{64,80},{80,64},{96,112},{112,96},{1... | collective-permute-start | bytes 294920 | tf_op jit(solution)/shard_map/ppermute | solution.py:291
  27.8 13.8 %collective-permute-done.3.b_ref = bf16[4,48,256]{2,1,0:T(8,128)(2,1)S(1)} collective-permute-done((bf16[4,48,256]{2,1,0:T(8,128)(2,1)S(1)}, bf16[4,48,256]{2,1,0:T(8,128)(2,1)S(1)}, u32[]{:S(2)}, u32[]{:S(2)}) %collective-permute-start.3) | collective-permute-done | bytes 98336 | tf_op jit(solution)/shard_map/ppermute | solution.py:291
  41.6 1.6 %collective-permute-start.4 = (bf16[8,48,256]{2,1,0:T(8,128)(2,1)S(1)}, bf16[8,48,256]{2,1,0:T(8,128)(2,1)S(1)}, u32[]{:S(2)}, u32[]{:S(2)}) collective-permute-start(bf16[8,48,256]{2,1,0:T(8,128)(2,1)S(1)} %join_4.1.a_ref), channel_id=1, source_target_pairs={{0,2},{2,0},{1,3},{3,1},{4,6},{6,4},{5,7},{7,5},{8,10},{10,8},{9,1... | collective-permute-start | bytes 589832 | tf_op jit(solution)/shard_map/ppermute | solution.py:289
  43.2 5.6 %collective-permute-done.4.b_ref = bf16[8,48,256]{2,1,0:T(8,128)(2,1)S(1)} collective-permute-done((bf16[8,48,256]{2,1,0:T(8,128)(2,1)S(1)}, bf16[8,48,256]{2,1,0:T(8,128)(2,1)S(1)}, u32[]{:S(2)}, u32[]{:S(2)}) %collective-permute-start.4) | collective-permute-done | bytes 196640 | tf_op jit(solution)/shard_map/ppermute | solution.py:289
  49.7 2.0 %collective-permute-start.8 = (bf16[16,48,256]{2,1,0:T(8,128)(2,1)S(1)}, bf16[16,48,256]{2,1,0:T(8,128)(2,1)S(1)}, u32[]{:S(2)}, u32[]{:S(2)}) collective-permute-start(bf16[16,48,256]{2,1,0:T(8,128)(2,1)S(1)} %join_8.1.low_ref.after_ref), channel_id=1, source_target_pairs={{0,1},{1,0},{2,3},{3,2},{4,5},{5,4},{6,7},{7,6},{8,9},{9,8},{10,11... | collective-permute-start | bytes 1179656 | tf_op jit(solution)/shard_map/ppermute | solution.py:306
  51.7 5.1 %replicas_far.1 = (bf16[4,8,256,512]{3,2,1,0:T(8,128)(2,1)S(1)}, s32[8,128]{1,0:T(8,128)}) custom-call(s32[5]{0:T(128)S(1)} %stack.23.place, s16[4,256,256]{2,1,0:T(8,128)(2,1)S(1)} %collective-permute-done.5.travel_ref, bf16[16,48,256]{2,1,0:T(8,128)(2,1)S(1)} %join_8.1.low_ref.after_ref), custom_call_target="tpu_custom_call" | custom-call | flops 40000000000 | bytes 1000000 | tf_op jit(solution)/shard_map/replicas_far/pallas_call | solution.py:113
  56.8 1.1 %collective-permute-done.7.high_ref.after_ref = bf16[16,48,256]{2,1,0:T(8,128)(2,1)S(1)} collective-permute-done((bf16[16,48,256]{2,1,0:T(8,128)(2,1)S(1)}, bf16[16,48,256]{2,1,0:T(8,128)(2,1)S(1)}, u32[]{:S(2)}, u32[]{:S(2)}) %collective-permute-start.7) | collective-permute-done | bytes 393248 | tf_op jit(solution)/shard_map/ppermute | solution.py:291
  57.9 2.6 %collective-permute-start.9 = (bf16[16,48,256]{2,1,0:T(8,128)(2,1)S(1)}, bf16[16,48,256]{2,1,0:T(8,128)(2,1)S(1)}, u32[]{:S(2)}, u32[]{:S(2)}) collective-permute-start(bf16[16,48,256]{2,1,0:T(8,128)(2,1)S(1)} %collective-permute-done.7.high_ref.after_ref), channel_id=1, source_target_pairs={{0,1},{1,0},{2,3},{3,2},{4,5},{5,4},{6,7},{7,6},{8,9},{9,8},{10,11... | collective-permute-start | bytes 1179656 | tf_op jit(solution)/shard_map/ppermute | solution.py:308
  60.5 5.1 %replicas_both.1 = (bf16[4,8,256,512]{3,2,1,0:T(8,128)(2,1)S(1)}, s32[8,128]{1,0:T(8,128)}) custom-call(s32[5]{0:T(128)S(1)} %stack.23.place, s16[4,256,256]{2,1,0:T(8,128)(2,1)S(1)} %collective-permute-done.6.travel_ref, bf16[16,48,256]{2,1,0:T(8,128)(2,1)S(1)} %collective-permute-done.7.high_ref.after_ref), custom_call_target="tpu_custom_call" | custom-call | flops 40000000000 | bytes 1000000 | tf_op jit(solution)/shard_map/replicas_both/pallas_call | solution.py:113
  67.4 2.4 %beams_0.1 = bf16[264,768]{1,0:T(8,128)(2,1)S(1)} custom-call(bf16[4,8,256,512]{3,2,1,0:T(8,128)(2,1)S(1)} %get-tuple-element.36.r0, bf16[4,8,256,512]{3,2,1,0:T(8,128)(2,1)S(1)} %get-tuple-element.37.r1, bf16[4,8,256,512]{3,2,1,0:T(8,128)(2,1)S(1)} %get-tuple-element.39.r2, bf16[4,8,256,512]{3,2,1,0:T(8,128)(2,1)S(1)} %get-tuple-element.41.r3, ...), custom_call_target="tpu_custom_call" | custom-call | flops 3000000000 | bytes 1000000 | tf_op jit(solution)/shard_map/beams_0/pallas_call | solution.py:163
  69.8 3.0 %collective-permute-start.10 = (bf16[264,768]{1,0:T(8,128)(2,1)S(1)}, bf16[264,768]{1,0:T(8,128)(2,1)S(1)}, u32[]{:S(2)}, u32[]{:S(2)}) collective-permute-start(bf16[264,768]{1,0:T(8,128)(2,1)S(1)} %beams_0.1), channel_id=1, source_target_pairs={{0,8},{4,12},{8,0},{12,4},{1,9},{5,13},{9,1},{13,5},{2,10},{6,14},... | collective-permute-start | bytes 1216520 | tf_op jit(solution)/shard_map/ppermute | solution.py:319
  72.8 2.4 %beams_1.1 = bf16[264,768]{1,0:T(8,128)(2,1)S(1)} custom-call(bf16[4,8,256,512]{3,2,1,0:T(8,128)(2,1)S(1)} %get-tuple-element.36.r0, bf16[4,8,256,512]{3,2,1,0:T(8,128)(2,1)S(1)} %get-tuple-element.37.r1, bf16[4,8,256,512]{3,2,1,0:T(8,128)(2,1)S(1)} %get-tuple-element.39.r2, bf16[4,8,256,512]{3,2,1,0:T(8,128)(2,1)S(1)} %get-tuple-element.41.r3, ...), custom_call_target="tpu_custom_call" | custom-call | flops 3000000000 | bytes 1000000 | tf_op jit(solution)/shard_map/beams_1/pallas_call | solution.py:163
  75.2 2.4 %beams_2.1 = bf16[264,768]{1,0:T(8,128)(2,1)S(1)} custom-call(bf16[4,8,256,512]{3,2,1,0:T(8,128)(2,1)S(1)} %get-tuple-element.36.r0, bf16[4,8,256,512]{3,2,1,0:T(8,128)(2,1)S(1)} %get-tuple-element.37.r1, bf16[4,8,256,512]{3,2,1,0:T(8,128)(2,1)S(1)} %get-tuple-element.39.r2, bf16[4,8,256,512]{3,2,1,0:T(8,128)(2,1)S(1)} %get-tuple-element.41.r3, ...), custom_call_target="tpu_custom_call" | custom-call | flops 3000000000 | bytes 1000000 | tf_op jit(solution)/shard_map/beams_2/pallas_call | solution.py:163
  78.0 2.4 %collective-permute-start.12 = (bf16[264,768]{1,0:T(8,128)(2,1)S(1)}, bf16[264,768]{1,0:T(8,128)(2,1)S(1)}, u32[]{:S(2)}, u32[]{:S(2)}) collective-permute-start(bf16[264,768]{1,0:T(8,128)(2,1)S(1)} %beams_2.1), channel_id=1, source_target_pairs={{0,12},{4,0},{8,4},{12,8},{1,13},{5,1},{9,5},{13,9},{2,14},{6,2},{... | collective-permute-start | bytes 1216520 | tf_op jit(solution)/shard_map/ppermute | solution.py:319
  80.4 2.2 %collective-permute-done.10.refs_0_ = bf16[264,768]{1,0:T(8,128)(2,1)S(1)} collective-permute-done((bf16[264,768]{1,0:T(8,128)(2,1)S(1)}, bf16[264,768]{1,0:T(8,128)(2,1)S(1)}, u32[]{:S(2)}, u32[]{:S(2)}) %collective-permute-start.10) | collective-permute-done | bytes 405536 | tf_op jit(solution)/shard_map/ppermute | solution.py:319
  82.6 2.4 %beams_3.1.refs_3_ = f32[256,768]{1,0:T(8,128)S(1)} custom-call(bf16[4,8,256,512]{3,2,1,0:T(8,128)(2,1)S(1)} %get-tuple-element.36.r0, bf16[4,8,256,512]{3,2,1,0:T(8,128)(2,1)S(1)} %get-tuple-element.37.r1, bf16[4,8,256,512]{3,2,1,0:T(8,128)(2,1)S(1)} %get-tuple-element.39.r2, bf16[4,8,256,512]{3,2,1,0:T(8,128)(2,1)S(1)} %get-tuple-element.41.r3, ...), custom_call_target="tpu_custom_call" | custom-call | flops 3000000000 | bytes 1000000 | tf_op jit(solution)/shard_map/beams_3/pallas_call | solution.py:163
  85.0 6.6 %collective-permute-done.11.refs_1_ = bf16[264,768]{1,0:T(8,128)(2,1)S(1)} collective-permute-done((bf16[264,768]{1,0:T(8,128)(2,1)S(1)}, bf16[264,768]{1,0:T(8,128)(2,1)S(1)}, u32[]{:S(2)}, u32[]{:S(2)}) %collective-permute-start.11) | collective-permute-done | bytes 405536 | tf_op jit(solution)/shard_map/ppermute | solution.py:319
  91.6 1.9 %finish.1 = f32[48,256]{1,0:T(8,128)} custom-call(s32[5]{0:T(128)S(1)} %stack.23.place, bf16[264,768]{1,0:T(8,128)(2,1)S(1)} %collective-permute-done.10.refs_0_, bf16[264,768]{1,0:T(8,128)(2,1)S(1)} %collective-permute-done.11.refs_1_, bf16[264,768]{1,0:T(8,128)(2,1)S(1)} %collective-permute-done.12.refs_2_, f32[256,768]{1,0:T(8,128)S(1)} %beams_3.1.refs_3_, ...), custom_call_target="tpu_custom_call" | custom-call | tf_op jit(solution)/shard_map/finish/pallas_call | solution.py:251
  (25 shorter events, 5.8 us)
Async XLA Ops:
  4.1 16.5 %collective-permute-start = (bf16[1,48,256]{2,1,0:T(8,128)(2,1)S(1)}, bf16[1,48,256]{2,1,0:T(8,128)(2,1)S(1)}, u32[]{:S(2)}, u32[]{:S(2)}) collective-permute-start(bf16[1,48,256]{2,1,0:T(8,128)(2,1)S(1)} %reshape.15.after_ref.a_ref), channel_id=1, source_target_pairs={{0,128},{16,144},{32,160},{48,176},{64,192},{80,208},{96,224},{112... | collective-permute-start | bytes 73736 | tf_op jit(solution)/shard_map/ppermute | solution.py:291
  11.9 9.9 %collective-permute-start.2 = (s16[4,256,256]{2,1,0:T(8,128)(2,1)S(1)}, s16[4,256,256]{2,1,0:T(8,128)(2,1)S(1)}, u32[]{:S(2)}, u32[]{:S(2)}) collective-permute-start(s16[4,256,256]{2,1,0:T(8,128)(2,1)S(1)} %get-tuple-element.30), channel_id=1, source_target_pairs={{0,1},{1,0},{2,3},{3,2},{4,5},{5,4},{6,7},{7,6},{8,9},{9,8},{10,11... | collective-permute-start | bytes 1572872 | tf_op jit(solution)/shard_map/ppermute | solution.py:285
  12.8 36.0 %collective-permute-start.5 = (s16[4,256,256]{2,1,0:T(8,128)(2,1)S(1)}, s16[4,256,256]{2,1,0:T(8,128)(2,1)S(1)}, u32[]{:S(2)}, u32[]{:S(2)}) collective-permute-start(s16[4,256,256]{2,1,0:T(8,128)(2,1)S(1)} %get-tuple-element.32), channel_id=1, source_target_pairs={{0,2},{1,3},{2,0},{3,1},{4,6},{5,7},{6,4},{7,5},{8,10},{9,11},{10,... | collective-permute-start | bytes 1572872 | tf_op jit(solution)/shard_map/ppermute | solution.py:285
  15.8 33.1 %collective-permute-start.6 = (s16[4,256,256]{2,1,0:T(8,128)(2,1)S(1)}, s16[4,256,256]{2,1,0:T(8,128)(2,1)S(1)}, u32[]{:S(2)}, u32[]{:S(2)}) collective-permute-start(s16[4,256,256]{2,1,0:T(8,128)(2,1)S(1)} %get-tuple-element.33), channel_id=1, source_target_pairs={{0,3},{1,2},{2,1},{3,0},{4,7},{5,6},{6,5},{7,4},{8,11},{9,10},{10,... | collective-permute-start | bytes 1572872 | tf_op jit(solution)/shard_map/ppermute | solution.py:285
  20.5 5.8 %collective-permute-start.1 = (bf16[2,48,256]{2,1,0:T(8,128)(2,1)S(1)}, bf16[2,48,256]{2,1,0:T(8,128)(2,1)S(1)}, u32[]{:S(2)}, u32[]{:S(2)}) collective-permute-start(bf16[2,48,256]{2,1,0:T(8,128)(2,1)S(1)} %join_1.1.after_ref.a_ref), channel_id=1, source_target_pairs={{0,64},{16,80},{32,96},{48,112},{64,0},{80,16},{96,32},{112,48},{1... | collective-permute-start | bytes 147464 | tf_op jit(solution)/shard_map/ppermute | solution.py:291
  26.4 15.2 %collective-permute-start.3 = (bf16[4,48,256]{2,1,0:T(8,128)(2,1)S(1)}, bf16[4,48,256]{2,1,0:T(8,128)(2,1)S(1)}, u32[]{:S(2)}, u32[]{:S(2)}) collective-permute-start(bf16[4,48,256]{2,1,0:T(8,128)(2,1)S(1)} %join_2.1.a_ref), channel_id=1, source_target_pairs={{0,16},{16,0},{32,48},{48,32},{64,80},{80,64},{96,112},{112,96},{1... | collective-permute-start | bytes 294920 | tf_op jit(solution)/shard_map/ppermute | solution.py:291
  41.6 7.2 %collective-permute-start.4 = (bf16[8,48,256]{2,1,0:T(8,128)(2,1)S(1)}, bf16[8,48,256]{2,1,0:T(8,128)(2,1)S(1)}, u32[]{:S(2)}, u32[]{:S(2)}) collective-permute-start(bf16[8,48,256]{2,1,0:T(8,128)(2,1)S(1)} %join_4.1.a_ref), channel_id=1, source_target_pairs={{0,2},{2,0},{1,3},{3,1},{4,6},{6,4},{5,7},{7,5},{8,10},{10,8},{9,1... | collective-permute-start | bytes 589832 | tf_op jit(solution)/shard_map/ppermute | solution.py:289
  48.9 9.0 %collective-permute-start.7 = (bf16[16,48,256]{2,1,0:T(8,128)(2,1)S(1)}, bf16[16,48,256]{2,1,0:T(8,128)(2,1)S(1)}, u32[]{:S(2)}, u32[]{:S(2)}) collective-permute-start(bf16[16,48,256]{2,1,0:T(8,128)(2,1)S(1)} %join_8.1.low_ref.after_ref), channel_id=1, source_target_pairs={{0,32},{16,48},{32,0},{48,16},{64,96},{80,112},{96,64},{112,80},{1... | collective-permute-start | bytes 1179656 | tf_op jit(solution)/shard_map/ppermute | solution.py:291
  49.7 16.8 %collective-permute-start.8 = (bf16[16,48,256]{2,1,0:T(8,128)(2,1)S(1)}, bf16[16,48,256]{2,1,0:T(8,128)(2,1)S(1)}, u32[]{:S(2)}, u32[]{:S(2)}) collective-permute-start(bf16[16,48,256]{2,1,0:T(8,128)(2,1)S(1)} %join_8.1.low_ref.after_ref), channel_id=1, source_target_pairs={{0,1},{1,0},{2,3},{3,2},{4,5},{5,4},{6,7},{7,6},{8,9},{9,8},{10,11... | collective-permute-start | bytes 1179656 | tf_op jit(solution)/shard_map/ppermute | solution.py:306
  57.9 8.6 %collective-permute-start.9 = (bf16[16,48,256]{2,1,0:T(8,128)(2,1)S(1)}, bf16[16,48,256]{2,1,0:T(8,128)(2,1)S(1)}, u32[]{:S(2)}, u32[]{:S(2)}) collective-permute-start(bf16[16,48,256]{2,1,0:T(8,128)(2,1)S(1)} %collective-permute-done.7.high_ref.after_ref), channel_id=1, source_target_pairs={{0,1},{1,0},{2,3},{3,2},{4,5},{5,4},{6,7},{7,6},{8,9},{9,8},{10,11... | collective-permute-start | bytes 1179656 | tf_op jit(solution)/shard_map/ppermute | solution.py:308
  69.8 12.8 %collective-permute-start.10 = (bf16[264,768]{1,0:T(8,128)(2,1)S(1)}, bf16[264,768]{1,0:T(8,128)(2,1)S(1)}, u32[]{:S(2)}, u32[]{:S(2)}) collective-permute-start(bf16[264,768]{1,0:T(8,128)(2,1)S(1)} %beams_0.1), channel_id=1, source_target_pairs={{0,8},{4,12},{8,0},{12,4},{1,9},{5,13},{9,1},{13,5},{2,10},{6,14},... | collective-permute-start | bytes 1216520 | tf_op jit(solution)/shard_map/ppermute | solution.py:319
  77.6 14.0 %copy-start = (s32[2,768]{1,0:T(2,128)S(1)}, s32[2,768]{1,0:T(2,128)}, u32[]{:S(2)}) copy-start(s32[2,768]{1,0:T(2,128)} %constant.54.clone.refs_6_) | copy-start | bytes 18436
  77.7 14.0 %collective-permute-start.11 = (bf16[264,768]{1,0:T(8,128)(2,1)S(1)}, bf16[264,768]{1,0:T(8,128)(2,1)S(1)}, u32[]{:S(2)}, u32[]{:S(2)}) collective-permute-start(bf16[264,768]{1,0:T(8,128)(2,1)S(1)} %beams_1.1), channel_id=1, source_target_pairs={{0,4},{4,8},{8,12},{12,0},{1,5},{5,9},{9,13},{13,1},{2,6},{6,10},{... | collective-permute-start | bytes 1216520 | tf_op jit(solution)/shard_map/ppermute | solution.py:319
  78.0 13.6 %collective-permute-start.12 = (bf16[264,768]{1,0:T(8,128)(2,1)S(1)}, bf16[264,768]{1,0:T(8,128)(2,1)S(1)}, u32[]{:S(2)}, u32[]{:S(2)}) collective-permute-start(bf16[264,768]{1,0:T(8,128)(2,1)S(1)} %beams_2.1), channel_id=1, source_target_pairs={{0,12},{4,0},{8,4},{12,8},{1,13},{5,1},{9,5},{13,9},{2,14},{6,2},{... | collective-permute-start | bytes 1216520 | tf_op jit(solution)/shard_map/ppermute | solution.py:319

commit v5 on v4

--- a/solution.py
+++ b/solution.py
@@ -19,7 +19,7 @@
 CH = 256
 COLS = 96
 TILE = 32
-NORM_ROWS = 8
+NORM_ROWS = 16
 
 
 def series_coefficients():
@@ -146,15 +146,15 @@
     )(a, b, token)
 
 
-def beams_kernel(r0, r1, r2, r3, wa_ref, wb_ref, na_ref, nb_ref, out_ref, *, slot):
-    columns = [
-        (product(r0[slot, f], wa_ref[0, f]) + product(r1[slot, f], wb_ref[0, f]))
-        + (product(r2[slot, f], wa_ref[1, f]) + product(r3[slot, f], wb_ref[1, f]))
-        for f in range(NF)
-    ]
+def beams_kernel(*refs, slot):
+    reps, weights, norms, out_ref = refs[0:4], refs[4:8], refs[8:12], refs[12]
+    columns = []
+    for f in range(NF):
+        parts = [product(rep[slot, f], w_ref[f]) for rep, w_ref in zip(reps, weights)]
+        columns.append((parts[0] + parts[1]) + (parts[2] + parts[3]))
     out_ref[0:ROWS] = jnp.concatenate(columns, axis=1).astype(out_ref.dtype)
     if out_ref.shape[0] > ROWS:
-        out_ref[ROWS : ROWS + NORM_ROWS] = na_ref[...] + nb_ref[...]
+        out_ref[ROWS : ROWS + NORM_ROWS] = (norms[0][...] + norms[1][...]) + (norms[2][...] + norms[3][...])
 
 
 def beams_block(reps, weights, norms, step):
@@ -162,7 +162,7 @@
     rows = ROWS if own else ROWS + NORM_ROWS
     return pl.pallas_call(
         functools.partial(beams_kernel, slot=step),
-        in_specs=[VMEM] * 8,
+        in_specs=[VMEM] * 12,
         out_specs=VMEM,
         out_shape=jax.ShapeDtypeStruct((rows, NF * COLS), f32 if own else bf16),
         cost_estimate=pl.CostEstimate(flops=3_000_000_000, bytes_accessed=1_000_000, transcendentals=0),
@@ -171,35 +171,33 @@
     )(*reps, *weights, *norms)
 
 
-def prepare_kernel(low_ref, high_ref, w_ref, norm_ref, wide, *, first_row):
+def prepare_kernel(source_ref, w_ref, norm_ref, wide, *, first_row):
+    for g in range(16):
+        for half in range(CH // 128):
+            lanes = slice(half * 128, (half + 1) * 128)
+            wide[half, g * 48 : (g + 1) * 48, :] = source_ref[g, :, lanes].astype(f32)
     squares = jnp.zeros((COLS, CH), f32)
-    for flip in range(2):
-        for g in range(16):
-            source = (low_ref, high_ref)[g // 8]
-            for half in range(CH // 128):
-                lanes = slice(half * 128, (half + 1) * 128)
-                wide[half, g * 48 : (g + 1) * 48, :] = source[flip * 8 + g % 8, :, lanes].astype(f32)
-        for f in range(NF):
-            real, imag = [
-                jnp.concatenate(
-                    [
-                        jnp.concatenate(
-                            [
-                                wide[half, pl.ds(p * 24 + f * 3 + i, 16, stride=48), :]
-                                for half in range(CH // 128)
-                            ],
-                            axis=1,
-                        )
-                        for i in range(3)
-                    ],
-                    axis=0,
-                )
-                for p in range(2)
-            ]
-            both = jnp.concatenate([real, imag], axis=0)
-            squares = squares + both * both
-            w_ref[flip, f, :, 0:CH] = both.astype(bf16)
-            w_ref[flip, f, :, CH : 2 * CH] = jnp.concatenate([-imag, real], axis=0).astype(bf16)
+    for f in range(NF):
+        real, imag = [
+            jnp.concatenate(
+                [
+                    jnp.concatenate(
+                        [
+                            wide[half, pl.ds(p * 24 + f * 3 + i, 16, stride=48), :]
+                            for half in range(CH // 128)
+                        ],
+                        axis=1,
+                    )
+                    for i in range(3)
+                ],
+                axis=0,
+            )
+            for p in range(2)
+        ]
+        both = jnp.concatenate([real, imag], axis=0)
+        squares = squares + both * both
+        w_ref[f, :, 0:CH] = both.astype(bf16)
+        w_ref[f, :, CH : 2 * CH] = jnp.concatenate([-imag, real], axis=0).astype(bf16)
     sums = exact_product(jnp.ones((NORM_ROWS, CH), bf16), squares)
     row = lax.broadcasted_iota(jnp.int32, sums.shape, 0) - first_row
     zero = jnp.zeros_like(sums)
@@ -209,36 +207,36 @@
     norm_ref[...] = jnp.concatenate([split] + [zero] * (NF - 1), axis=1).astype(bf16)
 
 
-def prepare(low, high, first_row):
+def prepare(source, first_row):
     return pl.pallas_call(
         functools.partial(prepare_kernel, first_row=first_row),
-        in_specs=[VMEM] * 2,
+        in_specs=[VMEM],
         out_specs=[VMEM, VMEM],
         scratch_shapes=[pltpu.VMEM((CH // 128, 768, 128), f32)],
         out_shape=[
-            jax.ShapeDtypeStruct((2, NF, COLS, 2 * CH), bf16),
+            jax.ShapeDtypeStruct((NF, COLS, 2 * CH), bf16),
             jax.ShapeDtypeStruct((NORM_ROWS, NF * COLS), bf16),
         ],
         cost_estimate=pl.CostEstimate(flops=1_000_000_000, bytes_accessed=1_000_000, transcendentals=0),
         compiler_params=pltpu.CompilerParams(vmem_limit_bytes=6 << 20),
         name=f"prepare_{first_row}",
-    )(low, high)
+    )(source)
 
 
 def column_tables():
     slot = np.arange(NF * COLS) % 48
     place = slot % 16
-    relative = sum(((place >> bit) & 1) * mask for bit, mask in enumerate((8, 4, 1, 2)))
+    relative = sum(((place >> bit) & 1) * mask for bit, mask in enumerate((8, 4, 2, 1)))
     return np.stack([relative, slot // 16]).astype(np.int32)
 
 
 def finish_kernel(place, *refs, count):
-    *received, own_ref, na_ref, nb_ref, table_ref, out_ref = refs
+    received, own_ref, norms, table_ref, out_ref = refs[0:3], refs[3], refs[4:8], refs[8], refs[9]
     window = lax.broadcasted_iota(jnp.int32, (48, NF * COLS), 0)
     source = table_ref[0:1, :] ^ place[4]
     pick = jnp.where(window == 3 * source + table_ref[1:2, :], 1.0, 0.0).astype(bf16)
     beams = own_ref[...]
-    norm_rows = na_ref[...].astype(f32) + nb_ref[...].astype(f32)
+    norm_rows = sum(ref[...].astype(f32) for ref in norms)
     for ref in received:
         beams = beams + ref[0:ROWS].astype(f32)
         norm_rows = norm_rows + ref[ROWS : ROWS + NORM_ROWS].astype(f32)
@@ -250,7 +248,7 @@
 def finish(place, received, own, norms, count):
     return pl.pallas_call(
         functools.partial(finish_kernel, count=count),
-        in_specs=[pl.BlockSpec(memory_space=pltpu.SMEM)] + [VMEM] * 7,
+        in_specs=[pl.BlockSpec(memory_space=pltpu.SMEM)] + [VMEM] * 9,
         out_specs=VMEM,
         out_shape=jax.ShapeDtypeStruct((48, ROWS), f32),
         compiler_params=pltpu.CompilerParams(vmem_limit_bytes=8 << 20),
@@ -279,15 +277,15 @@
 
     block = (spectra * quality.astype(bf16)).reshape(1, 48, CH)
     parts = [travel_for(flip // 2, flip % 2) for flip in range(4)]
-    block, place, *parts = tie(block, place, *parts)
+    place, *parts = tie(place, *parts)
 
     def moved(flip):
         return lax.ppermute(parts[flip], ("yh", "c"), [(i, i ^ flip) for i in range(4)])
 
     def exchange(values, stage):
-        if stage == 3:
+        if stage == 4:
             return lax.ppermute(values, "yh", SWAP)
-        mask = (8, 4, 1, None, 2)[stage]
+        mask = (8, 4, 2, 1)[stage]
         return lax.ppermute(values, ("z", "yl"), [(i, i ^ mask) for i in range(16)])
 
     far, near, both = moved(2), moved(1), moved(3)
@@ -307,17 +305,18 @@
     rep_far, token = replicas(place, far, held, "far")
     other_swapped = lax.ppermute(other, "c", SWAP)
     rep_both, _ = replicas(place, both, other, "both")
-    w_a, n_a = prepare(held, other, 0)
-    w_b, n_b = prepare(held_swapped, other_swapped, 3)
+    sources = (held, held_swapped, other, other_swapped)
+    prepared = [prepare(source, 4 * index) for index, source in enumerate(sources)]
+    weights, norms = [w for w, _ in prepared], [n for _, n in prepared]
     reps = (rep_own, rep_near, rep_far, rep_both)
     received = []
     for step, dx in enumerate(STEPS):
         if step == 3:
-            n_a, received[0] = tie(n_a, received[0])
-        beams = beams_block(reps, (w_a, w_b), (n_a, n_b), step)
+            norms[0], received[0] = tie(norms[0], received[0])
+        beams = beams_block(reps, weights, norms, step)
         if dx:
             received.append(lax.ppermute(beams, "x", [(i, (i + dx) % 4) for i in range(4)]))
-    return finish(place, received, beams, (n_a, n_b), float(NF * CH * 16))
+    return finish(place, received, beams, norms, float(NF * CH * 16))
 
 
 def solution(mesh):

time: 93.6 us -> 90.1 us (0.963)
  waiting for transfers between devices: 29.4 us -> 27.3 us
  starting transfers between devices: 27.4 us -> 25.9 us
    ppermute x1, waiting for transfers between devices: 5.59 us -> 3 us  [exchange(): return lax.ppermute(values, 'yh', SWAP)]
  transfers between devices with their start and end apart: 13 -> 13, of which waited for: 5 -> 5; matrix products, arithmetic and copies ran while one was open for 0% -> 3% of each run, Pallas kernels for 29% -> 31%
where the time goes in v5:
time: 90.1 us; the launch traced here: 89.9 us
  Pallas kernels  32.5 us (36%)
  waiting for transfers between devices  27.3 us (30%)
  starting transfers between devices  25.9 us (29%)
  other arithmetic  3.85 us (4%)
    pallas_call x4, Pallas kernels, replicas(): pl.pallas_call(replicas_kernel, grid_spec=pltpu.PrefetchScalarGridSpec(nu...  19.3 us
    ppermute x4, waiting for transfers between devices, exchange(): return lax.ppermute(values, ('z', 'yl'), [(i, i ^ mask) for i in range(16)])  14.9 us
    ppermute x4, starting transfers between devices, exchange(): return lax.ppermute(values, ('z', 'yl'), [(i, i ^ mask) for i in range(16)])  11.3 us
    pallas_call x4, Pallas kernels, beams_block(): pl.pallas_call(functools.partial(beams_kernel, slot=step), in_specs=[VMEM...  9.56 us
    ppermute x3, waiting for transfers between devices, per_device(): lax.ppermute(beams, 'x', [(i, (i + dx) % 4) for i in range(4)])  9.37 us
    ppermute x3, starting transfers between devices, per_device(): lax.ppermute(beams, 'x', [(i, (i + dx) % 4) for i in range(4)])  5.76 us
    ppermute x3, starting transfers between devices, moved(): lax.ppermute(parts[flip], ('yh', 'c'), [(i, i ^ flip) for i in range(4)])  4.28 us
    ppermute x1, waiting for transfers between devices, exchange(): return lax.ppermute(values, 'yh', SWAP)  3 us
  transfers between devices with their start and end apart: 13, of which 5 were waited for; matrix products, arithmetic and copies ran while one was open for 3% of the time, Pallas kernels for 31%

profile of v5, /device:TPU:1, one launch (start us, length us, event | category | flops | bytes accessed | tf_op | source)
XLA Modules:
  0.0 89.9 jit_solution(160712730855637471)
XLA Ops:
  1.5 7.8 %collective-permute-start = (bf16[1,48,256]{2,1,0:T(8,128)(2,1)S(1)}, bf16[1,48,256]{2,1,0:T(8,128)(2,1)S(1)}, u32[]{:S(2)}, u32[]{:S(2)}) collective-permute-start(bf16[1,48,256]{2,1,0:T(8,128)(2,1)S(1)} %reshape.16.after_ref.a_ref), channel_id=1, source_target_pairs={{0,128},{16,144},{32,160},{48,176},{64,192},{80,208},{96,224},{112... | collective-permute-start | bytes 73736 | tf_op jit(solution)/shard_map/ppermute | solution.py:289
  9.4 2.4 %fusion.3 = (s16[4,256,256]{2,1,0:T(8,128)(2,1)S(1)}, s16[4,256,256]{2,1,0:T(8,128)(2,1)S(1)}, s16[4,256,256]{2,1,0:T(8,128)(2,1)S(1)}, s16[4,256,256]{2,1,0:T(8,128)(2,1)S(1)}) fusion(s32[4,2,2,256,256]{4,3,2,1,0:T(8,128)} %bitcast.30, s32[]{:T(128)S(6)} %select_n.42, s32[]{:T(128)S(6)} %select_n.41, s32[]{:T(128)S(6)} %select_n.40, s32[]{:T(128)S(6)} %select_n.39), kind=kLoop, calls=%fused_computation.7 | loop fusion | flops 1048576 | bytes 6291472 | tf_op jit(solution)/shard_map/convert_element_type | solution.py:276
  12.9 2.9 %collective-permute-start.5 = (s16[4,256,256]{2,1,0:T(8,128)(2,1)S(1)}, s16[4,256,256]{2,1,0:T(8,128)(2,1)S(1)}, u32[]{:S(2)}, u32[]{:S(2)}) collective-permute-start(s16[4,256,256]{2,1,0:T(8,128)(2,1)S(1)} %get-tuple-element.34), channel_id=1, source_target_pairs={{0,2},{1,3},{2,0},{3,1},{4,6},{5,7},{6,4},{7,5},{8,10},{9,11},{10,... | collective-permute-start | bytes 1572872 | tf_op jit(solution)/shard_map/ppermute | solution.py:283
  16.1 4.5 %replicas_own.1 = (bf16[4,8,256,512]{3,2,1,0:T(8,128)(2,1)S(1)}, s32[8,128]{1,0:T(8,128)S(1)}) custom-call(s32[5]{0:T(128)S(1)} %stack.23.place, s16[4,256,256]{2,1,0:T(8,128)(2,1)S(1)} %get-tuple-element.30.travel_ref, bf16[1,48,256]{2,1,0:T(8,128)(2,1)S(1)} %reshape.16.after_ref.a_ref), custom_call_target="tpu_custom_call" | custom-call | flops 40000000000 | bytes 1000000 | tf_op jit(solution)/shard_map/replicas_own/pallas_call | solution.py:113
  20.7 1.3 %collective-permute-start.1 = (bf16[2,48,256]{2,1,0:T(8,128)(2,1)S(1)}, bf16[2,48,256]{2,1,0:T(8,128)(2,1)S(1)}, u32[]{:S(2)}, u32[]{:S(2)}) collective-permute-start(bf16[2,48,256]{2,1,0:T(8,128)(2,1)S(1)} %join_1.1.after_ref.a_ref), channel_id=1, source_target_pairs={{0,64},{16,80},{32,96},{48,112},{64,0},{80,16},{96,32},{112,48},{1... | collective-permute-start | bytes 147464 | tf_op jit(solution)/shard_map/ppermute | solution.py:289
  21.9 4.5 %replicas_near.1 = (bf16[4,8,256,512]{3,2,1,0:T(8,128)(2,1)S(1)}, s32[8,128]{1,0:T(8,128)S(1)}) custom-call(s32[5]{0:T(128)S(1)} %stack.23.place, s16[4,256,256]{2,1,0:T(8,128)(2,1)S(1)} %collective-permute-done.2.travel_ref, bf16[2,48,256]{2,1,0:T(8,128)(2,1)S(1)} %join_1.1.after_ref.a_ref), custom_call_target="tpu_custom_call" | custom-call | flops 40000000000 | bytes 1000000 | tf_op jit(solution)/shard_map/replicas_near/pallas_call | solution.py:113
  27.3 3.2 %collective-permute-done.3.b_ref = bf16[4,48,256]{2,1,0:T(8,128)(2,1)S(1)} collective-permute-done((bf16[4,48,256]{2,1,0:T(8,128)(2,1)S(1)}, bf16[4,48,256]{2,1,0:T(8,128)(2,1)S(1)}, u32[]{:S(2)}, u32[]{:S(2)}) %collective-permute-start.3) | collective-permute-done | bytes 98336 | tf_op jit(solution)/shard_map/ppermute | solution.py:289
  30.5 1.4 %collective-permute-start.4 = (bf16[8,48,256]{2,1,0:T(8,128)(2,1)S(1)}, bf16[8,48,256]{2,1,0:T(8,128)(2,1)S(1)}, u32[]{:S(2)}, u32[]{:S(2)}) collective-permute-start(bf16[8,48,256]{2,1,0:T(8,128)(2,1)S(1)} %join_4.1.a_ref), channel_id=1, source_target_pairs={{0,16},{16,0},{32,48},{48,32},{64,80},{80,64},{96,112},{112,96},{1... | collective-permute-start | bytes 589832 | tf_op jit(solution)/shard_map/ppermute | solution.py:289
  31.9 11.7 %collective-permute-done.4.b_ref = bf16[8,48,256]{2,1,0:T(8,128)(2,1)S(1)} collective-permute-done((bf16[8,48,256]{2,1,0:T(8,128)(2,1)S(1)}, bf16[8,48,256]{2,1,0:T(8,128)(2,1)S(1)}, u32[]{:S(2)}, u32[]{:S(2)}) %collective-permute-start.4) | collective-permute-done | bytes 196640 | tf_op jit(solution)/shard_map/ppermute | solution.py:289
  43.7 1.6 %collective-permute-start.7 = (bf16[16,48,256]{2,1,0:T(8,128)(2,1)S(1)}, bf16[16,48,256]{2,1,0:T(8,128)(2,1)S(1)}, u32[]{:S(2)}, u32[]{:S(2)}) collective-permute-start(bf16[16,48,256]{2,1,0:T(8,128)(2,1)S(1)} %join_8.1.source_ref.after_ref), channel_id=1, source_target_pairs={{0,2},{2,0},{1,3},{3,1},{4,6},{6,4},{5,7},{7,5},{8,10},{10,8},{9,1... | collective-permute-start | bytes 1179656 | tf_op jit(solution)/shard_map/ppermute | solution.py:287
  45.3 1.2 %collective-permute-start.8 = (bf16[16,48,256]{2,1,0:T(8,128)(2,1)S(1)}, bf16[16,48,256]{2,1,0:T(8,128)(2,1)S(1)}, u32[]{:S(2)}, u32[]{:S(2)}) collective-permute-start(bf16[16,48,256]{2,1,0:T(8,128)(2,1)S(1)} %join_8.1.source_ref.after_ref), channel_id=1, source_target_pairs={{0,1},{1,0},{2,3},{3,2},{4,5},{5,4},{6,7},{7,6},{8,9},{9,8},{10,11... | collective-permute-start | bytes 1179656 | tf_op jit(solution)/shard_map/ppermute | solution.py:304
  46.5 5.1 %replicas_far.1 = (bf16[4,8,256,512]{3,2,1,0:T(8,128)(2,1)S(1)}, s32[8,128]{1,0:T(8,128)}) custom-call(s32[5]{0:T(128)S(1)} %stack.23.place, s16[4,256,256]{2,1,0:T(8,128)(2,1)S(1)} %collective-permute-done.5.travel_ref, bf16[16,48,256]{2,1,0:T(8,128)(2,1)S(1)} %join_8.1.source_ref.after_ref), custom_call_target="tpu_custom_call" | custom-call | flops 40000000000 | bytes 1000000 | tf_op jit(solution)/shard_map/replicas_far/pallas_call | solution.py:113
  52.1 3.0 %collective-permute-done.7.after_ref.source_ref = bf16[16,48,256]{2,1,0:T(8,128)(2,1)S(1)} collective-permute-done((bf16[16,48,256]{2,1,0:T(8,128)(2,1)S(1)}, bf16[16,48,256]{2,1,0:T(8,128)(2,1)S(1)}, u32[]{:S(2)}, u32[]{:S(2)}) %collective-permute-start.7) | collective-permute-done | bytes 393248 | tf_op jit(solution)/shard_map/ppermute | solution.py:287
  55.1 1.8 %collective-permute-start.9 = (bf16[16,48,256]{2,1,0:T(8,128)(2,1)S(1)}, bf16[16,48,256]{2,1,0:T(8,128)(2,1)S(1)}, u32[]{:S(2)}, u32[]{:S(2)}) collective-permute-start(bf16[16,48,256]{2,1,0:T(8,128)(2,1)S(1)} %collective-permute-done.7.after_ref.source_ref), channel_id=1, source_target_pairs={{0,1},{1,0},{2,3},{3,2},{4,5},{5,4},{6,7},{7,6},{8,9},{9,8},{10,11... | collective-permute-start | bytes 1179656 | tf_op jit(solution)/shard_map/ppermute | solution.py:306
  56.8 5.1 %replicas_both.1 = (bf16[4,8,256,512]{3,2,1,0:T(8,128)(2,1)S(1)}, s32[8,128]{1,0:T(8,128)}) custom-call(s32[5]{0:T(128)S(1)} %stack.23.place, s16[4,256,256]{2,1,0:T(8,128)(2,1)S(1)} %collective-permute-done.6.travel_ref, bf16[16,48,256]{2,1,0:T(8,128)(2,1)S(1)} %collective-permute-done.7.after_ref.source_ref), custom_call_target="tpu_custom_call" | custom-call | flops 40000000000 | bytes 1000000 | tf_op jit(solution)/shard_map/replicas_both/pallas_call | solution.py:113
  63.3 2.4 %beams_0.1 = bf16[272,768]{1,0:T(8,128)(2,1)S(1)} custom-call(bf16[4,8,256,512]{3,2,1,0:T(8,128)(2,1)S(1)} %get-tuple-element.38.refs_0_, bf16[4,8,256,512]{3,2,1,0:T(8,128)(2,1)S(1)} %get-tuple-element.39.refs_1_, bf16[4,8,256,512]{3,2,1,0:T(8,128)(2,1)S(1)} %get-tuple-element.41.refs_2_, bf16[4,8,256,512]{3,2,1,0:T(8,128)(2,1)S(1)} %get-tuple-element.43.refs_3_, ...), custom_call_target="tpu_custom_call" | custom-call | flops 3000000000 | bytes 1000000 | tf_op jit(solution)/shard_map/beams_0/pallas_call | solution.py:163
  65.7 3.0 %collective-permute-start.10 = (bf16[272,768]{1,0:T(8,128)(2,1)S(1)}, bf16[272,768]{1,0:T(8,128)(2,1)S(1)}, u32[]{:S(2)}, u32[]{:S(2)}) collective-permute-start(bf16[272,768]{1,0:T(8,128)(2,1)S(1)} %beams_0.1), channel_id=1, source_target_pairs={{0,8},{4,12},{8,0},{12,4},{1,9},{5,13},{9,1},{13,5},{2,10},{6,14},... | collective-permute-start | bytes 1253384 | tf_op jit(solution)/shard_map/ppermute | solution.py:318
  68.7 2.4 %beams_1.1 = bf16[272,768]{1,0:T(8,128)(2,1)S(1)} custom-call(bf16[4,8,256,512]{3,2,1,0:T(8,128)(2,1)S(1)} %get-tuple-element.38.refs_0_, bf16[4,8,256,512]{3,2,1,0:T(8,128)(2,1)S(1)} %get-tuple-element.39.refs_1_, bf16[4,8,256,512]{3,2,1,0:T(8,128)(2,1)S(1)} %get-tuple-element.41.refs_2_, bf16[4,8,256,512]{3,2,1,0:T(8,128)(2,1)S(1)} %get-tuple-element.43.refs_3_, ...), custom_call_target="tpu_custom_call" | custom-call | flops 3000000000 | bytes 1000000 | tf_op jit(solution)/shard_map/beams_1/pallas_call | solution.py:163
  71.1 2.4 %beams_2.1 = bf16[272,768]{1,0:T(8,128)(2,1)S(1)} custom-call(bf16[4,8,256,512]{3,2,1,0:T(8,128)(2,1)S(1)} %get-tuple-element.38.refs_0_, bf16[4,8,256,512]{3,2,1,0:T(8,128)(2,1)S(1)} %get-tuple-element.39.refs_1_, bf16[4,8,256,512]{3,2,1,0:T(8,128)(2,1)S(1)} %get-tuple-element.41.refs_2_, bf16[4,8,256,512]{3,2,1,0:T(8,128)(2,1)S(1)} %get-tuple-element.43.refs_3_, ...), custom_call_target="tpu_custom_call" | custom-call | flops 3000000000 | bytes 1000000 | tf_op jit(solution)/shard_map/beams_2/pallas_call | solution.py:163
  73.9 2.4 %collective-permute-start.12 = (bf16[272,768]{1,0:T(8,128)(2,1)S(1)}, bf16[272,768]{1,0:T(8,128)(2,1)S(1)}, u32[]{:S(2)}, u32[]{:S(2)}) collective-permute-start(bf16[272,768]{1,0:T(8,128)(2,1)S(1)} %beams_2.1), channel_id=1, source_target_pairs={{0,12},{4,0},{8,4},{12,8},{1,13},{5,1},{9,5},{13,9},{2,14},{6,2},{... | collective-permute-start | bytes 1253384 | tf_op jit(solution)/shard_map/ppermute | solution.py:318
  76.3 2.5 %collective-permute-done.10.refs_0_ = bf16[272,768]{1,0:T(8,128)(2,1)S(1)} collective-permute-done((bf16[272,768]{1,0:T(8,128)(2,1)S(1)}, bf16[272,768]{1,0:T(8,128)(2,1)S(1)}, u32[]{:S(2)}, u32[]{:S(2)}) %collective-permute-start.10) | collective-permute-done | bytes 417824 | tf_op jit(solution)/shard_map/ppermute | solution.py:318
  78.8 2.4 %beams_3.1.refs_3_ = f32[256,768]{1,0:T(8,128)S(1)} custom-call(bf16[4,8,256,512]{3,2,1,0:T(8,128)(2,1)S(1)} %get-tuple-element.38.refs_0_, bf16[4,8,256,512]{3,2,1,0:T(8,128)(2,1)S(1)} %get-tuple-element.39.refs_1_, bf16[4,8,256,512]{3,2,1,0:T(8,128)(2,1)S(1)} %get-tuple-element.41.refs_2_, bf16[4,8,256,512]{3,2,1,0:T(8,128)(2,1)S(1)} %get-tuple-element.43.refs_3_, ...), custom_call_target="tpu_custom_call" | custom-call | flops 3000000000 | bytes 1000000 | tf_op jit(solution)/shard_map/beams_3/pallas_call | solution.py:163
  81.1 6.9 %collective-permute-done.11.refs_1_ = bf16[272,768]{1,0:T(8,128)(2,1)S(1)} collective-permute-done((bf16[272,768]{1,0:T(8,128)(2,1)S(1)}, bf16[272,768]{1,0:T(8,128)(2,1)S(1)}, u32[]{:S(2)}, u32[]{:S(2)}) %collective-permute-start.11) | collective-permute-done | bytes 417824 | tf_op jit(solution)/shard_map/ppermute | solution.py:318
  88.0 1.9 %finish.1 = f32[48,256]{1,0:T(8,128)} custom-call(s32[5]{0:T(128)S(1)} %stack.23.place, bf16[272,768]{1,0:T(8,128)(2,1)S(1)} %collective-permute-done.10.refs_0_, bf16[272,768]{1,0:T(8,128)(2,1)S(1)} %collective-permute-done.11.refs_1_, bf16[272,768]{1,0:T(8,128)(2,1)S(1)} %collective-permute-done.12.refs_2_, f32[256,768]{1,0:T(8,128)S(1)} %beams_3.1.refs_3_, ...), custom_call_target="tpu_custom_call" | custom-call | tf_op jit(solution)/shard_map/finish/pallas_call | solution.py:249
  (27 shorter events, 5.9 us)
Async XLA Ops:
  1.5 19.2 %collective-permute-start = (bf16[1,48,256]{2,1,0:T(8,128)(2,1)S(1)}, bf16[1,48,256]{2,1,0:T(8,128)(2,1)S(1)}, u32[]{:S(2)}, u32[]{:S(2)}) collective-permute-start(bf16[1,48,256]{2,1,0:T(8,128)(2,1)S(1)} %reshape.16.after_ref.a_ref), channel_id=1, source_target_pairs={{0,128},{16,144},{32,160},{48,176},{64,192},{80,208},{96,224},{112... | collective-permute-start | bytes 73736 | tf_op jit(solution)/shard_map/ppermute | solution.py:289
  11.8 10.1 %collective-permute-start.2 = (s16[4,256,256]{2,1,0:T(8,128)(2,1)S(1)}, s16[4,256,256]{2,1,0:T(8,128)(2,1)S(1)}, u32[]{:S(2)}, u32[]{:S(2)}) collective-permute-start(s16[4,256,256]{2,1,0:T(8,128)(2,1)S(1)} %get-tuple-element.32), channel_id=1, source_target_pairs={{0,1},{1,0},{2,3},{3,2},{4,5},{5,4},{6,7},{7,6},{8,9},{9,8},{10,11... | collective-permute-start | bytes 1572872 | tf_op jit(solution)/shard_map/ppermute | solution.py:283
  12.9 30.8 %collective-permute-start.5 = (s16[4,256,256]{2,1,0:T(8,128)(2,1)S(1)}, s16[4,256,256]{2,1,0:T(8,128)(2,1)S(1)}, u32[]{:S(2)}, u32[]{:S(2)}) collective-permute-start(s16[4,256,256]{2,1,0:T(8,128)(2,1)S(1)} %get-tuple-element.34), channel_id=1, source_target_pairs={{0,2},{1,3},{2,0},{3,1},{4,6},{5,7},{6,4},{7,5},{8,10},{9,11},{10,... | collective-permute-start | bytes 1572872 | tf_op jit(solution)/shard_map/ppermute | solution.py:283
  15.8 27.9 %collective-permute-start.6 = (s16[4,256,256]{2,1,0:T(8,128)(2,1)S(1)}, s16[4,256,256]{2,1,0:T(8,128)(2,1)S(1)}, u32[]{:S(2)}, u32[]{:S(2)}) collective-permute-start(s16[4,256,256]{2,1,0:T(8,128)(2,1)S(1)} %get-tuple-element.35), channel_id=1, source_target_pairs={{0,3},{1,2},{2,1},{3,0},{4,7},{5,6},{6,5},{7,4},{8,11},{9,10},{10,... | collective-permute-start | bytes 1572872 | tf_op jit(solution)/shard_map/ppermute | solution.py:283
  20.7 5.8 %collective-permute-start.1 = (bf16[2,48,256]{2,1,0:T(8,128)(2,1)S(1)}, bf16[2,48,256]{2,1,0:T(8,128)(2,1)S(1)}, u32[]{:S(2)}, u32[]{:S(2)}) collective-permute-start(bf16[2,48,256]{2,1,0:T(8,128)(2,1)S(1)} %join_1.1.after_ref.a_ref), channel_id=1, source_target_pairs={{0,64},{16,80},{32,96},{48,112},{64,0},{80,16},{96,32},{112,48},{1... | collective-permute-start | bytes 147464 | tf_op jit(solution)/shard_map/ppermute | solution.py:289
  26.5 4.0 %collective-permute-start.3 = (bf16[4,48,256]{2,1,0:T(8,128)(2,1)S(1)}, bf16[4,48,256]{2,1,0:T(8,128)(2,1)S(1)}, u32[]{:S(2)}, u32[]{:S(2)}) collective-permute-start(bf16[4,48,256]{2,1,0:T(8,128)(2,1)S(1)} %join_2.1.a_ref), channel_id=1, source_target_pairs={{0,32},{16,48},{32,0},{48,16},{64,96},{80,112},{96,64},{112,80},{1... | collective-permute-start | bytes 294920 | tf_op jit(solution)/shard_map/ppermute | solution.py:289
  30.5 13.1 %collective-permute-start.4 = (bf16[8,48,256]{2,1,0:T(8,128)(2,1)S(1)}, bf16[8,48,256]{2,1,0:T(8,128)(2,1)S(1)}, u32[]{:S(2)}, u32[]{:S(2)}) collective-permute-start(bf16[8,48,256]{2,1,0:T(8,128)(2,1)S(1)} %join_4.1.a_ref), channel_id=1, source_target_pairs={{0,16},{16,0},{32,48},{48,32},{64,80},{80,64},{96,112},{112,96},{1... | collective-permute-start | bytes 589832 | tf_op jit(solution)/shard_map/ppermute | solution.py:289
  43.7 11.3 %collective-permute-start.7 = (bf16[16,48,256]{2,1,0:T(8,128)(2,1)S(1)}, bf16[16,48,256]{2,1,0:T(8,128)(2,1)S(1)}, u32[]{:S(2)}, u32[]{:S(2)}) collective-permute-start(bf16[16,48,256]{2,1,0:T(8,128)(2,1)S(1)} %join_8.1.source_ref.after_ref), channel_id=1, source_target_pairs={{0,2},{2,0},{1,3},{3,1},{4,6},{6,4},{5,7},{7,5},{8,10},{10,8},{9,1... | collective-permute-start | bytes 1179656 | tf_op jit(solution)/shard_map/ppermute | solution.py:287
  45.3 17.0 %collective-permute-start.8 = (bf16[16,48,256]{2,1,0:T(8,128)(2,1)S(1)}, bf16[16,48,256]{2,1,0:T(8,128)(2,1)S(1)}, u32[]{:S(2)}, u32[]{:S(2)}) collective-permute-start(bf16[16,48,256]{2,1,0:T(8,128)(2,1)S(1)} %join_8.1.source_ref.after_ref), channel_id=1, source_target_pairs={{0,1},{1,0},{2,3},{3,2},{4,5},{5,4},{6,7},{7,6},{8,9},{9,8},{10,11... | collective-permute-start | bytes 1179656 | tf_op jit(solution)/shard_map/ppermute | solution.py:304
  55.1 7.8 %collective-permute-start.9 = (bf16[16,48,256]{2,1,0:T(8,128)(2,1)S(1)}, bf16[16,48,256]{2,1,0:T(8,128)(2,1)S(1)}, u32[]{:S(2)}, u32[]{:S(2)}) collective-permute-start(bf16[16,48,256]{2,1,0:T(8,128)(2,1)S(1)} %collective-permute-done.7.after_ref.source_ref), channel_id=1, source_target_pairs={{0,1},{1,0},{2,3},{3,2},{4,5},{5,4},{6,7},{7,6},{8,9},{9,8},{10,11... | collective-permute-start | bytes 1179656 | tf_op jit(solution)/shard_map/ppermute | solution.py:306
  65.7 13.0 %collective-permute-start.10 = (bf16[272,768]{1,0:T(8,128)(2,1)S(1)}, bf16[272,768]{1,0:T(8,128)(2,1)S(1)}, u32[]{:S(2)}, u32[]{:S(2)}) collective-permute-start(bf16[272,768]{1,0:T(8,128)(2,1)S(1)} %beams_0.1), channel_id=1, source_target_pairs={{0,8},{4,12},{8,0},{12,4},{1,9},{5,13},{9,1},{13,5},{2,10},{6,14},... | collective-permute-start | bytes 1253384 | tf_op jit(solution)/shard_map/ppermute | solution.py:318
  73.5 14.5 %copy-start = (s32[2,768]{1,0:T(2,128)S(1)}, s32[2,768]{1,0:T(2,128)}, u32[]{:S(2)}) copy-start(s32[2,768]{1,0:T(2,128)} %constant.54.clone.refs_8_) | copy-start | bytes 18436
  73.5 14.5 %collective-permute-start.11 = (bf16[272,768]{1,0:T(8,128)(2,1)S(1)}, bf16[272,768]{1,0:T(8,128)(2,1)S(1)}, u32[]{:S(2)}, u32[]{:S(2)}) collective-permute-start(bf16[272,768]{1,0:T(8,128)(2,1)S(1)} %beams_1.1), channel_id=1, source_target_pairs={{0,4},{4,8},{8,12},{12,0},{1,5},{5,9},{9,13},{13,1},{2,6},{6,10},{... | collective-permute-start | bytes 1253384 | tf_op jit(solution)/shard_map/ppermute | solution.py:318
  73.9 14.1 %collective-permute-start.12 = (bf16[272,768]{1,0:T(8,128)(2,1)S(1)}, bf16[272,768]{1,0:T(8,128)(2,1)S(1)}, u32[]{:S(2)}, u32[]{:S(2)}) collective-permute-start(bf16[272,768]{1,0:T(8,128)(2,1)S(1)} %beams_2.1), channel_id=1, source_target_pairs={{0,12},{4,0},{8,4},{12,8},{1,13},{5,1},{9,5},{13,9},{2,14},{6,2},{... | collective-permute-start | bytes 1253384 | tf_op jit(solution)/shard_map/ppermute | solution.py:318

commit v6 on v5

--- a/solution.py
+++ b/solution.py
@@ -171,11 +171,12 @@
     )(*reps, *weights, *norms)
 
 
-def prepare_kernel(source_ref, w_ref, norm_ref, wide, *, first_row):
+def prepare_kernel(low_ref, high_ref, w_ref, norm_ref, wide, *, flip, first_row):
     for g in range(16):
+        source_ref = (low_ref, high_ref)[g // 8]
         for half in range(CH // 128):
             lanes = slice(half * 128, (half + 1) * 128)
-            wide[half, g * 48 : (g + 1) * 48, :] = source_ref[g, :, lanes].astype(f32)
+            wide[half, g * 48 : (g + 1) * 48, :] = source_ref[2 * (g % 8) + flip, :, lanes].astype(f32)
     squares = jnp.zeros((COLS, CH), f32)
     for f in range(NF):
         real, imag = [
@@ -207,10 +208,10 @@
     norm_ref[...] = jnp.concatenate([split] + [zero] * (NF - 1), axis=1).astype(bf16)
 
 
-def prepare(source, first_row):
-    return pl.pallas_call(
-        functools.partial(prepare_kernel, first_row=first_row),
-        in_specs=[VMEM],
+def prepare(low, high, flip, first_row):
+    return pl.pallas_call(
+        functools.partial(prepare_kernel, flip=flip, first_row=first_row),
+        in_specs=[VMEM] * 2,
         out_specs=[VMEM, VMEM],
         scratch_shapes=[pltpu.VMEM((CH // 128, 768, 128), f32)],
         out_shape=[
@@ -220,13 +221,13 @@
         cost_estimate=pl.CostEstimate(flops=1_000_000_000, bytes_accessed=1_000_000, transcendentals=0),
         compiler_params=pltpu.CompilerParams(vmem_limit_bytes=6 << 20),
         name=f"prepare_{first_row}",
-    )(source)
+    )(low, high)
 
 
 def column_tables():
     slot = np.arange(NF * COLS) % 48
     place = slot % 16
-    relative = sum(((place >> bit) & 1) * mask for bit, mask in enumerate((8, 4, 2, 1)))
+    relative = sum(((place >> bit) & 1) * mask for bit, mask in enumerate((1, 8, 4, 2)))
     return np.stack([relative, slot // 16]).astype(np.int32)
 
 
@@ -283,30 +284,32 @@
         return lax.ppermute(parts[flip], ("yh", "c"), [(i, i ^ flip) for i in range(4)])
 
     def exchange(values, stage):
-        if stage == 4:
+        if stage == 0:
             return lax.ppermute(values, "yh", SWAP)
-        mask = (8, 4, 2, 1)[stage]
+        mask = (1, 8, 4, 2)[stage - 1]
         return lax.ppermute(values, ("z", "yl"), [(i, i ^ mask) for i in range(16)])
 
-    far, near, both = moved(2), moved(1), moved(3)
     held = block
     other = exchange(held, 0)
+    held = join(held, other, other)
+    held, *parts = tie(held, *parts)
+    far, near, both = moved(2), moved(1), moved(3)
+    other = exchange(held, 1)
     rep_own, token = replicas(place, parts[0], held, "own")
     held = join(held, other, token)
-    other = exchange(held, 1)
+    other = exchange(held, 2)
     rep_near, token = replicas(place, near, held, "near")
     held = join(held, other, token)
-    for stage in (2, 3):
-        other = exchange(held, stage)
-        held = join(held, other, token)
-    held, far, both = tie(held, far, both)
+    other = exchange(held, 3)
+    held = join(held, other, token)
+    held, far = tie(held, far)
     other = exchange(held, 4)
     held_swapped = lax.ppermute(held, "c", SWAP)
     rep_far, token = replicas(place, far, held, "far")
     other_swapped = lax.ppermute(other, "c", SWAP)
     rep_both, _ = replicas(place, both, other, "both")
-    sources = (held, held_swapped, other, other_swapped)
-    prepared = [prepare(source, 4 * index) for index, source in enumerate(sources)]
+    halves = ((held, other, 0), (held_swapped, other_swapped, 0), (held, other, 1), (held_swapped, other_swapped, 1))
+    prepared = [prepare(*half, 4 * index) for index, half in enumerate(halves)]
     weights, norms = [w for w, _ in prepared], [n for _, n in prepared]
     reps = (rep_own, rep_near, rep_far, rep_both)
     received = []

time: 90.1 us -> 85.7 us (0.951)
  waiting for transfers between devices: 27.3 us -> 21 us
  starting transfers between devices: 25.9 us -> 27.8 us
    ppermute x4, waiting for transfers between devices: 14.9 us -> 11.6 us  [exchange(): return lax.ppermute(values, ('z', 'yl'), [(i, i ^ mask) for i in range(16)])]
    ppermute x1, waiting for transfers between devices: 3 us -> 0.01 us  [exchange(): return lax.ppermute(values, 'yh', SWAP)]
    ppermute x1, starting transfers between devices: 1.65 us -> 3.83 us  [exchange(): return lax.ppermute(values, 'yh', SWAP)]
    ppermute x4, starting transfers between devices: 11.3 us -> 9.32 us  [exchange(): return lax.ppermute(values, ('z', 'yl'), [(i, i ^ mask) for i in range(16)])]
    ppermute x3, starting transfers between devices: 4.28 us -> 6.03 us  [moved(): lax.ppermute(parts[flip], ('yh', 'c'), [(i, i ^ flip) for i in range(4)])]
  transfers between devices with their start and end apart: 13 -> 13, of which waited for: 5 -> 4; matrix products, arithmetic and copies ran while one was open for 3% -> 3% of each run, Pallas kernels for 31% -> 32%
where the time goes in v6:
time: 85.7 us; the launch traced here: 85.5 us
  Pallas kernels  32.5 us (38%)
  starting transfers between devices  27.8 us (32%)
  waiting for transfers between devices  21 us (25%)
  other arithmetic  3.82 us (4%)
    pallas_call x4, Pallas kernels, replicas(): pl.pallas_call(replicas_kernel, grid_spec=pltpu.PrefetchScalarGridSpec(nu...  19.3 us
    ppermute x4, waiting for transfers between devices, exchange(): return lax.ppermute(values, ('z', 'yl'), [(i, i ^ mask) for i in range(16)])  11.6 us
    pallas_call x4, Pallas kernels, beams_block(): pl.pallas_call(functools.partial(beams_kernel, slot=step), in_specs=[VMEM...  9.55 us
    ppermute x3, waiting for transfers between devices, per_device(): lax.ppermute(beams, 'x', [(i, (i + dx) % 4) for i in range(4)])  9.37 us
    ppermute x4, starting transfers between devices, exchange(): return lax.ppermute(values, ('z', 'yl'), [(i, i ^ mask) for i in range(16)])  9.32 us
    ppermute x3, starting transfers between devices, moved(): lax.ppermute(parts[flip], ('yh', 'c'), [(i, i ^ flip) for i in range(4)])  6.03 us
    ppermute x3, starting transfers between devices, per_device(): lax.ppermute(beams, 'x', [(i, (i + dx) % 4) for i in range(4)])  5.77 us
    ppermute x1, starting transfers between devices, exchange(): return lax.ppermute(values, 'yh', SWAP)  3.83 us
  transfers between devices with their start and end apart: 13, of which 4 were waited for; matrix products, arithmetic and copies ran while one was open for 3% of the time, Pallas kernels for 32%

profile of v6, /device:TPU:1, one launch (start us, length us, event | category | flops | bytes accessed | tf_op | source)
XLA Modules:
  0.0 85.5 jit_solution(8857417131750751879)
XLA Ops:
  1.5 3.8 %collective-permute-start = (bf16[1,48,256]{2,1,0:T(8,128)(2,1)S(1)}, bf16[1,48,256]{2,1,0:T(8,128)(2,1)S(1)}, u32[]{:S(2)}, u32[]{:S(2)}) collective-permute-start(bf16[1,48,256]{2,1,0:T(8,128)(2,1)S(1)} %reshape.16.a_ref), channel_id=1, source_target_pairs={{0,2},{2,0},{1,3},{3,1},{4,6},{6,4},{5,7},{7,5},{8,10},{10,8},{9,1... | collective-permute-start | bytes 73736 | tf_op jit(solution)/shard_map/ppermute | solution.py:288
  5.3 2.4 %fusion.3 = (s16[4,256,256]{2,1,0:T(8,128)(2,1)S(1)}, s16[4,256,256]{2,1,0:T(8,128)(2,1)S(1)}, s16[4,256,256]{2,1,0:T(8,128)(2,1)S(1)}, s16[4,256,256]{2,1,0:T(8,128)(2,1)S(1)}) fusion(s32[4,2,2,256,256]{4,3,2,1,0:T(8,128)} %bitcast.30, s32[]{:T(128)S(6)} %select_n.42, s32[]{:T(128)S(6)} %select_n.41, s32[]{:T(128)S(6)} %select_n.40, s32[]{:T(128)S(6)} %select_n.39), kind=kLoop, calls=%fused_computation.7 | loop fusion | flops 1048576 | bytes 6291472 | tf_op jit(solution)/shard_map/convert_element_type | solution.py:277
  8.3 1.9 %collective-permute-start.3 = (s16[4,256,256]{2,1,0:T(8,128)(2,1)S(1)}, s16[4,256,256]{2,1,0:T(8,128)(2,1)S(1)}, u32[]{:S(2)}, u32[]{:S(2)}) collective-permute-start(s16[4,256,256]{2,1,0:T(8,128)(2,1)S(1)} %get-tuple-element.41), channel_id=1, source_target_pairs={{0,1},{1,0},{2,3},{3,2},{4,5},{5,4},{6,7},{7,6},{8,9},{9,8},{10,11... | collective-permute-start | bytes 1572872 | tf_op jit(solution)/shard_map/ppermute | solution.py:284
  10.2 2.4 %collective-permute-start.5 = (s16[4,256,256]{2,1,0:T(8,128)(2,1)S(1)}, s16[4,256,256]{2,1,0:T(8,128)(2,1)S(1)}, u32[]{:S(2)}, u32[]{:S(2)}) collective-permute-start(s16[4,256,256]{2,1,0:T(8,128)(2,1)S(1)} %get-tuple-element.43), channel_id=1, source_target_pairs={{0,2},{1,3},{2,0},{3,1},{4,6},{5,7},{6,4},{7,5},{8,10},{9,11},{10,... | collective-permute-start | bytes 1572872 | tf_op jit(solution)/shard_map/ppermute | solution.py:284
  12.6 4.5 %replicas_own.1 = (bf16[4,8,256,512]{3,2,1,0:T(8,128)(2,1)S(1)}, s32[8,128]{1,0:T(8,128)S(1)}) custom-call(s32[5]{0:T(128)S(1)} %stack.23.place, s16[4,256,256]{2,1,0:T(8,128)(2,1)S(1)} %get-tuple-element.39.travel_ref, bf16[2,48,256]{2,1,0:T(8,128)(2,1)S(1)} %join_1.1.after_ref.a_ref), custom_call_target="tpu_custom_call" | custom-call | flops 40000000000 | bytes 1000000 | tf_op jit(solution)/shard_map/replicas_own/pallas_call | solution.py:113
  17.2 7.0 %collective-permute-start.2 = (bf16[4,48,256]{2,1,0:T(8,128)(2,1)S(1)}, bf16[4,48,256]{2,1,0:T(8,128)(2,1)S(1)}, u32[]{:S(2)}, u32[]{:S(2)}) collective-permute-start(bf16[4,48,256]{2,1,0:T(8,128)(2,1)S(1)} %join_2.1.after_ref.a_ref), channel_id=1, source_target_pairs={{0,128},{16,144},{32,160},{48,176},{64,192},{80,208},{96,224},{112... | collective-permute-start | bytes 294920 | tf_op jit(solution)/shard_map/ppermute | solution.py:290
  24.2 4.5 %replicas_near.1 = (bf16[4,8,256,512]{3,2,1,0:T(8,128)(2,1)S(1)}, s32[8,128]{1,0:T(8,128)S(1)}) custom-call(s32[5]{0:T(128)S(1)} %stack.23.place, s16[4,256,256]{2,1,0:T(8,128)(2,1)S(1)} %collective-permute-done.3.travel_ref, bf16[4,48,256]{2,1,0:T(8,128)(2,1)S(1)} %join_2.1.after_ref.a_ref), custom_call_target="tpu_custom_call" | custom-call | flops 40000000000 | bytes 1000000 | tf_op jit(solution)/shard_map/replicas_near/pallas_call | solution.py:113
  28.7 1.7 %collective-permute-start.4 = (bf16[8,48,256]{2,1,0:T(8,128)(2,1)S(1)}, bf16[8,48,256]{2,1,0:T(8,128)(2,1)S(1)}, u32[]{:S(2)}, u32[]{:S(2)}) collective-permute-start(bf16[8,48,256]{2,1,0:T(8,128)(2,1)S(1)} %join_4.1.a_ref), channel_id=1, source_target_pairs={{0,64},{16,80},{32,96},{48,112},{64,0},{80,16},{96,32},{112,48},{1... | collective-permute-start | bytes 589832 | tf_op jit(solution)/shard_map/ppermute | solution.py:290
  30.5 1.8 %collective-permute-start.7 = (s16[4,256,256]{2,1,0:T(8,128)(2,1)S(1)}, s16[4,256,256]{2,1,0:T(8,128)(2,1)S(1)}, u32[]{:S(2)}, u32[]{:S(2)}) collective-permute-start(s16[4,256,256]{2,1,0:T(8,128)(2,1)S(1)} %get-tuple-element.50), channel_id=1, source_target_pairs={{0,3},{1,2},{2,1},{3,0},{4,7},{5,6},{6,5},{7,4},{8,11},{9,10},{10,... | collective-permute-start | bytes 1572872 | tf_op jit(solution)/shard_map/ppermute | solution.py:284
  32.2 8.1 %collective-permute-done.4.b_ref = bf16[8,48,256]{2,1,0:T(8,128)(2,1)S(1)} collective-permute-done((bf16[8,48,256]{2,1,0:T(8,128)(2,1)S(1)}, bf16[8,48,256]{2,1,0:T(8,128)(2,1)S(1)}, u32[]{:S(2)}, u32[]{:S(2)}) %collective-permute-start.4) | collective-permute-done | bytes 196640 | tf_op jit(solution)/shard_map/ppermute | solution.py:290
  40.4 1.0 %collective-permute-start.8 = (bf16[16,48,256]{2,1,0:T(8,128)(2,1)S(1)}, bf16[16,48,256]{2,1,0:T(8,128)(2,1)S(1)}, u32[]{:S(2)}, u32[]{:S(2)}) collective-permute-start(bf16[16,48,256]{2,1,0:T(8,128)(2,1)S(1)} %join_8.1.low_ref.after_ref), channel_id=1, source_target_pairs={{0,1},{1,0},{2,3},{3,2},{4,5},{5,4},{6,7},{7,6},{8,9},{9,8},{10,11... | collective-permute-start | bytes 1179656 | tf_op jit(solution)/shard_map/ppermute | solution.py:307
  41.5 5.1 %replicas_far.1 = (bf16[4,8,256,512]{3,2,1,0:T(8,128)(2,1)S(1)}, s32[8,128]{1,0:T(8,128)}) custom-call(s32[5]{0:T(128)S(1)} %stack.23.place, s16[4,256,256]{2,1,0:T(8,128)(2,1)S(1)} %collective-permute-done.5.travel_ref, bf16[16,48,256]{2,1,0:T(8,128)(2,1)S(1)} %join_8.1.low_ref.after_ref), custom_call_target="tpu_custom_call" | custom-call | flops 40000000000 | bytes 1000000 | tf_op jit(solution)/shard_map/replicas_far/pallas_call | solution.py:113
  46.6 3.5 %collective-permute-done.6.high_ref.after_ref = bf16[16,48,256]{2,1,0:T(8,128)(2,1)S(1)} collective-permute-done((bf16[16,48,256]{2,1,0:T(8,128)(2,1)S(1)}, bf16[16,48,256]{2,1,0:T(8,128)(2,1)S(1)}, u32[]{:S(2)}, u32[]{:S(2)}) %collective-permute-start.6) | collective-permute-done | bytes 393248 | tf_op jit(solution)/shard_map/ppermute | solution.py:290
  50.1 1.9 %collective-permute-start.9 = (bf16[16,48,256]{2,1,0:T(8,128)(2,1)S(1)}, bf16[16,48,256]{2,1,0:T(8,128)(2,1)S(1)}, u32[]{:S(2)}, u32[]{:S(2)}) collective-permute-start(bf16[16,48,256]{2,1,0:T(8,128)(2,1)S(1)} %collective-permute-done.6.high_ref.after_ref), channel_id=1, source_target_pairs={{0,1},{1,0},{2,3},{3,2},{4,5},{5,4},{6,7},{7,6},{8,9},{9,8},{10,11... | collective-permute-start | bytes 1179656 | tf_op jit(solution)/shard_map/ppermute | solution.py:309
  52.0 5.1 %replicas_both.1 = (bf16[4,8,256,512]{3,2,1,0:T(8,128)(2,1)S(1)}, s32[8,128]{1,0:T(8,128)}) custom-call(s32[5]{0:T(128)S(1)} %stack.23.place, s16[4,256,256]{2,1,0:T(8,128)(2,1)S(1)} %collective-permute-done.7.travel_ref, bf16[16,48,256]{2,1,0:T(8,128)(2,1)S(1)} %collective-permute-done.6.high_ref.after_ref), custom_call_target="tpu_custom_call" | custom-call | flops 40000000000 | bytes 1000000 | tf_op jit(solution)/shard_map/replicas_both/pallas_call | solution.py:113
  58.9 2.4 %beams_0.1 = bf16[272,768]{1,0:T(8,128)(2,1)S(1)} custom-call(bf16[4,8,256,512]{3,2,1,0:T(8,128)(2,1)S(1)} %get-tuple-element.46.refs_0_, bf16[4,8,256,512]{3,2,1,0:T(8,128)(2,1)S(1)} %get-tuple-element.47.refs_1_, bf16[4,8,256,512]{3,2,1,0:T(8,128)(2,1)S(1)} %get-tuple-element.49.refs_2_, bf16[4,8,256,512]{3,2,1,0:T(8,128)(2,1)S(1)} %get-tuple-element.51.refs_3_, ...), custom_call_target="tpu_custom_call" | custom-call | flops 3000000000 | bytes 1000000 | tf_op jit(solution)/shard_map/beams_0/pallas_call | solution.py:163
  61.3 3.0 %collective-permute-start.10 = (bf16[272,768]{1,0:T(8,128)(2,1)S(1)}, bf16[272,768]{1,0:T(8,128)(2,1)S(1)}, u32[]{:S(2)}, u32[]{:S(2)}) collective-permute-start(bf16[272,768]{1,0:T(8,128)(2,1)S(1)} %beams_0.1), channel_id=1, source_target_pairs={{0,8},{4,12},{8,0},{12,4},{1,9},{5,13},{9,1},{13,5},{2,10},{6,14},... | collective-permute-start | bytes 1253384 | tf_op jit(solution)/shard_map/ppermute | solution.py:321
  64.3 2.4 %beams_1.1 = bf16[272,768]{1,0:T(8,128)(2,1)S(1)} custom-call(bf16[4,8,256,512]{3,2,1,0:T(8,128)(2,1)S(1)} %get-tuple-element.46.refs_0_, bf16[4,8,256,512]{3,2,1,0:T(8,128)(2,1)S(1)} %get-tuple-element.47.refs_1_, bf16[4,8,256,512]{3,2,1,0:T(8,128)(2,1)S(1)} %get-tuple-element.49.refs_2_, bf16[4,8,256,512]{3,2,1,0:T(8,128)(2,1)S(1)} %get-tuple-element.51.refs_3_, ...), custom_call_target="tpu_custom_call" | custom-call | flops 3000000000 | bytes 1000000 | tf_op jit(solution)/shard_map/beams_1/pallas_call | solution.py:163
  66.7 2.4 %beams_2.1 = bf16[272,768]{1,0:T(8,128)(2,1)S(1)} custom-call(bf16[4,8,256,512]{3,2,1,0:T(8,128)(2,1)S(1)} %get-tuple-element.46.refs_0_, bf16[4,8,256,512]{3,2,1,0:T(8,128)(2,1)S(1)} %get-tuple-element.47.refs_1_, bf16[4,8,256,512]{3,2,1,0:T(8,128)(2,1)S(1)} %get-tuple-element.49.refs_2_, bf16[4,8,256,512]{3,2,1,0:T(8,128)(2,1)S(1)} %get-tuple-element.51.refs_3_, ...), custom_call_target="tpu_custom_call" | custom-call | flops 3000000000 | bytes 1000000 | tf_op jit(solution)/shard_map/beams_2/pallas_call | solution.py:163
  69.5 2.4 %collective-permute-start.12 = (bf16[272,768]{1,0:T(8,128)(2,1)S(1)}, bf16[272,768]{1,0:T(8,128)(2,1)S(1)}, u32[]{:S(2)}, u32[]{:S(2)}) collective-permute-start(bf16[272,768]{1,0:T(8,128)(2,1)S(1)} %beams_2.1), channel_id=1, source_target_pairs={{0,12},{4,0},{8,4},{12,8},{1,13},{5,1},{9,5},{13,9},{2,14},{6,2},{... | collective-permute-start | bytes 1253384 | tf_op jit(solution)/shard_map/ppermute | solution.py:321
  71.9 2.5 %collective-permute-done.10.refs_0_ = bf16[272,768]{1,0:T(8,128)(2,1)S(1)} collective-permute-done((bf16[272,768]{1,0:T(8,128)(2,1)S(1)}, bf16[272,768]{1,0:T(8,128)(2,1)S(1)}, u32[]{:S(2)}, u32[]{:S(2)}) %collective-permute-start.10) | collective-permute-done | bytes 417824 | tf_op jit(solution)/shard_map/ppermute | solution.py:321
  74.4 2.4 %beams_3.1.refs_3_ = f32[256,768]{1,0:T(8,128)S(1)} custom-call(bf16[4,8,256,512]{3,2,1,0:T(8,128)(2,1)S(1)} %get-tuple-element.46.refs_0_, bf16[4,8,256,512]{3,2,1,0:T(8,128)(2,1)S(1)} %get-tuple-element.47.refs_1_, bf16[4,8,256,512]{3,2,1,0:T(8,128)(2,1)S(1)} %get-tuple-element.49.refs_2_, bf16[4,8,256,512]{3,2,1,0:T(8,128)(2,1)S(1)} %get-tuple-element.51.refs_3_, ...), custom_call_target="tpu_custom_call" | custom-call | flops 3000000000 | bytes 1000000 | tf_op jit(solution)/shard_map/beams_3/pallas_call | solution.py:163
  76.8 6.9 %collective-permute-done.11.refs_1_ = bf16[272,768]{1,0:T(8,128)(2,1)S(1)} collective-permute-done((bf16[272,768]{1,0:T(8,128)(2,1)S(1)}, bf16[272,768]{1,0:T(8,128)(2,1)S(1)}, u32[]{:S(2)}, u32[]{:S(2)}) %collective-permute-start.11) | collective-permute-done | bytes 417824 | tf_op jit(solution)/shard_map/ppermute | solution.py:321
  83.6 1.9 %finish.1 = f32[48,256]{1,0:T(8,128)} custom-call(s32[5]{0:T(128)S(1)} %stack.23.place, bf16[272,768]{1,0:T(8,128)(2,1)S(1)} %collective-permute-done.10.refs_0_, bf16[272,768]{1,0:T(8,128)(2,1)S(1)} %collective-permute-done.11.refs_1_, bf16[272,768]{1,0:T(8,128)(2,1)S(1)} %collective-permute-done.12.refs_2_, f32[256,768]{1,0:T(8,128)S(1)} %beams_3.1.refs_3_, ...), custom_call_target="tpu_custom_call" | custom-call | tf_op jit(solution)/shard_map/finish/pallas_call | solution.py:250
  (27 shorter events, 4.4 us)
Async XLA Ops:
  1.5 6.4 %collective-permute-start = (bf16[1,48,256]{2,1,0:T(8,128)(2,1)S(1)}, bf16[1,48,256]{2,1,0:T(8,128)(2,1)S(1)}, u32[]{:S(2)}, u32[]{:S(2)}) collective-permute-start(bf16[1,48,256]{2,1,0:T(8,128)(2,1)S(1)} %reshape.16.a_ref), channel_id=1, source_target_pairs={{0,2},{2,0},{1,3},{3,1},{4,6},{6,4},{5,7},{7,5},{8,10},{10,8},{9,1... | collective-permute-start | bytes 73736 | tf_op jit(solution)/shard_map/ppermute | solution.py:288
  7.8 9.3 %collective-permute-start.1 = (bf16[2,48,256]{2,1,0:T(8,128)(2,1)S(1)}, bf16[2,48,256]{2,1,0:T(8,128)(2,1)S(1)}, u32[]{:S(2)}, u32[]{:S(2)}) collective-permute-start(bf16[2,48,256]{2,1,0:T(8,128)(2,1)S(1)} %join_1.1.after_ref.a_ref), channel_id=1, source_target_pairs={{0,16},{16,0},{32,48},{48,32},{64,80},{80,64},{96,112},{112,96},{1... | collective-permute-start | bytes 147464 | tf_op jit(solution)/shard_map/ppermute | solution.py:290
  8.3 15.8 %collective-permute-start.3 = (s16[4,256,256]{2,1,0:T(8,128)(2,1)S(1)}, s16[4,256,256]{2,1,0:T(8,128)(2,1)S(1)}, u32[]{:S(2)}, u32[]{:S(2)}) collective-permute-start(s16[4,256,256]{2,1,0:T(8,128)(2,1)S(1)} %get-tuple-element.41), channel_id=1, source_target_pairs={{0,1},{1,0},{2,3},{3,2},{4,5},{5,4},{6,7},{7,6},{8,9},{9,8},{10,11... | collective-permute-start | bytes 1572872 | tf_op jit(solution)/shard_map/ppermute | solution.py:284
  10.2 30.1 %collective-permute-start.5 = (s16[4,256,256]{2,1,0:T(8,128)(2,1)S(1)}, s16[4,256,256]{2,1,0:T(8,128)(2,1)S(1)}, u32[]{:S(2)}, u32[]{:S(2)}) collective-permute-start(s16[4,256,256]{2,1,0:T(8,128)(2,1)S(1)} %get-tuple-element.43), channel_id=1, source_target_pairs={{0,2},{1,3},{2,0},{3,1},{4,6},{5,7},{6,4},{7,5},{8,10},{9,11},{10,... | collective-permute-start | bytes 1572872 | tf_op jit(solution)/shard_map/ppermute | solution.py:284
  17.2 11.5 %collective-permute-start.2 = (bf16[4,48,256]{2,1,0:T(8,128)(2,1)S(1)}, bf16[4,48,256]{2,1,0:T(8,128)(2,1)S(1)}, u32[]{:S(2)}, u32[]{:S(2)}) collective-permute-start(bf16[4,48,256]{2,1,0:T(8,128)(2,1)S(1)} %join_2.1.after_ref.a_ref), channel_id=1, source_target_pairs={{0,128},{16,144},{32,160},{48,176},{64,192},{80,208},{96,224},{112... | collective-permute-start | bytes 294920 | tf_op jit(solution)/shard_map/ppermute | solution.py:290
  28.7 11.6 %collective-permute-start.4 = (bf16[8,48,256]{2,1,0:T(8,128)(2,1)S(1)}, bf16[8,48,256]{2,1,0:T(8,128)(2,1)S(1)}, u32[]{:S(2)}, u32[]{:S(2)}) collective-permute-start(bf16[8,48,256]{2,1,0:T(8,128)(2,1)S(1)} %join_4.1.a_ref), channel_id=1, source_target_pairs={{0,64},{16,80},{32,96},{48,112},{64,0},{80,16},{96,32},{112,48},{1... | collective-permute-start | bytes 589832 | tf_op jit(solution)/shard_map/ppermute | solution.py:290
  30.5 21.5 %collective-permute-start.7 = (s16[4,256,256]{2,1,0:T(8,128)(2,1)S(1)}, s16[4,256,256]{2,1,0:T(8,128)(2,1)S(1)}, u32[]{:S(2)}, u32[]{:S(2)}) collective-permute-start(s16[4,256,256]{2,1,0:T(8,128)(2,1)S(1)} %get-tuple-element.50), channel_id=1, source_target_pairs={{0,3},{1,2},{2,1},{3,0},{4,7},{5,6},{6,5},{7,4},{8,11},{9,10},{10,... | collective-permute-start | bytes 1572872 | tf_op jit(solution)/shard_map/ppermute | solution.py:284
  40.3 9.8 %collective-permute-start.6 = (bf16[16,48,256]{2,1,0:T(8,128)(2,1)S(1)}, bf16[16,48,256]{2,1,0:T(8,128)(2,1)S(1)}, u32[]{:S(2)}, u32[]{:S(2)}) collective-permute-start(bf16[16,48,256]{2,1,0:T(8,128)(2,1)S(1)} %join_8.1.low_ref.after_ref), channel_id=1, source_target_pairs={{0,32},{16,48},{32,0},{48,16},{64,96},{80,112},{96,64},{112,80},{1... | collective-permute-start | bytes 1179656 | tf_op jit(solution)/shard_map/ppermute | solution.py:290
  40.4 17.6 %collective-permute-start.8 = (bf16[16,48,256]{2,1,0:T(8,128)(2,1)S(1)}, bf16[16,48,256]{2,1,0:T(8,128)(2,1)S(1)}, u32[]{:S(2)}, u32[]{:S(2)}) collective-permute-start(bf16[16,48,256]{2,1,0:T(8,128)(2,1)S(1)} %join_8.1.low_ref.after_ref), channel_id=1, source_target_pairs={{0,1},{1,0},{2,3},{3,2},{4,5},{5,4},{6,7},{7,6},{8,9},{9,8},{10,11... | collective-permute-start | bytes 1179656 | tf_op jit(solution)/shard_map/ppermute | solution.py:307
  50.1 7.9 %collective-permute-start.9 = (bf16[16,48,256]{2,1,0:T(8,128)(2,1)S(1)}, bf16[16,48,256]{2,1,0:T(8,128)(2,1)S(1)}, u32[]{:S(2)}, u32[]{:S(2)}) collective-permute-start(bf16[16,48,256]{2,1,0:T(8,128)(2,1)S(1)} %collective-permute-done.6.high_ref.after_ref), channel_id=1, source_target_pairs={{0,1},{1,0},{2,3},{3,2},{4,5},{5,4},{6,7},{7,6},{8,9},{9,8},{10,11... | collective-permute-start | bytes 1179656 | tf_op jit(solution)/shard_map/ppermute | solution.py:309
  61.3 13.0 %collective-permute-start.10 = (bf16[272,768]{1,0:T(8,128)(2,1)S(1)}, bf16[272,768]{1,0:T(8,128)(2,1)S(1)}, u32[]{:S(2)}, u32[]{:S(2)}) collective-permute-start(bf16[272,768]{1,0:T(8,128)(2,1)S(1)} %beams_0.1), channel_id=1, source_target_pairs={{0,8},{4,12},{8,0},{12,4},{1,9},{5,13},{9,1},{13,5},{2,10},{6,14},... | collective-permute-start | bytes 1253384 | tf_op jit(solution)/shard_map/ppermute | solution.py:321
  69.1 14.5 %copy-start = (s32[2,768]{1,0:T(2,128)S(1)}, s32[2,768]{1,0:T(2,128)}, u32[]{:S(2)}) copy-start(s32[2,768]{1,0:T(2,128)} %constant.54.clone.refs_8_) | copy-start | bytes 18436
  69.1 14.5 %collective-permute-start.11 = (bf16[272,768]{1,0:T(8,128)(2,1)S(1)}, bf16[272,768]{1,0:T(8,128)(2,1)S(1)}, u32[]{:S(2)}, u32[]{:S(2)}) collective-permute-start(bf16[272,768]{1,0:T(8,128)(2,1)S(1)} %beams_1.1), channel_id=1, source_target_pairs={{0,4},{4,8},{8,12},{12,0},{1,5},{5,9},{9,13},{13,1},{2,6},{6,10},{... | collective-permute-start | bytes 1253384 | tf_op jit(solution)/shard_map/ppermute | solution.py:321
  69.5 14.1 %collective-permute-start.12 = (bf16[272,768]{1,0:T(8,128)(2,1)S(1)}, bf16[272,768]{1,0:T(8,128)(2,1)S(1)}, u32[]{:S(2)}, u32[]{:S(2)}) collective-permute-start(bf16[272,768]{1,0:T(8,128)(2,1)S(1)} %beams_2.1), channel_id=1, source_target_pairs={{0,12},{4,0},{8,4},{12,8},{1,13},{5,1},{9,5},{13,9},{2,14},{6,2},{... | collective-permute-start | bytes 1253384 | tf_op jit(solution)/shard_map/ppermute | solution.py:321

commit v7 on v6

--- a/solution.py
+++ b/solution.py
@@ -128,22 +128,24 @@
     )(place, travel, after)
 
 
-def join_kernel(a_ref, b_ref, token_ref, out_ref):
-    half = a_ref.shape[0]
-    out_ref[0:half] = a_ref[...]
-    out_ref[half : 2 * half] = b_ref[...]
-
-
-def join(a, b, token):
+def join_kernel(*refs):
+    *sources, token_ref, out_ref = refs
+    rows = sources[0].shape[0]
+    for index, source in enumerate(sources):
+        out_ref[index * rows : (index + 1) * rows] = source[...]
+
+
+def join(token, *arrays):
+    first = arrays[0]
     return pl.pallas_call(
         join_kernel,
-        in_specs=[VMEM] * 3,
+        in_specs=[VMEM] * (len(arrays) + 1),
         out_specs=VMEM,
-        out_shape=jax.ShapeDtypeStruct((2 * a.shape[0],) + a.shape[1:], a.dtype),
+        out_shape=jax.ShapeDtypeStruct((len(arrays) * first.shape[0],) + first.shape[1:], first.dtype),
         cost_estimate=pl.CostEstimate(flops=0, bytes_accessed=100_000, transcendentals=0),
         compiler_params=pltpu.CompilerParams(vmem_limit_bytes=2 << 20),
-        name=f"join_{a.shape[0]}",
-    )(a, b, token)
+        name=f"join_{first.shape[0]}",
+    )(*arrays, token)
 
 
 def beams_kernel(*refs, slot):
@@ -173,10 +175,10 @@
 
 def prepare_kernel(low_ref, high_ref, w_ref, norm_ref, wide, *, flip, first_row):
     for g in range(16):
-        source_ref = (low_ref, high_ref)[g // 8]
+        source_ref, class_row = (low_ref, 0) if g < 4 else (high_ref, 8 * (g // 4 - 1))
         for half in range(CH // 128):
             lanes = slice(half * 128, (half + 1) * 128)
-            wide[half, g * 48 : (g + 1) * 48, :] = source_ref[2 * (g % 8) + flip, :, lanes].astype(f32)
+            wide[half, g * 48 : (g + 1) * 48, :] = source_ref[class_row + 2 * (g % 4) + flip, :, lanes].astype(f32)
     squares = jnp.zeros((COLS, CH), f32)
     for f in range(NF):
         real, imag = [
@@ -226,16 +228,19 @@
 
 def column_tables():
     slot = np.arange(NF * COLS) % 48
-    place = slot % 16
-    relative = sum(((place >> bit) & 1) * mask for bit, mask in enumerate((1, 8, 4, 2)))
-    return np.stack([relative, slot // 16]).astype(np.int32)
+    source = slot % 16
+    step_z = np.array([0, 1, 7, 2])[source // 4]
+    return np.stack([step_z, source % 2, source % 4 // 2 * 4, slot // 16]).astype(np.int32)
 
 
 def finish_kernel(place, *refs, count):
     received, own_ref, norms, table_ref, out_ref = refs[0:3], refs[3], refs[4:8], refs[8], refs[9]
     window = lax.broadcasted_iota(jnp.int32, (48, NF * COLS), 0)
-    source = table_ref[0:1, :] ^ place[4]
-    pick = jnp.where(window == 3 * source + table_ref[1:2, :], 1.0, 0.0).astype(bf16)
+    step_z, flip_yl, flip_z, part = [table_ref[row : row + 1, :] for row in range(4)]
+    z, yl = place[4], place[5]
+    step_z = step_z + jnp.where(step_z == 2, 4 * (1 - z % 2), 0)
+    source = 2 * (((z + step_z) & 7) ^ flip_z) + (yl ^ flip_yl)
+    pick = jnp.where(window == 3 * source + part, 1.0, 0.0).astype(bf16)
     beams = own_ref[...]
     norm_rows = sum(ref[...].astype(f32) for ref in norms)
     for ref in received:
@@ -268,7 +273,7 @@
 def per_device(spectra, travel, quality):
     x, yh, core = lax.axis_index("x"), lax.axis_index("yh"), lax.axis_index("c")
     order = [(x + dx) % 4 for dx in STEPS]
-    place = jnp.stack(order + [lax.axis_index("z") * 2 + lax.axis_index("yl")]).astype(jnp.int32)
+    place = jnp.stack(order + [lax.axis_index("z"), lax.axis_index("yl")]).astype(jnp.int32)
     blocks = travel.reshape(4, 2, 2, ROWS, CH)
 
     def travel_for(flip_y, flip_c):
@@ -283,29 +288,26 @@
     def moved(flip):
         return lax.ppermute(parts[flip], ("yh", "c"), [(i, i ^ flip) for i in range(4)])
 
-    def exchange(values, stage):
-        if stage == 0:
-            return lax.ppermute(values, "yh", SWAP)
-        mask = (1, 8, 4, 2)[stage - 1]
-        return lax.ppermute(values, ("z", "yl"), [(i, i ^ mask) for i in range(16)])
+    def along_z(values, target):
+        return lax.ppermute(values, "z", [(i, target(i) % 8) for i in range(8)])
 
     held = block
-    other = exchange(held, 0)
-    held = join(held, other, other)
+    other = lax.ppermute(held, "yh", SWAP)
+    held = join(other, held, other)
     held, *parts = tie(held, *parts)
     far, near, both = moved(2), moved(1), moved(3)
-    other = exchange(held, 1)
+    other = lax.ppermute(held, "yl", SWAP)
     rep_own, token = replicas(place, parts[0], held, "own")
-    held = join(held, other, token)
-    other = exchange(held, 2)
+    held = join(token, held, other)
+    other = along_z(held, lambda i: i ^ 4)
     rep_near, token = replicas(place, near, held, "near")
-    held = join(held, other, token)
-    other = exchange(held, 3)
-    held = join(held, other, token)
-    held, far = tie(held, far)
-    other = exchange(held, 4)
+    held = join(token, held, other)
+    two_away = along_z(held, lambda i: i - 2 if i % 2 else i + 2)
+    above = along_z(held, lambda i: i - 1)
+    below = along_z(held, lambda i: i + 1)
     held_swapped = lax.ppermute(held, "c", SWAP)
     rep_far, token = replicas(place, far, held, "far")
+    other = join(token, above, below, two_away)
     other_swapped = lax.ppermute(other, "c", SWAP)
     rep_both, _ = replicas(place, both, other, "both")
     halves = ((held, other, 0), (held_swapped, other_swapped, 0), (held, other, 1), (held_swapped, other_swapped, 1))

time: 85.7 us -> 79.6 us (0.929)
  waiting for transfers between devices: 21 us -> 13.6 us
  starting transfers between devices: 27.8 us -> 29.7 us
    ppermute x5 -> x6, waiting for transfers between devices: 11.6 us -> 4.21 us  [the longest x4 4.2 us: along_z(): return lax.ppermute(values, 'z', [(i, target(i) % 8) for i in range(8)])]
    ppermute x5 -> x6, starting transfers between devices: 13.2 us -> 14.7 us  [the longest x4 10.4 us: along_z(): return lax.ppermute(values, 'z', [(i, target(i) % 8) for i in range(8)])]
    ppermute x3, starting transfers between devices: 6.03 us -> 5.14 us  [moved(): lax.ppermute(parts[flip], ('yh', 'c'), [(i, i ^ flip) for i in range(4)])]
  transfers between devices with their start and end apart: 13 -> 14, of which waited for: 4 -> 4; matrix products, arithmetic and copies ran while one was open for 3% -> 3% of each run, Pallas kernels for 32% -> 34%
where the time goes in v7:
time: 79.6 us; the launch traced here: 79.5 us
  Pallas kernels  32 us (40%)
  starting transfers between devices  29.7 us (37%)
  waiting for transfers between devices  13.6 us (17%)
  other arithmetic  3.82 us (5%)
    pallas_call x4, Pallas kernels, replicas(): pl.pallas_call(replicas_kernel, grid_spec=pltpu.PrefetchScalarGridSpec(nu...  18.7 us
    ppermute x4, starting transfers between devices, along_z(): return lax.ppermute(values, 'z', [(i, target(i) % 8) for i in range(8)])  10.4 us
    pallas_call x4, Pallas kernels, beams_block(): pl.pallas_call(functools.partial(beams_kernel, slot=step), in_specs=[VMEM...  9.55 us
    ppermute x3, waiting for transfers between devices, per_device(): lax.ppermute(beams, 'x', [(i, (i + dx) % 4) for i in range(4)])  9.37 us
    ppermute x3, starting transfers between devices, per_device(): lax.ppermute(beams, 'x', [(i, (i + dx) % 4) for i in range(4)])  5.77 us
    ppermute x3, starting transfers between devices, moved(): lax.ppermute(parts[flip], ('yh', 'c'), [(i, i ^ flip) for i in range(4)])  5.14 us
    ppermute x4, waiting for transfers between devices, along_z(): return lax.ppermute(values, 'z', [(i, target(i) % 8) for i in range(8)])  4.2 us
    ppermute x1, starting transfers between devices, per_device(): other = lax.ppermute(held, 'yh', SWAP)  3.83 us
  transfers between devices with their start and end apart: 14, of which 4 were waited for; matrix products, arithmetic and copies ran while one was open for 3% of the time, Pallas kernels for 34%

profile of v7, /device:TPU:1, one launch (start us, length us, event | category | flops | bytes accessed | tf_op | source)
XLA Modules:
  0.0 79.5 jit_solution(8602315885974527833)
XLA Ops:
  1.5 3.8 %collective-permute-start = (bf16[1,48,256]{2,1,0:T(8,128)(2,1)S(1)}, bf16[1,48,256]{2,1,0:T(8,128)(2,1)S(1)}, u32[]{:S(2)}, u32[]{:S(2)}) collective-permute-start(bf16[1,48,256]{2,1,0:T(8,128)(2,1)S(1)} %reshape.16.refs_0_), channel_id=1, source_target_pairs={{0,2},{2,0},{1,3},{3,1},{4,6},{6,4},{5,7},{7,5},{8,10},{10,8},{9,1... | collective-permute-start | bytes 73736 | tf_op jit(solution)/shard_map/ppermute | solution.py:295
  5.3 2.4 %fusion.3 = (s16[4,256,256]{2,1,0:T(8,128)(2,1)S(1)}, s16[4,256,256]{2,1,0:T(8,128)(2,1)S(1)}, s16[4,256,256]{2,1,0:T(8,128)(2,1)S(1)}, s16[4,256,256]{2,1,0:T(8,128)(2,1)S(1)}) fusion(s32[4,2,2,256,256]{4,3,2,1,0:T(8,128)} %bitcast.31, s32[]{:T(128)S(6)} %select_n.42, s32[]{:T(128)S(6)} %select_n.41, s32[]{:T(128)S(6)} %select_n.40, s32[]{:T(128)S(6)} %select_n.39), kind=kLoop, calls=%fused_computation.7 | loop fusion | flops 1048576 | bytes 6291472 | tf_op jit(solution)/shard_map/convert_element_type | solution.py:282
  8.3 1.9 %collective-permute-start.3 = (s16[4,256,256]{2,1,0:T(8,128)(2,1)S(1)}, s16[4,256,256]{2,1,0:T(8,128)(2,1)S(1)}, u32[]{:S(2)}, u32[]{:S(2)}) collective-permute-start(s16[4,256,256]{2,1,0:T(8,128)(2,1)S(1)} %get-tuple-element.40), channel_id=1, source_target_pairs={{0,1},{1,0},{2,3},{3,2},{4,5},{5,4},{6,7},{7,6},{8,9},{9,8},{10,11... | collective-permute-start | bytes 1572872 | tf_op jit(solution)/shard_map/ppermute | solution.py:289
  10.2 2.4 %collective-permute-start.7 = (s16[4,256,256]{2,1,0:T(8,128)(2,1)S(1)}, s16[4,256,256]{2,1,0:T(8,128)(2,1)S(1)}, u32[]{:S(2)}, u32[]{:S(2)}) collective-permute-start(s16[4,256,256]{2,1,0:T(8,128)(2,1)S(1)} %get-tuple-element.42), channel_id=1, source_target_pairs={{0,2},{1,3},{2,0},{3,1},{4,6},{5,7},{6,4},{7,5},{8,10},{9,11},{10,... | collective-permute-start | bytes 1572872 | tf_op jit(solution)/shard_map/ppermute | solution.py:289
  12.6 0.9 %collective-permute-start.8 = (s16[4,256,256]{2,1,0:T(8,128)(2,1)S(1)}, s16[4,256,256]{2,1,0:T(8,128)(2,1)S(1)}, u32[]{:S(2)}, u32[]{:S(2)}) collective-permute-start(s16[4,256,256]{2,1,0:T(8,128)(2,1)S(1)} %get-tuple-element.48), channel_id=1, source_target_pairs={{0,3},{1,2},{2,1},{3,0},{4,7},{5,6},{6,5},{7,4},{8,11},{9,10},{10,... | collective-permute-start | bytes 1572872 | tf_op jit(solution)/shard_map/ppermute | solution.py:289
  13.5 4.5 %replicas_own.1 = (bf16[4,8,256,512]{3,2,1,0:T(8,128)(2,1)S(1)}, s32[8,128]{1,0:T(8,128)S(1)}) custom-call(s32[6]{0:T(128)S(1)} %stack.27.place, s16[4,256,256]{2,1,0:T(8,128)(2,1)S(1)} %get-tuple-element.38.travel_ref, bf16[2,48,256]{2,1,0:T(8,128)(2,1)S(1)} %join_1.1.after_ref.refs_0_), custom_call_target="tpu_custom_call" | custom-call | flops 40000000000 | bytes 1000000 | tf_op jit(solution)/shard_map/replicas_own/pallas_call | solution.py:113
  18.0 6.6 %collective-permute-start.2 = (bf16[4,48,256]{2,1,0:T(8,128)(2,1)S(1)}, bf16[4,48,256]{2,1,0:T(8,128)(2,1)S(1)}, u32[]{:S(2)}, u32[]{:S(2)}) collective-permute-start(bf16[4,48,256]{2,1,0:T(8,128)(2,1)S(1)} %join_2.1.after_ref.refs_0_), channel_id=1, source_target_pairs={{0,128},{32,160},{64,192},{96,224},{128,0},{160,32},{192,64},{224,... | collective-permute-start | bytes 294920 | tf_op jit(solution)/shard_map/ppermute | solution.py:292
  24.7 4.5 %replicas_near.1 = (bf16[4,8,256,512]{3,2,1,0:T(8,128)(2,1)S(1)}, s32[8,128]{1,0:T(8,128)S(1)}) custom-call(s32[6]{0:T(128)S(1)} %stack.27.place, s16[4,256,256]{2,1,0:T(8,128)(2,1)S(1)} %collective-permute-done.3.travel_ref, bf16[4,48,256]{2,1,0:T(8,128)(2,1)S(1)} %join_2.1.after_ref.refs_0_), custom_call_target="tpu_custom_call" | custom-call | flops 40000000000 | bytes 1000000 | tf_op jit(solution)/shard_map/replicas_near/pallas_call | solution.py:113
  29.2 3.8 %collective-permute-start.4 = (bf16[8,48,256]{2,1,0:T(8,128)(2,1)S(1)}, bf16[8,48,256]{2,1,0:T(8,128)(2,1)S(1)}, u32[]{:S(2)}, u32[]{:S(2)}) collective-permute-start(bf16[8,48,256]{2,1,0:T(8,128)(2,1)S(1)} %join_4.1.after_ref.low_ref), channel_id=1, source_target_pairs={{0,224},{32,0},{64,32},{96,64},{128,96},{160,128},{192,160},{224,1... | collective-permute-start | bytes 589832 | tf_op jit(solution)/shard_map/ppermute | solution.py:292
  33.0 1.5 %collective-permute-start.9 = (bf16[8,48,256]{2,1,0:T(8,128)(2,1)S(1)}, bf16[8,48,256]{2,1,0:T(8,128)(2,1)S(1)}, u32[]{:S(2)}, u32[]{:S(2)}) collective-permute-start(bf16[8,48,256]{2,1,0:T(8,128)(2,1)S(1)} %join_4.1.after_ref.low_ref), channel_id=1, source_target_pairs={{0,1},{1,0},{2,3},{3,2},{4,5},{5,4},{6,7},{7,6},{8,9},{9,8},{10,11... | collective-permute-start | bytes 589832 | tf_op jit(solution)/shard_map/ppermute | solution.py:308
  34.5 4.5 %replicas_far.1 = (bf16[4,8,256,512]{3,2,1,0:T(8,128)(2,1)S(1)}, s32[8,128]{1,0:T(8,128)S(1)}) custom-call(s32[6]{0:T(128)S(1)} %stack.27.place, s16[4,256,256]{2,1,0:T(8,128)(2,1)S(1)} %collective-permute-done.7.travel_ref, bf16[8,48,256]{2,1,0:T(8,128)(2,1)S(1)} %join_4.1.after_ref.low_ref), custom_call_target="tpu_custom_call" | custom-call | flops 40000000000 | bytes 1000000 | tf_op jit(solution)/shard_map/replicas_far/pallas_call | solution.py:113
  39.1 1.4 %collective-permute-done.5.refs_1_ = bf16[8,48,256]{2,1,0:T(8,128)(2,1)S(1)} collective-permute-done((bf16[8,48,256]{2,1,0:T(8,128)(2,1)S(1)}, bf16[8,48,256]{2,1,0:T(8,128)(2,1)S(1)}, u32[]{:S(2)}, u32[]{:S(2)}) %collective-permute-start.5) | collective-permute-done | bytes 196640 | tf_op jit(solution)/shard_map/ppermute | solution.py:292
  40.5 2.7 %collective-permute-done.6.refs_2_ = bf16[8,48,256]{2,1,0:T(8,128)(2,1)S(1)} collective-permute-done((bf16[8,48,256]{2,1,0:T(8,128)(2,1)S(1)}, bf16[8,48,256]{2,1,0:T(8,128)(2,1)S(1)}, u32[]{:S(2)}, u32[]{:S(2)}) %collective-permute-start.6) | collective-permute-done | bytes 196640 | tf_op jit(solution)/shard_map/ppermute | solution.py:292
  43.3 2.6 %collective-permute-start.10 = (bf16[24,48,256]{2,1,0:T(8,128)(2,1)S(1)}, bf16[24,48,256]{2,1,0:T(8,128)(2,1)S(1)}, u32[]{:S(2)}, u32[]{:S(2)}) collective-permute-start(bf16[24,48,256]{2,1,0:T(8,128)(2,1)S(1)} %join_8.1.high_ref.after_ref), channel_id=1, source_target_pairs={{0,1},{1,0},{2,3},{3,2},{4,5},{5,4},{6,7},{7,6},{8,9},{9,8},{10,11... | collective-permute-start | bytes 1769480 | tf_op jit(solution)/shard_map/ppermute | solution.py:311
  45.9 5.1 %replicas_both.1 = (bf16[4,8,256,512]{3,2,1,0:T(8,128)(2,1)S(1)}, s32[8,128]{1,0:T(8,128)}) custom-call(s32[6]{0:T(128)S(1)} %stack.27.place, s16[4,256,256]{2,1,0:T(8,128)(2,1)S(1)} %collective-permute-done.8.travel_ref, bf16[24,48,256]{2,1,0:T(8,128)(2,1)S(1)} %join_8.1.high_ref.after_ref), custom_call_target="tpu_custom_call" | custom-call | flops 40000000000 | bytes 1000000 | tf_op jit(solution)/shard_map/replicas_both/pallas_call | solution.py:113
  52.8 2.4 %beams_0.1 = bf16[272,768]{1,0:T(8,128)(2,1)S(1)} custom-call(bf16[4,8,256,512]{3,2,1,0:T(8,128)(2,1)S(1)} %get-tuple-element.45.refs_0_, bf16[4,8,256,512]{3,2,1,0:T(8,128)(2,1)S(1)} %get-tuple-element.46.refs_1_, bf16[4,8,256,512]{3,2,1,0:T(8,128)(2,1)S(1)} %get-tuple-element.47.refs_2_, bf16[4,8,256,512]{3,2,1,0:T(8,128)(2,1)S(1)} %get-tuple-element.49.refs_3_, ...), custom_call_target="tpu_custom_call" | custom-call | flops 3000000000 | bytes 1000000 | tf_op jit(solution)/shard_map/beams_0/pallas_call | solution.py:165
  55.3 3.0 %collective-permute-start.11 = (bf16[272,768]{1,0:T(8,128)(2,1)S(1)}, bf16[272,768]{1,0:T(8,128)(2,1)S(1)}, u32[]{:S(2)}, u32[]{:S(2)}) collective-permute-start(bf16[272,768]{1,0:T(8,128)(2,1)S(1)} %beams_0.1), channel_id=1, source_target_pairs={{0,8},{4,12},{8,0},{12,4},{1,9},{5,13},{9,1},{13,5},{2,10},{6,14},... | collective-permute-start | bytes 1253384 | tf_op jit(solution)/shard_map/ppermute | solution.py:323
  58.3 2.4 %beams_1.1 = bf16[272,768]{1,0:T(8,128)(2,1)S(1)} custom-call(bf16[4,8,256,512]{3,2,1,0:T(8,128)(2,1)S(1)} %get-tuple-element.45.refs_0_, bf16[4,8,256,512]{3,2,1,0:T(8,128)(2,1)S(1)} %get-tuple-element.46.refs_1_, bf16[4,8,256,512]{3,2,1,0:T(8,128)(2,1)S(1)} %get-tuple-element.47.refs_2_, bf16[4,8,256,512]{3,2,1,0:T(8,128)(2,1)S(1)} %get-tuple-element.49.refs_3_, ...), custom_call_target="tpu_custom_call" | custom-call | flops 3000000000 | bytes 1000000 | tf_op jit(solution)/shard_map/beams_1/pallas_call | solution.py:165
  60.7 2.4 %beams_2.1 = bf16[272,768]{1,0:T(8,128)(2,1)S(1)} custom-call(bf16[4,8,256,512]{3,2,1,0:T(8,128)(2,1)S(1)} %get-tuple-element.45.refs_0_, bf16[4,8,256,512]{3,2,1,0:T(8,128)(2,1)S(1)} %get-tuple-element.46.refs_1_, bf16[4,8,256,512]{3,2,1,0:T(8,128)(2,1)S(1)} %get-tuple-element.47.refs_2_, bf16[4,8,256,512]{3,2,1,0:T(8,128)(2,1)S(1)} %get-tuple-element.49.refs_3_, ...), custom_call_target="tpu_custom_call" | custom-call | flops 3000000000 | bytes 1000000 | tf_op jit(solution)/shard_map/beams_2/pallas_call | solution.py:165
  63.4 2.4 %collective-permute-start.13 = (bf16[272,768]{1,0:T(8,128)(2,1)S(1)}, bf16[272,768]{1,0:T(8,128)(2,1)S(1)}, u32[]{:S(2)}, u32[]{:S(2)}) collective-permute-start(bf16[272,768]{1,0:T(8,128)(2,1)S(1)} %beams_2.1), channel_id=1, source_target_pairs={{0,12},{4,0},{8,4},{12,8},{1,13},{5,1},{9,5},{13,9},{2,14},{6,2},{... | collective-permute-start | bytes 1253384 | tf_op jit(solution)/shard_map/ppermute | solution.py:323
  65.8 2.5 %collective-permute-done.11.refs_0_ = bf16[272,768]{1,0:T(8,128)(2,1)S(1)} collective-permute-done((bf16[272,768]{1,0:T(8,128)(2,1)S(1)}, bf16[272,768]{1,0:T(8,128)(2,1)S(1)}, u32[]{:S(2)}, u32[]{:S(2)}) %collective-permute-start.11) | collective-permute-done | bytes 417824 | tf_op jit(solution)/shard_map/ppermute | solution.py:323
  68.3 2.4 %beams_3.1.refs_3_ = f32[256,768]{1,0:T(8,128)S(1)} custom-call(bf16[4,8,256,512]{3,2,1,0:T(8,128)(2,1)S(1)} %get-tuple-element.45.refs_0_, bf16[4,8,256,512]{3,2,1,0:T(8,128)(2,1)S(1)} %get-tuple-element.46.refs_1_, bf16[4,8,256,512]{3,2,1,0:T(8,128)(2,1)S(1)} %get-tuple-element.47.refs_2_, bf16[4,8,256,512]{3,2,1,0:T(8,128)(2,1)S(1)} %get-tuple-element.49.refs_3_, ...), custom_call_target="tpu_custom_call" | custom-call | flops 3000000000 | bytes 1000000 | tf_op jit(solution)/shard_map/beams_3/pallas_call | solution.py:165
  70.7 6.9 %collective-permute-done.12.refs_1_ = bf16[272,768]{1,0:T(8,128)(2,1)S(1)} collective-permute-done((bf16[272,768]{1,0:T(8,128)(2,1)S(1)}, bf16[272,768]{1,0:T(8,128)(2,1)S(1)}, u32[]{:S(2)}, u32[]{:S(2)}) %collective-permute-start.12) | collective-permute-done | bytes 417824 | tf_op jit(solution)/shard_map/ppermute | solution.py:323
  77.6 1.9 %finish.1 = f32[48,256]{1,0:T(8,128)} custom-call(s32[6]{0:T(128)S(1)} %stack.27.place, bf16[272,768]{1,0:T(8,128)(2,1)S(1)} %collective-permute-done.11.refs_0_, bf16[272,768]{1,0:T(8,128)(2,1)S(1)} %collective-permute-done.12.refs_1_, bf16[272,768]{1,0:T(8,128)(2,1)S(1)} %collective-permute-done.13.refs_2_, f32[256,768]{1,0:T(8,128)S(1)} %beams_3.1.refs_3_, ...), custom_call_target="tpu_custom_call" | custom-call | tf_op jit(solution)/shard_map/finish/pallas_call | solution.py:255
  (29 shorter events, 4.3 us)
Async XLA Ops:
  1.5 6.4 %collective-permute-start = (bf16[1,48,256]{2,1,0:T(8,128)(2,1)S(1)}, bf16[1,48,256]{2,1,0:T(8,128)(2,1)S(1)}, u32[]{:S(2)}, u32[]{:S(2)}) collective-permute-start(bf16[1,48,256]{2,1,0:T(8,128)(2,1)S(1)} %reshape.16.refs_0_), channel_id=1, source_target_pairs={{0,2},{2,0},{1,3},{3,1},{4,6},{6,4},{5,7},{7,5},{8,10},{10,8},{9,1... | collective-permute-start | bytes 73736 | tf_op jit(solution)/shard_map/ppermute | solution.py:295
  7.8 10.2 %collective-permute-start.1 = (bf16[2,48,256]{2,1,0:T(8,128)(2,1)S(1)}, bf16[2,48,256]{2,1,0:T(8,128)(2,1)S(1)}, u32[]{:S(2)}, u32[]{:S(2)}) collective-permute-start(bf16[2,48,256]{2,1,0:T(8,128)(2,1)S(1)} %join_1.1.after_ref.refs_0_), channel_id=1, source_target_pairs={{0,16},{16,0},{1,17},{17,1},{2,18},{18,2},{3,19},{19,3},{4,20},{20... | collective-permute-start | bytes 147464 | tf_op jit(solution)/shard_map/ppermute | solution.py:299
  8.3 16.4 %collective-permute-start.3 = (s16[4,256,256]{2,1,0:T(8,128)(2,1)S(1)}, s16[4,256,256]{2,1,0:T(8,128)(2,1)S(1)}, u32[]{:S(2)}, u32[]{:S(2)}) collective-permute-start(s16[4,256,256]{2,1,0:T(8,128)(2,1)S(1)} %get-tuple-element.40), channel_id=1, source_target_pairs={{0,1},{1,0},{2,3},{3,2},{4,5},{5,4},{6,7},{7,6},{8,9},{9,8},{10,11... | collective-permute-start | bytes 1572872 | tf_op jit(solution)/shard_map/ppermute | solution.py:289
  10.2 22.8 %collective-permute-start.7 = (s16[4,256,256]{2,1,0:T(8,128)(2,1)S(1)}, s16[4,256,256]{2,1,0:T(8,128)(2,1)S(1)}, u32[]{:S(2)}, u32[]{:S(2)}) collective-permute-start(s16[4,256,256]{2,1,0:T(8,128)(2,1)S(1)} %get-tuple-element.42), channel_id=1, source_target_pairs={{0,2},{1,3},{2,0},{3,1},{4,6},{5,7},{6,4},{7,5},{8,10},{9,11},{10,... | collective-permute-start | bytes 1572872 | tf_op jit(solution)/shard_map/ppermute | solution.py:289
  12.6 33.3 %collective-permute-start.8 = (s16[4,256,256]{2,1,0:T(8,128)(2,1)S(1)}, s16[4,256,256]{2,1,0:T(8,128)(2,1)S(1)}, u32[]{:S(2)}, u32[]{:S(2)}) collective-permute-start(s16[4,256,256]{2,1,0:T(8,128)(2,1)S(1)} %get-tuple-element.48), channel_id=1, source_target_pairs={{0,3},{1,2},{2,1},{3,0},{4,7},{5,6},{6,5},{7,4},{8,11},{9,10},{10,... | collective-permute-start | bytes 1572872 | tf_op jit(solution)/shard_map/ppermute | solution.py:289
  18.0 11.2 %collective-permute-start.2 = (bf16[4,48,256]{2,1,0:T(8,128)(2,1)S(1)}, bf16[4,48,256]{2,1,0:T(8,128)(2,1)S(1)}, u32[]{:S(2)}, u32[]{:S(2)}) collective-permute-start(bf16[4,48,256]{2,1,0:T(8,128)(2,1)S(1)} %join_2.1.after_ref.refs_0_), channel_id=1, source_target_pairs={{0,128},{32,160},{64,192},{96,224},{128,0},{160,32},{192,64},{224,... | collective-permute-start | bytes 294920 | tf_op jit(solution)/shard_map/ppermute | solution.py:292
  29.2 9.8 %collective-permute-start.4 = (bf16[8,48,256]{2,1,0:T(8,128)(2,1)S(1)}, bf16[8,48,256]{2,1,0:T(8,128)(2,1)S(1)}, u32[]{:S(2)}, u32[]{:S(2)}) collective-permute-start(bf16[8,48,256]{2,1,0:T(8,128)(2,1)S(1)} %join_4.1.after_ref.low_ref), channel_id=1, source_target_pairs={{0,224},{32,0},{64,32},{96,64},{128,96},{160,128},{192,160},{224,1... | collective-permute-start | bytes 589832 | tf_op jit(solution)/shard_map/ppermute | solution.py:292
  33.0 7.5 %collective-permute-start.5 = (bf16[8,48,256]{2,1,0:T(8,128)(2,1)S(1)}, bf16[8,48,256]{2,1,0:T(8,128)(2,1)S(1)}, u32[]{:S(2)}, u32[]{:S(2)}) collective-permute-start(bf16[8,48,256]{2,1,0:T(8,128)(2,1)S(1)} %join_4.1.after_ref.low_ref), channel_id=1, source_target_pairs={{0,32},{32,64},{64,96},{96,128},{128,160},{160,192},{192,224},{224... | collective-permute-start | bytes 589832 | tf_op jit(solution)/shard_map/ppermute | solution.py:292
  33.0 10.3 %collective-permute-start.6 = (bf16[8,48,256]{2,1,0:T(8,128)(2,1)S(1)}, bf16[8,48,256]{2,1,0:T(8,128)(2,1)S(1)}, u32[]{:S(2)}, u32[]{:S(2)}) collective-permute-start(bf16[8,48,256]{2,1,0:T(8,128)(2,1)S(1)} %join_4.1.after_ref.low_ref), channel_id=1, source_target_pairs={{0,64},{32,224},{64,128},{96,32},{128,192},{160,96},{192,0},{224,1... | collective-permute-start | bytes 589832 | tf_op jit(solution)/shard_map/ppermute | solution.py:292
  33.0 18.9 %collective-permute-start.9 = (bf16[8,48,256]{2,1,0:T(8,128)(2,1)S(1)}, bf16[8,48,256]{2,1,0:T(8,128)(2,1)S(1)}, u32[]{:S(2)}, u32[]{:S(2)}) collective-permute-start(bf16[8,48,256]{2,1,0:T(8,128)(2,1)S(1)} %join_4.1.after_ref.low_ref), channel_id=1, source_target_pairs={{0,1},{1,0},{2,3},{3,2},{4,5},{5,4},{6,7},{7,6},{8,9},{9,8},{10,11... | collective-permute-start | bytes 589832 | tf_op jit(solution)/shard_map/ppermute | solution.py:308
  43.3 8.6 %collective-permute-start.10 = (bf16[24,48,256]{2,1,0:T(8,128)(2,1)S(1)}, bf16[24,48,256]{2,1,0:T(8,128)(2,1)S(1)}, u32[]{:S(2)}, u32[]{:S(2)}) collective-permute-start(bf16[24,48,256]{2,1,0:T(8,128)(2,1)S(1)} %join_8.1.high_ref.after_ref), channel_id=1, source_target_pairs={{0,1},{1,0},{2,3},{3,2},{4,5},{5,4},{6,7},{7,6},{8,9},{9,8},{10,11... | collective-permute-start | bytes 1769480 | tf_op jit(solution)/shard_map/ppermute | solution.py:311
  55.3 13.0 %collective-permute-start.11 = (bf16[272,768]{1,0:T(8,128)(2,1)S(1)}, bf16[272,768]{1,0:T(8,128)(2,1)S(1)}, u32[]{:S(2)}, u32[]{:S(2)}) collective-permute-start(bf16[272,768]{1,0:T(8,128)(2,1)S(1)} %beams_0.1), channel_id=1, source_target_pairs={{0,8},{4,12},{8,0},{12,4},{1,9},{5,13},{9,1},{13,5},{2,10},{6,14},... | collective-permute-start | bytes 1253384 | tf_op jit(solution)/shard_map/ppermute | solution.py:323
  63.0 14.5 %copy-start = (s32[4,768]{1,0:T(4,128)S(1)}, s32[4,768]{1,0:T(4,128)}, u32[]{:S(2)}) copy-start(s32[4,768]{1,0:T(4,128)} %constant.54.clone.refs_8_) | copy-start | bytes 36868
  63.1 14.5 %collective-permute-start.12 = (bf16[272,768]{1,0:T(8,128)(2,1)S(1)}, bf16[272,768]{1,0:T(8,128)(2,1)S(1)}, u32[]{:S(2)}, u32[]{:S(2)}) collective-permute-start(bf16[272,768]{1,0:T(8,128)(2,1)S(1)} %beams_1.1), channel_id=1, source_target_pairs={{0,4},{4,8},{8,12},{12,0},{1,5},{5,9},{9,13},{13,1},{2,6},{6,10},{... | collective-permute-start | bytes 1253384 | tf_op jit(solution)/shard_map/ppermute | solution.py:323
  63.4 14.1 %collective-permute-start.13 = (bf16[272,768]{1,0:T(8,128)(2,1)S(1)}, bf16[272,768]{1,0:T(8,128)(2,1)S(1)}, u32[]{:S(2)}, u32[]{:S(2)}) collective-permute-start(bf16[272,768]{1,0:T(8,128)(2,1)S(1)} %beams_2.1), channel_id=1, source_target_pairs={{0,12},{4,0},{8,4},{12,8},{1,13},{5,1},{9,5},{13,9},{2,14},{6,2},{... | collective-permute-start | bytes 1253384 | tf_op jit(solution)/shard_map/ppermute | solution.py:323

commit v8 on v7

--- a/solution.py
+++ b/solution.py
@@ -22,16 +22,8 @@
 NORM_ROWS = 16
 
 
-def series_coefficients():
-    nodes = np.cos(np.linspace(0, np.pi, 4002)) / 8
-    squares = nodes**2
-    angles = 2 * np.pi * nodes
-    sine = np.linalg.lstsq(squares[:, None] ** np.arange(4), np.sin(angles) / nodes, rcond=None)[0]
-    cosine = np.linalg.lstsq(squares[:, None] ** np.arange(5), np.cos(angles), rcond=None)[0]
-    return [np.float32(v) for v in sine], [np.float32(v) for v in cosine]
-
-
-SINE, COSINE = series_coefficients()
+SINE = [np.float32(1.570796305), np.float32(-0.6459629382), np.float32(0.07967590293), np.float32(-0.004592288967)]
+COSINE = [np.float32(0.9999999724), np.float32(-1.233697014), np.float32(0.2535986436), np.float32(-0.02040835128)]
 
 
 def horner(coefficients, value):
@@ -45,9 +37,8 @@
     turns = turns_times * np.float32(multiple / NFFT)
     magic = np.float32(1.5 * 2**23)
     part = turns - ((turns + magic) - magic)
-    quarter = part * np.float32(0.25)
-    square = quarter * quarter
-    sine = quarter * horner(SINE, square)
+    square = part * part
+    sine = part * horner(SINE, square)
     cosine = horner(COSINE, square)
     for _ in range(2):
         twice = sine + sine
@@ -76,12 +67,16 @@
     return lax.dot_general(left, right, BY_COLUMNS, preferred_element_type=f32)
 
 
+def eight_bits(values):
+    scaled = values * np.float32(65537.0)
+    return scaled - (scaled - values)
+
+
 def thirds(values):
-    high = values.astype(bf16)
-    rest = values - high.astype(f32)
-    middle = rest.astype(bf16)
-    low = (rest - middle.astype(f32)).astype(bf16)
-    return high, middle, low
+    high = eight_bits(values)
+    rest = values - high
+    middle = eight_bits(rest)
+    return high.astype(bf16), middle.astype(bf16), (rest - middle).astype(bf16)
 
 
 def exact_product(ones, values):
@@ -173,9 +168,9 @@
     )(*reps, *weights, *norms)
 
 
-def prepare_kernel(low_ref, high_ref, w_ref, norm_ref, wide, *, flip, first_row):
+def prepare_kernel(source_ref, w_ref, norm_ref, wide, *, flip, first_row):
     for g in range(16):
-        source_ref, class_row = (low_ref, 0) if g < 4 else (high_ref, 8 * (g // 4 - 1))
+        class_row = 8 * (g // 4)
         for half in range(CH // 128):
             lanes = slice(half * 128, (half + 1) * 128)
             wide[half, g * 48 : (g + 1) * 48, :] = source_ref[class_row + 2 * (g % 4) + flip, :, lanes].astype(f32)
@@ -210,10 +205,10 @@
     norm_ref[...] = jnp.concatenate([split] + [zero] * (NF - 1), axis=1).astype(bf16)
 
 
-def prepare(low, high, flip, first_row):
+def prepare(source, flip, first_row):
     return pl.pallas_call(
         functools.partial(prepare_kernel, flip=flip, first_row=first_row),
-        in_specs=[VMEM] * 2,
+        in_specs=[VMEM],
         out_specs=[VMEM, VMEM],
         scratch_shapes=[pltpu.VMEM((CH // 128, 768, 128), f32)],
         out_shape=[
@@ -223,7 +218,7 @@
         cost_estimate=pl.CostEstimate(flops=1_000_000_000, bytes_accessed=1_000_000, transcendentals=0),
         compiler_params=pltpu.CompilerParams(vmem_limit_bytes=6 << 20),
         name=f"prepare_{first_row}",
-    )(low, high)
+    )(source)
 
 
 def column_tables():
@@ -305,12 +300,11 @@
     two_away = along_z(held, lambda i: i - 2 if i % 2 else i + 2)
     above = along_z(held, lambda i: i - 1)
     below = along_z(held, lambda i: i + 1)
-    held_swapped = lax.ppermute(held, "c", SWAP)
     rep_far, token = replicas(place, far, held, "far")
-    other = join(token, above, below, two_away)
-    other_swapped = lax.ppermute(other, "c", SWAP)
-    rep_both, _ = replicas(place, both, other, "both")
-    halves = ((held, other, 0), (held_swapped, other_swapped, 0), (held, other, 1), (held_swapped, other_swapped, 1))
+    held = join(token, held, above, below, two_away)
+    swapped = lax.ppermute(held, "c", SWAP)
+    rep_both, _ = replicas(place, both, held, "both")
+    halves = ((held, 0), (swapped, 0), (held, 1), (swapped, 1))
     prepared = [prepare(*half, 4 * index) for index, half in enumerate(halves)]
     weights, norms = [w for w, _ in prepared], [n for _, n in prepared]
     reps = (rep_own, rep_near, rep_far, rep_both)

time: 79.6 us -> 79.3 us (level)
  waiting for transfers between devices: 13.6 us -> 15.3 us
  starting transfers between devices: 29.7 us -> 28.4 us
  Pallas kernels: 32 us -> 31.2 us
    ppermute x4, waiting for transfers between devices: 4.2 us -> 5.93 us  [along_z(): return lax.ppermute(values, 'z', [(i, target(i) % 8) for i in range(8)])]
    ppermute x2 -> x1, starting transfers between devices: 4.08 us -> 2.57 us  [per_device(): swapped = lax.ppermute(held, 'c', SWAP)]
    pallas_call x4, Pallas kernels: 18.7 us -> 17.8 us  [replicas(): pl.pallas_call(replicas_kernel, grid_spec=pltpu.PrefetchScalarGridSpec(nu...]
  transfers between devices with their start and end apart: 14 -> 13, of which waited for: 4 -> 4; matrix products, arithmetic and copies ran while one was open for 3% -> 3% of each run, Pallas kernels for 34% -> 33%
where the time goes in v8:
time: 79.3 us; the launch traced here: 79.2 us
  Pallas kernels  31.2 us (39%)
  starting transfers between devices  28.4 us (36%)
  waiting for transfers between devices  15.3 us (19%)
  other arithmetic  3.82 us (5%)
    pallas_call x4, Pallas kernels, replicas(): pl.pallas_call(replicas_kernel, grid_spec=pltpu.PrefetchScalarGridSpec(nu...  17.8 us
    ppermute x4, starting transfers between devices, along_z(): return lax.ppermute(values, 'z', [(i, target(i) % 8) for i in range(8)])  10.6 us
    pallas_call x4, Pallas kernels, beams_block(): pl.pallas_call(functools.partial(beams_kernel, slot=step), in_specs=[VMEM...  9.56 us
    ppermute x3, waiting for transfers between devices, per_device(): lax.ppermute(beams, 'x', [(i, (i + dx) % 4) for i in range(4)])  9.37 us
    ppermute x4, waiting for transfers between devices, along_z(): return lax.ppermute(values, 'z', [(i, target(i) % 8) for i in range(8)])  5.93 us
    ppermute x3, starting transfers between devices, per_device(): lax.ppermute(beams, 'x', [(i, (i + dx) % 4) for i in range(4)])  5.76 us
    ppermute x3, starting transfers between devices, moved(): lax.ppermute(parts[flip], ('yh', 'c'), [(i, i ^ flip) for i in range(4)])  5.14 us
    ppermute x1, starting transfers between devices, per_device(): other = lax.ppermute(held, 'yh', SWAP)  3.83 us
  transfers between devices with their start and end apart: 13, of which 4 were waited for; matrix products, arithmetic and copies ran while one was open for 3% of the time, Pallas kernels for 33%

profile of v8, /device:TPU:1, one launch (start us, length us, event | category | flops | bytes accessed | tf_op | source)
XLA Modules:
  0.0 79.2 jit_solution(18273041581683063358)
XLA Ops:
  0.7 0.7 broadcast_multiply_fusion
  1.5 3.8 %collective-permute-start = (bf16[1,48,256]{2,1,0:T(8,128)(2,1)S(1)}, bf16[1,48,256]{2,1,0:T(8,128)(2,1)S(1)}, u32[]{:S(2)}, u32[]{:S(2)}) collective-permute-start(bf16[1,48,256]{2,1,0:T(8,128)(2,1)S(1)} %reshape.16.refs_0_), channel_id=1, source_target_pairs={{0,2},{2,0},{1,3},{3,1},{4,6},{6,4},{5,7},{7,5},{8,10},{10,8},{9,1... | collective-permute-start | bytes 73736 | tf_op jit(solution)/shard_map/ppermute | solution.py:290
  5.3 2.4 %fusion.3 = (s16[4,256,256]{2,1,0:T(8,128)(2,1)S(1)}, s16[4,256,256]{2,1,0:T(8,128)(2,1)S(1)}, s16[4,256,256]{2,1,0:T(8,128)(2,1)S(1)}, s16[4,256,256]{2,1,0:T(8,128)(2,1)S(1)}) fusion(s32[4,2,2,256,256]{4,3,2,1,0:T(8,128)} %bitcast.31, s32[]{:T(128)S(6)} %select_n.42, s32[]{:T(128)S(6)} %select_n.41, s32[]{:T(128)S(6)} %select_n.40, s32[]{:T(128)S(6)} %select_n.39), kind=kLoop, calls=%fused_computation.7 | loop fusion | flops 1048576 | bytes 6291472 | tf_op jit(solution)/shard_map/convert_element_type | solution.py:277
  8.3 1.9 %collective-permute-start.3 = (s16[4,256,256]{2,1,0:T(8,128)(2,1)S(1)}, s16[4,256,256]{2,1,0:T(8,128)(2,1)S(1)}, u32[]{:S(2)}, u32[]{:S(2)}) collective-permute-start(s16[4,256,256]{2,1,0:T(8,128)(2,1)S(1)} %get-tuple-element.40), channel_id=1, source_target_pairs={{0,1},{1,0},{2,3},{3,2},{4,5},{5,4},{6,7},{7,6},{8,9},{9,8},{10,11... | collective-permute-start | bytes 1572872 | tf_op jit(solution)/shard_map/ppermute | solution.py:284
  10.2 2.4 %collective-permute-start.7 = (s16[4,256,256]{2,1,0:T(8,128)(2,1)S(1)}, s16[4,256,256]{2,1,0:T(8,128)(2,1)S(1)}, u32[]{:S(2)}, u32[]{:S(2)}) collective-permute-start(s16[4,256,256]{2,1,0:T(8,128)(2,1)S(1)} %get-tuple-element.42), channel_id=1, source_target_pairs={{0,2},{1,3},{2,0},{3,1},{4,6},{5,7},{6,4},{7,5},{8,10},{9,11},{10,... | collective-permute-start | bytes 1572872 | tf_op jit(solution)/shard_map/ppermute | solution.py:284
  12.6 0.9 %collective-permute-start.8 = (s16[4,256,256]{2,1,0:T(8,128)(2,1)S(1)}, s16[4,256,256]{2,1,0:T(8,128)(2,1)S(1)}, u32[]{:S(2)}, u32[]{:S(2)}) collective-permute-start(s16[4,256,256]{2,1,0:T(8,128)(2,1)S(1)} %get-tuple-element.48), channel_id=1, source_target_pairs={{0,3},{1,2},{2,1},{3,0},{4,7},{5,6},{6,5},{7,4},{8,11},{9,10},{10,... | collective-permute-start | bytes 1572872 | tf_op jit(solution)/shard_map/ppermute | solution.py:284
  13.5 4.3 %replicas_own.1 = (bf16[4,8,256,512]{3,2,1,0:T(8,128)(2,1)S(1)}, s32[8,128]{1,0:T(8,128)S(1)}) custom-call(s32[6]{0:T(128)S(1)} %stack.27.place, s16[4,256,256]{2,1,0:T(8,128)(2,1)S(1)} %get-tuple-element.38.travel_ref, bf16[2,48,256]{2,1,0:T(8,128)(2,1)S(1)} %join_1.1.after_ref.refs_0_), custom_call_target="tpu_custom_call" | custom-call | flops 40000000000 | bytes 1000000 | tf_op jit(solution)/shard_map/replicas_own/pallas_call | solution.py:108
  17.8 6.6 %collective-permute-start.2 = (bf16[4,48,256]{2,1,0:T(8,128)(2,1)S(1)}, bf16[4,48,256]{2,1,0:T(8,128)(2,1)S(1)}, u32[]{:S(2)}, u32[]{:S(2)}) collective-permute-start(bf16[4,48,256]{2,1,0:T(8,128)(2,1)S(1)} %join_2.1.after_ref.refs_0_), channel_id=1, source_target_pairs={{0,128},{32,160},{64,192},{96,224},{128,0},{160,32},{192,64},{224,... | collective-permute-start | bytes 294920 | tf_op jit(solution)/shard_map/ppermute | solution.py:287
  24.5 4.3 %replicas_near.1 = (bf16[4,8,256,512]{3,2,1,0:T(8,128)(2,1)S(1)}, s32[8,128]{1,0:T(8,128)S(1)}) custom-call(s32[6]{0:T(128)S(1)} %stack.27.place, s16[4,256,256]{2,1,0:T(8,128)(2,1)S(1)} %collective-permute-done.3.travel_ref, bf16[4,48,256]{2,1,0:T(8,128)(2,1)S(1)} %join_2.1.after_ref.refs_0_), custom_call_target="tpu_custom_call" | custom-call | flops 40000000000 | bytes 1000000 | tf_op jit(solution)/shard_map/replicas_near/pallas_call | solution.py:108
  28.8 4.0 %collective-permute-start.4 = (bf16[8,48,256]{2,1,0:T(8,128)(2,1)S(1)}, bf16[8,48,256]{2,1,0:T(8,128)(2,1)S(1)}, u32[]{:S(2)}, u32[]{:S(2)}) collective-permute-start(bf16[8,48,256]{2,1,0:T(8,128)(2,1)S(1)} %join_4.1.after_ref.refs_0_), channel_id=1, source_target_pairs={{0,224},{32,0},{64,32},{96,64},{128,96},{160,128},{192,160},{224,1... | collective-permute-start | bytes 589832 | tf_op jit(solution)/shard_map/ppermute | solution.py:287
  32.8 4.3 %replicas_far.1 = (bf16[4,8,256,512]{3,2,1,0:T(8,128)(2,1)S(1)}, s32[8,128]{1,0:T(8,128)S(1)}) custom-call(s32[6]{0:T(128)S(1)} %stack.27.place, s16[4,256,256]{2,1,0:T(8,128)(2,1)S(1)} %collective-permute-done.7.travel_ref, bf16[8,48,256]{2,1,0:T(8,128)(2,1)S(1)} %join_4.1.after_ref.refs_0_), custom_call_target="tpu_custom_call" | custom-call | flops 40000000000 | bytes 1000000 | tf_op jit(solution)/shard_map/replicas_far/pallas_call | solution.py:108
  37.1 3.2 %collective-permute-done.5.refs_2_ = bf16[8,48,256]{2,1,0:T(8,128)(2,1)S(1)} collective-permute-done((bf16[8,48,256]{2,1,0:T(8,128)(2,1)S(1)}, bf16[8,48,256]{2,1,0:T(8,128)(2,1)S(1)}, u32[]{:S(2)}, u32[]{:S(2)}) %collective-permute-start.5) | collective-permute-done | bytes 196640 | tf_op jit(solution)/shard_map/ppermute | solution.py:287
  40.3 2.7 %collective-permute-done.6.refs_3_ = bf16[8,48,256]{2,1,0:T(8,128)(2,1)S(1)} collective-permute-done((bf16[8,48,256]{2,1,0:T(8,128)(2,1)S(1)}, bf16[8,48,256]{2,1,0:T(8,128)(2,1)S(1)}, u32[]{:S(2)}, u32[]{:S(2)}) %collective-permute-start.6) | collective-permute-done | bytes 196640 | tf_op jit(solution)/shard_map/ppermute | solution.py:287
  43.1 2.6 %collective-permute-start.9 = (bf16[32,48,256]{2,1,0:T(8,128)(2,1)S(1)}, bf16[32,48,256]{2,1,0:T(8,128)(2,1)S(1)}, u32[]{:S(2)}, u32[]{:S(2)}) collective-permute-start(bf16[32,48,256]{2,1,0:T(8,128)(2,1)S(1)} %join_8.1.source_ref.after_ref), channel_id=1, source_target_pairs={{0,1},{1,0},{2,3},{3,2},{4,5},{5,4},{6,7},{7,6},{8,9},{9,8},{10,11... | collective-permute-start | bytes 2359304 | tf_op jit(solution)/shard_map/ppermute | solution.py:305
  45.7 4.9 %replicas_both.1 = (bf16[4,8,256,512]{3,2,1,0:T(8,128)(2,1)S(1)}, s32[8,128]{1,0:T(8,128)}) custom-call(s32[6]{0:T(128)S(1)} %stack.27.place, s16[4,256,256]{2,1,0:T(8,128)(2,1)S(1)} %collective-permute-done.8.travel_ref, bf16[32,48,256]{2,1,0:T(8,128)(2,1)S(1)} %join_8.1.source_ref.after_ref), custom_call_target="tpu_custom_call" | custom-call | flops 40000000000 | bytes 1000000 | tf_op jit(solution)/shard_map/replicas_both/pallas_call | solution.py:108
  52.5 2.4 %beams_0.1 = bf16[272,768]{1,0:T(8,128)(2,1)S(1)} custom-call(bf16[4,8,256,512]{3,2,1,0:T(8,128)(2,1)S(1)} %get-tuple-element.45.refs_0_, bf16[4,8,256,512]{3,2,1,0:T(8,128)(2,1)S(1)} %get-tuple-element.46.refs_1_, bf16[4,8,256,512]{3,2,1,0:T(8,128)(2,1)S(1)} %get-tuple-element.47.refs_2_, bf16[4,8,256,512]{3,2,1,0:T(8,128)(2,1)S(1)} %get-tuple-element.49.refs_3_, ...), custom_call_target="tpu_custom_call" | custom-call | flops 3000000000 | bytes 1000000 | tf_op jit(solution)/shard_map/beams_0/pallas_call | solution.py:160
  54.9 3.0 %collective-permute-start.10 = (bf16[272,768]{1,0:T(8,128)(2,1)S(1)}, bf16[272,768]{1,0:T(8,128)(2,1)S(1)}, u32[]{:S(2)}, u32[]{:S(2)}) collective-permute-start(bf16[272,768]{1,0:T(8,128)(2,1)S(1)} %beams_0.1), channel_id=1, source_target_pairs={{0,8},{4,12},{8,0},{12,4},{1,9},{5,13},{9,1},{13,5},{2,10},{6,14},... | collective-permute-start | bytes 1253384 | tf_op jit(solution)/shard_map/ppermute | solution.py:317
  57.9 2.4 %beams_1.1 = bf16[272,768]{1,0:T(8,128)(2,1)S(1)} custom-call(bf16[4,8,256,512]{3,2,1,0:T(8,128)(2,1)S(1)} %get-tuple-element.45.refs_0_, bf16[4,8,256,512]{3,2,1,0:T(8,128)(2,1)S(1)} %get-tuple-element.46.refs_1_, bf16[4,8,256,512]{3,2,1,0:T(8,128)(2,1)S(1)} %get-tuple-element.47.refs_2_, bf16[4,8,256,512]{3,2,1,0:T(8,128)(2,1)S(1)} %get-tuple-element.49.refs_3_, ...), custom_call_target="tpu_custom_call" | custom-call | flops 3000000000 | bytes 1000000 | tf_op jit(solution)/shard_map/beams_1/pallas_call | solution.py:160
  60.3 2.4 %beams_2.1 = bf16[272,768]{1,0:T(8,128)(2,1)S(1)} custom-call(bf16[4,8,256,512]{3,2,1,0:T(8,128)(2,1)S(1)} %get-tuple-element.45.refs_0_, bf16[4,8,256,512]{3,2,1,0:T(8,128)(2,1)S(1)} %get-tuple-element.46.refs_1_, bf16[4,8,256,512]{3,2,1,0:T(8,128)(2,1)S(1)} %get-tuple-element.47.refs_2_, bf16[4,8,256,512]{3,2,1,0:T(8,128)(2,1)S(1)} %get-tuple-element.49.refs_3_, ...), custom_call_target="tpu_custom_call" | custom-call | flops 3000000000 | bytes 1000000 | tf_op jit(solution)/shard_map/beams_2/pallas_call | solution.py:160
  63.1 2.4 %collective-permute-start.12 = (bf16[272,768]{1,0:T(8,128)(2,1)S(1)}, bf16[272,768]{1,0:T(8,128)(2,1)S(1)}, u32[]{:S(2)}, u32[]{:S(2)}) collective-permute-start(bf16[272,768]{1,0:T(8,128)(2,1)S(1)} %beams_2.1), channel_id=1, source_target_pairs={{0,12},{4,0},{8,4},{12,8},{1,13},{5,1},{9,5},{13,9},{2,14},{6,2},{... | collective-permute-start | bytes 1253384 | tf_op jit(solution)/shard_map/ppermute | solution.py:317
  65.4 2.5 %collective-permute-done.10.refs_0_ = bf16[272,768]{1,0:T(8,128)(2,1)S(1)} collective-permute-done((bf16[272,768]{1,0:T(8,128)(2,1)S(1)}, bf16[272,768]{1,0:T(8,128)(2,1)S(1)}, u32[]{:S(2)}, u32[]{:S(2)}) %collective-permute-start.10) | collective-permute-done | bytes 417824 | tf_op jit(solution)/shard_map/ppermute | solution.py:317
  67.9 2.4 %beams_3.1.refs_3_ = f32[256,768]{1,0:T(8,128)S(1)} custom-call(bf16[4,8,256,512]{3,2,1,0:T(8,128)(2,1)S(1)} %get-tuple-element.45.refs_0_, bf16[4,8,256,512]{3,2,1,0:T(8,128)(2,1)S(1)} %get-tuple-element.46.refs_1_, bf16[4,8,256,512]{3,2,1,0:T(8,128)(2,1)S(1)} %get-tuple-element.47.refs_2_, bf16[4,8,256,512]{3,2,1,0:T(8,128)(2,1)S(1)} %get-tuple-element.49.refs_3_, ...), custom_call_target="tpu_custom_call" | custom-call | flops 3000000000 | bytes 1000000 | tf_op jit(solution)/shard_map/beams_3/pallas_call | solution.py:160
  70.3 6.9 %collective-permute-done.11.refs_1_ = bf16[272,768]{1,0:T(8,128)(2,1)S(1)} collective-permute-done((bf16[272,768]{1,0:T(8,128)(2,1)S(1)}, bf16[272,768]{1,0:T(8,128)(2,1)S(1)}, u32[]{:S(2)}, u32[]{:S(2)}) %collective-permute-start.11) | collective-permute-done | bytes 417824 | tf_op jit(solution)/shard_map/ppermute | solution.py:317
  77.2 2.0 %finish.1 = f32[48,256]{1,0:T(8,128)} custom-call(s32[6]{0:T(128)S(1)} %stack.27.place, bf16[272,768]{1,0:T(8,128)(2,1)S(1)} %collective-permute-done.10.refs_0_, bf16[272,768]{1,0:T(8,128)(2,1)S(1)} %collective-permute-done.11.refs_1_, bf16[272,768]{1,0:T(8,128)(2,1)S(1)} %collective-permute-done.12.refs_2_, f32[256,768]{1,0:T(8,128)S(1)} %beams_3.1.refs_3_, ...), custom_call_target="tpu_custom_call" | custom-call | tf_op jit(solution)/shard_map/finish/pallas_call | solution.py:250
  (27 shorter events, 3.6 us)
Async XLA Ops:
  1.5 6.4 %collective-permute-start = (bf16[1,48,256]{2,1,0:T(8,128)(2,1)S(1)}, bf16[1,48,256]{2,1,0:T(8,128)(2,1)S(1)}, u32[]{:S(2)}, u32[]{:S(2)}) collective-permute-start(bf16[1,48,256]{2,1,0:T(8,128)(2,1)S(1)} %reshape.16.refs_0_), channel_id=1, source_target_pairs={{0,2},{2,0},{1,3},{3,1},{4,6},{6,4},{5,7},{7,5},{8,10},{10,8},{9,1... | collective-permute-start | bytes 73736 | tf_op jit(solution)/shard_map/ppermute | solution.py:290
  7.8 9.9 %collective-permute-start.1 = (bf16[2,48,256]{2,1,0:T(8,128)(2,1)S(1)}, bf16[2,48,256]{2,1,0:T(8,128)(2,1)S(1)}, u32[]{:S(2)}, u32[]{:S(2)}) collective-permute-start(bf16[2,48,256]{2,1,0:T(8,128)(2,1)S(1)} %join_1.1.after_ref.refs_0_), channel_id=1, source_target_pairs={{0,16},{16,0},{1,17},{17,1},{2,18},{18,2},{3,19},{19,3},{4,20},{20... | collective-permute-start | bytes 147464 | tf_op jit(solution)/shard_map/ppermute | solution.py:294
  8.3 16.1 %collective-permute-start.3 = (s16[4,256,256]{2,1,0:T(8,128)(2,1)S(1)}, s16[4,256,256]{2,1,0:T(8,128)(2,1)S(1)}, u32[]{:S(2)}, u32[]{:S(2)}) collective-permute-start(s16[4,256,256]{2,1,0:T(8,128)(2,1)S(1)} %get-tuple-element.40), channel_id=1, source_target_pairs={{0,1},{1,0},{2,3},{3,2},{4,5},{5,4},{6,7},{7,6},{8,9},{9,8},{10,11... | collective-permute-start | bytes 1572872 | tf_op jit(solution)/shard_map/ppermute | solution.py:284
  10.2 22.6 %collective-permute-start.7 = (s16[4,256,256]{2,1,0:T(8,128)(2,1)S(1)}, s16[4,256,256]{2,1,0:T(8,128)(2,1)S(1)}, u32[]{:S(2)}, u32[]{:S(2)}) collective-permute-start(s16[4,256,256]{2,1,0:T(8,128)(2,1)S(1)} %get-tuple-element.42), channel_id=1, source_target_pairs={{0,2},{1,3},{2,0},{3,1},{4,6},{5,7},{6,4},{7,5},{8,10},{9,11},{10,... | collective-permute-start | bytes 1572872 | tf_op jit(solution)/shard_map/ppermute | solution.py:284
  12.6 33.1 %collective-permute-start.8 = (s16[4,256,256]{2,1,0:T(8,128)(2,1)S(1)}, s16[4,256,256]{2,1,0:T(8,128)(2,1)S(1)}, u32[]{:S(2)}, u32[]{:S(2)}) collective-permute-start(s16[4,256,256]{2,1,0:T(8,128)(2,1)S(1)} %get-tuple-element.48), channel_id=1, source_target_pairs={{0,3},{1,2},{2,1},{3,0},{4,7},{5,6},{6,5},{7,4},{8,11},{9,10},{10,... | collective-permute-start | bytes 1572872 | tf_op jit(solution)/shard_map/ppermute | solution.py:284
  17.8 11.0 %collective-permute-start.2 = (bf16[4,48,256]{2,1,0:T(8,128)(2,1)S(1)}, bf16[4,48,256]{2,1,0:T(8,128)(2,1)S(1)}, u32[]{:S(2)}, u32[]{:S(2)}) collective-permute-start(bf16[4,48,256]{2,1,0:T(8,128)(2,1)S(1)} %join_2.1.after_ref.refs_0_), channel_id=1, source_target_pairs={{0,128},{32,160},{64,192},{96,224},{128,0},{160,32},{192,64},{224,... | collective-permute-start | bytes 294920 | tf_op jit(solution)/shard_map/ppermute | solution.py:287
  28.8 8.3 %collective-permute-start.4 = (bf16[8,48,256]{2,1,0:T(8,128)(2,1)S(1)}, bf16[8,48,256]{2,1,0:T(8,128)(2,1)S(1)}, u32[]{:S(2)}, u32[]{:S(2)}) collective-permute-start(bf16[8,48,256]{2,1,0:T(8,128)(2,1)S(1)} %join_4.1.after_ref.refs_0_), channel_id=1, source_target_pairs={{0,224},{32,0},{64,32},{96,64},{128,96},{160,128},{192,160},{224,1... | collective-permute-start | bytes 589832 | tf_op jit(solution)/shard_map/ppermute | solution.py:287
  32.8 7.5 %collective-permute-start.5 = (bf16[8,48,256]{2,1,0:T(8,128)(2,1)S(1)}, bf16[8,48,256]{2,1,0:T(8,128)(2,1)S(1)}, u32[]{:S(2)}, u32[]{:S(2)}) collective-permute-start(bf16[8,48,256]{2,1,0:T(8,128)(2,1)S(1)} %join_4.1.after_ref.refs_0_), channel_id=1, source_target_pairs={{0,32},{32,64},{64,96},{96,128},{128,160},{160,192},{192,224},{224... | collective-permute-start | bytes 589832 | tf_op jit(solution)/shard_map/ppermute | solution.py:287
  32.8 10.3 %collective-permute-start.6 = (bf16[8,48,256]{2,1,0:T(8,128)(2,1)S(1)}, bf16[8,48,256]{2,1,0:T(8,128)(2,1)S(1)}, u32[]{:S(2)}, u32[]{:S(2)}) collective-permute-start(bf16[8,48,256]{2,1,0:T(8,128)(2,1)S(1)} %join_4.1.after_ref.refs_0_), channel_id=1, source_target_pairs={{0,64},{32,224},{64,128},{96,32},{128,192},{160,96},{192,0},{224,1... | collective-permute-start | bytes 589832 | tf_op jit(solution)/shard_map/ppermute | solution.py:287
  43.1 8.4 %collective-permute-start.9 = (bf16[32,48,256]{2,1,0:T(8,128)(2,1)S(1)}, bf16[32,48,256]{2,1,0:T(8,128)(2,1)S(1)}, u32[]{:S(2)}, u32[]{:S(2)}) collective-permute-start(bf16[32,48,256]{2,1,0:T(8,128)(2,1)S(1)} %join_8.1.source_ref.after_ref), channel_id=1, source_target_pairs={{0,1},{1,0},{2,3},{3,2},{4,5},{5,4},{6,7},{7,6},{8,9},{9,8},{10,11... | collective-permute-start | bytes 2359304 | tf_op jit(solution)/shard_map/ppermute | solution.py:305
  54.9 13.0 %collective-permute-start.10 = (bf16[272,768]{1,0:T(8,128)(2,1)S(1)}, bf16[272,768]{1,0:T(8,128)(2,1)S(1)}, u32[]{:S(2)}, u32[]{:S(2)}) collective-permute-start(bf16[272,768]{1,0:T(8,128)(2,1)S(1)} %beams_0.1), channel_id=1, source_target_pairs={{0,8},{4,12},{8,0},{12,4},{1,9},{5,13},{9,1},{13,5},{2,10},{6,14},... | collective-permute-start | bytes 1253384 | tf_op jit(solution)/shard_map/ppermute | solution.py:317
  62.7 14.5 %copy-start = (s32[4,768]{1,0:T(4,128)S(1)}, s32[4,768]{1,0:T(4,128)}, u32[]{:S(2)}) copy-start(s32[4,768]{1,0:T(4,128)} %constant.54.clone.refs_8_) | copy-start | bytes 36868
  62.7 14.5 %collective-permute-start.11 = (bf16[272,768]{1,0:T(8,128)(2,1)S(1)}, bf16[272,768]{1,0:T(8,128)(2,1)S(1)}, u32[]{:S(2)}, u32[]{:S(2)}) collective-permute-start(bf16[272,768]{1,0:T(8,128)(2,1)S(1)} %beams_1.1), channel_id=1, source_target_pairs={{0,4},{4,8},{8,12},{12,0},{1,5},{5,9},{9,13},{13,1},{2,6},{6,10},{... | collective-permute-start | bytes 1253384 | tf_op jit(solution)/shard_map/ppermute | solution.py:317
  63.1 14.1 %collective-permute-start.12 = (bf16[272,768]{1,0:T(8,128)(2,1)S(1)}, bf16[272,768]{1,0:T(8,128)(2,1)S(1)}, u32[]{:S(2)}, u32[]{:S(2)}) collective-permute-start(bf16[272,768]{1,0:T(8,128)(2,1)S(1)} %beams_2.1), channel_id=1, source_target_pairs={{0,12},{4,0},{8,4},{12,8},{1,13},{5,1},{9,5},{13,9},{2,14},{6,2},{... | collective-permute-start | bytes 1253384 | tf_op jit(solution)/shard_map/ppermute | solution.py:317

commit v9 on v8

--- a/solution.py
+++ b/solution.py
@@ -19,7 +19,7 @@
 CH = 256
 COLS = 96
 TILE = 32
-NORM_ROWS = 16
+NORM_ROWS = 8
 
 
 SINE = [np.float32(1.570796305), np.float32(-0.6459629382), np.float32(0.07967590293), np.float32(-0.004592288967)]
@@ -200,7 +200,7 @@
     row = lax.broadcasted_iota(jnp.int32, sums.shape, 0) - first_row
     zero = jnp.zeros_like(sums)
     split = zero
-    for index, part in enumerate(thirds(sums)):
+    for index, part in enumerate(thirds(sums)[:2]):
         split = jnp.where(row == index, part.astype(f32), split)
     norm_ref[...] = jnp.concatenate([split] + [zero] * (NF - 1), axis=1).astype(bf16)
 
@@ -292,10 +292,10 @@
     held, *parts = tie(held, *parts)
     far, near, both = moved(2), moved(1), moved(3)
     other = lax.ppermute(held, "yl", SWAP)
+    held = join(other, held, other)
+    other = along_z(held, lambda i: i ^ 4)
     rep_own, token = replicas(place, parts[0], held, "own")
-    held = join(token, held, other)
-    other = along_z(held, lambda i: i ^ 4)
-    rep_near, token = replicas(place, near, held, "near")
+    rep_near, token = replicas(place, near, token, "near")
     held = join(token, held, other)
     two_away = along_z(held, lambda i: i - 2 if i % 2 else i + 2)
     above = along_z(held, lambda i: i - 1)
@@ -305,7 +305,7 @@
     swapped = lax.ppermute(held, "c", SWAP)
     rep_both, _ = replicas(place, both, held, "both")
     halves = ((held, 0), (swapped, 0), (held, 1), (swapped, 1))
-    prepared = [prepare(*half, 4 * index) for index, half in enumerate(halves)]
+    prepared = [prepare(*half, 2 * index) for index, half in enumerate(halves)]
     weights, norms = [w for w, _ in prepared], [n for _, n in prepared]
     reps = (rep_own, rep_near, rep_far, rep_both)
     received = []

time: 79.3 us -> 75 us (0.946)
  waiting for transfers between devices: 15.3 us -> 12.5 us
  starting transfers between devices: 28.4 us -> 26.9 us
    ppermute x4, waiting for transfers between devices: 5.93 us -> 3.59 us  [along_z(): return lax.ppermute(values, 'z', [(i, target(i) % 8) for i in range(8)])]
    ppermute x4, starting transfers between devices: 10.6 us -> 9.38 us  [along_z(): return lax.ppermute(values, 'z', [(i, target(i) % 8) for i in range(8)])]
  transfers between devices with their start and end apart: 13 -> 13, of which waited for: 4 -> 4; matrix products, arithmetic and copies ran while one was open for 3% -> 3% of each run, Pallas kernels for 33% -> 35%
where the time goes in v9:
time: 75 us; the launch traced here: 74.8 us
  Pallas kernels  31.2 us (42%)
  starting transfers between devices  26.9 us (36%)
  waiting for transfers between devices  12.5 us (17%)
  other arithmetic  3.82 us (5%)
    pallas_call x4, Pallas kernels, replicas(): pl.pallas_call(replicas_kernel, grid_spec=pltpu.PrefetchScalarGridSpec(nu...  17.8 us
    pallas_call x4, Pallas kernels, beams_block(): pl.pallas_call(functools.partial(beams_kernel, slot=step), in_specs=[VMEM...  9.56 us
    ppermute x4, starting transfers between devices, along_z(): return lax.ppermute(values, 'z', [(i, target(i) % 8) for i in range(8)])  9.38 us
    ppermute x3, waiting for transfers between devices, per_device(): lax.ppermute(beams, 'x', [(i, (i + dx) % 4) for i in range(4)])  8.84 us
    ppermute x3, starting transfers between devices, per_device(): lax.ppermute(beams, 'x', [(i, (i + dx) % 4) for i in range(4)])  5.77 us
    ppermute x3, starting transfers between devices, moved(): lax.ppermute(parts[flip], ('yh', 'c'), [(i, i ^ flip) for i in range(4)])  5.14 us
    ppermute x1, starting transfers between devices, per_device(): other = lax.ppermute(held, 'yh', SWAP)  3.83 us
    ppermute x4, waiting for transfers between devices, along_z(): return lax.ppermute(values, 'z', [(i, target(i) % 8) for i in range(8)])  3.59 us
  transfers between devices with their start and end apart: 13, of which 4 were waited for; matrix products, arithmetic and copies ran while one was open for 3% of the time, Pallas kernels for 35%

profile of v9, /device:TPU:1, one launch (start us, length us, event | category | flops | bytes accessed | tf_op | source)
XLA Modules:
  0.0 74.8 jit_solution(4045565130735016461)
XLA Ops:
  1.5 3.8 %collective-permute-start = (bf16[1,48,256]{2,1,0:T(8,128)(2,1)S(1)}, bf16[1,48,256]{2,1,0:T(8,128)(2,1)S(1)}, u32[]{:S(2)}, u32[]{:S(2)}) collective-permute-start(bf16[1,48,256]{2,1,0:T(8,128)(2,1)S(1)} %reshape.16.refs_0_), channel_id=1, source_target_pairs={{0,2},{2,0},{1,3},{3,1},{4,6},{6,4},{5,7},{7,5},{8,10},{10,8},{9,1... | collective-permute-start | bytes 73736 | tf_op jit(solution)/shard_map/ppermute | solution.py:290
  5.3 2.4 %fusion.3 = (s16[4,256,256]{2,1,0:T(8,128)(2,1)S(1)}, s16[4,256,256]{2,1,0:T(8,128)(2,1)S(1)}, s16[4,256,256]{2,1,0:T(8,128)(2,1)S(1)}, s16[4,256,256]{2,1,0:T(8,128)(2,1)S(1)}) fusion(s32[4,2,2,256,256]{4,3,2,1,0:T(8,128)} %bitcast.31, s32[]{:T(128)S(6)} %select_n.42, s32[]{:T(128)S(6)} %select_n.41, s32[]{:T(128)S(6)} %select_n.40, s32[]{:T(128)S(6)} %select_n.39), kind=kLoop, calls=%fused_computation.7 | loop fusion | flops 1048576 | bytes 6291472 | tf_op jit(solution)/shard_map/convert_element_type | solution.py:277
  8.3 1.9 %collective-permute-start.3 = (s16[4,256,256]{2,1,0:T(8,128)(2,1)S(1)}, s16[4,256,256]{2,1,0:T(8,128)(2,1)S(1)}, u32[]{:S(2)}, u32[]{:S(2)}) collective-permute-start(s16[4,256,256]{2,1,0:T(8,128)(2,1)S(1)} %get-tuple-element.38), channel_id=1, source_target_pairs={{0,1},{1,0},{2,3},{3,2},{4,5},{5,4},{6,7},{7,6},{8,9},{9,8},{10,11... | collective-permute-start | bytes 1572872 | tf_op jit(solution)/shard_map/ppermute | solution.py:284
  10.2 2.4 %collective-permute-start.7 = (s16[4,256,256]{2,1,0:T(8,128)(2,1)S(1)}, s16[4,256,256]{2,1,0:T(8,128)(2,1)S(1)}, u32[]{:S(2)}, u32[]{:S(2)}) collective-permute-start(s16[4,256,256]{2,1,0:T(8,128)(2,1)S(1)} %get-tuple-element.42), channel_id=1, source_target_pairs={{0,2},{1,3},{2,0},{3,1},{4,6},{5,7},{6,4},{7,5},{8,10},{9,11},{10,... | collective-permute-start | bytes 1572872 | tf_op jit(solution)/shard_map/ppermute | solution.py:284
  12.6 0.9 %collective-permute-start.8 = (s16[4,256,256]{2,1,0:T(8,128)(2,1)S(1)}, s16[4,256,256]{2,1,0:T(8,128)(2,1)S(1)}, u32[]{:S(2)}, u32[]{:S(2)}) collective-permute-start(s16[4,256,256]{2,1,0:T(8,128)(2,1)S(1)} %get-tuple-element.48), channel_id=1, source_target_pairs={{0,3},{1,2},{2,1},{3,0},{4,7},{5,6},{6,5},{7,4},{8,11},{9,10},{10,... | collective-permute-start | bytes 1572872 | tf_op jit(solution)/shard_map/ppermute | solution.py:284
  13.5 6.6 %collective-permute-start.2 = (bf16[4,48,256]{2,1,0:T(8,128)(2,1)S(1)}, bf16[4,48,256]{2,1,0:T(8,128)(2,1)S(1)}, u32[]{:S(2)}, u32[]{:S(2)}) collective-permute-start(bf16[4,48,256]{2,1,0:T(8,128)(2,1)S(1)} %join_2.1.after_ref.refs_0_), channel_id=1, source_target_pairs={{0,128},{32,160},{64,192},{96,224},{128,0},{160,32},{192,64},{224,... | collective-permute-start | bytes 294920 | tf_op jit(solution)/shard_map/ppermute | solution.py:287
  20.1 4.3 %replicas_own.1 = (bf16[4,8,256,512]{3,2,1,0:T(8,128)(2,1)S(1)}, s32[8,128]{1,0:T(8,128)S(1)}) custom-call(s32[6]{0:T(128)S(1)} %stack.27.place, s16[4,256,256]{2,1,0:T(8,128)(2,1)S(1)} %get-tuple-element.39.travel_ref, bf16[4,48,256]{2,1,0:T(8,128)(2,1)S(1)} %join_2.1.after_ref.refs_0_), custom_call_target="tpu_custom_call" | custom-call | flops 40000000000 | bytes 1000000 | tf_op jit(solution)/shard_map/replicas_own/pallas_call | solution.py:108
  24.5 4.3 %replicas_near.1 = (bf16[4,8,256,512]{3,2,1,0:T(8,128)(2,1)S(1)}, s32[8,128]{1,0:T(8,128)S(1)}) custom-call(s32[6]{0:T(128)S(1)} %stack.27.place, s16[4,256,256]{2,1,0:T(8,128)(2,1)S(1)} %collective-permute-done.3.travel_ref, s32[8,128]{1,0:T(8,128)S(1)} %get-tuple-element.40.after_ref), custom_call_target="tpu_custom_call" | custom-call | flops 40000000000 | bytes 1000000 | tf_op jit(solution)/shard_map/replicas_near/pallas_call | solution.py:108
  28.9 1.5 %collective-permute-start.5 = (bf16[8,48,256]{2,1,0:T(8,128)(2,1)S(1)}, bf16[8,48,256]{2,1,0:T(8,128)(2,1)S(1)}, u32[]{:S(2)}, u32[]{:S(2)}) collective-permute-start(bf16[8,48,256]{2,1,0:T(8,128)(2,1)S(1)} %join_4.1.after_ref.refs_0_), channel_id=1, source_target_pairs={{0,32},{32,64},{64,96},{96,128},{128,160},{160,192},{192,224},{224... | collective-permute-start | bytes 589832 | tf_op jit(solution)/shard_map/ppermute | solution.py:287
  30.3 1.2 %collective-permute-start.6 = (bf16[8,48,256]{2,1,0:T(8,128)(2,1)S(1)}, bf16[8,48,256]{2,1,0:T(8,128)(2,1)S(1)}, u32[]{:S(2)}, u32[]{:S(2)}) collective-permute-start(bf16[8,48,256]{2,1,0:T(8,128)(2,1)S(1)} %join_4.1.after_ref.refs_0_), channel_id=1, source_target_pairs={{0,64},{32,224},{64,128},{96,32},{128,192},{160,96},{192,0},{224,1... | collective-permute-start | bytes 589832 | tf_op jit(solution)/shard_map/ppermute | solution.py:287
  31.5 4.3 %replicas_far.1 = (bf16[4,8,256,512]{3,2,1,0:T(8,128)(2,1)S(1)}, s32[8,128]{1,0:T(8,128)S(1)}) custom-call(s32[6]{0:T(128)S(1)} %stack.27.place, s16[4,256,256]{2,1,0:T(8,128)(2,1)S(1)} %collective-permute-done.7.travel_ref, bf16[8,48,256]{2,1,0:T(8,128)(2,1)S(1)} %join_4.1.after_ref.refs_0_), custom_call_target="tpu_custom_call" | custom-call | flops 40000000000 | bytes 1000000 | tf_op jit(solution)/shard_map/replicas_far/pallas_call | solution.py:108
  35.9 1.2 %collective-permute-done.5.refs_2_ = bf16[8,48,256]{2,1,0:T(8,128)(2,1)S(1)} collective-permute-done((bf16[8,48,256]{2,1,0:T(8,128)(2,1)S(1)}, bf16[8,48,256]{2,1,0:T(8,128)(2,1)S(1)}, u32[]{:S(2)}, u32[]{:S(2)}) %collective-permute-start.5) | collective-permute-done | bytes 196640 | tf_op jit(solution)/shard_map/ppermute | solution.py:287
  37.1 2.4 %collective-permute-done.6.refs_3_ = bf16[8,48,256]{2,1,0:T(8,128)(2,1)S(1)} collective-permute-done((bf16[8,48,256]{2,1,0:T(8,128)(2,1)S(1)}, bf16[8,48,256]{2,1,0:T(8,128)(2,1)S(1)}, u32[]{:S(2)}, u32[]{:S(2)}) %collective-permute-start.6) | collective-permute-done | bytes 196640 | tf_op jit(solution)/shard_map/ppermute | solution.py:287
  39.5 2.4 %collective-permute-start.9 = (bf16[32,48,256]{2,1,0:T(8,128)(2,1)S(1)}, bf16[32,48,256]{2,1,0:T(8,128)(2,1)S(1)}, u32[]{:S(2)}, u32[]{:S(2)}) collective-permute-start(bf16[32,48,256]{2,1,0:T(8,128)(2,1)S(1)} %join_8.1.source_ref.after_ref), channel_id=1, source_target_pairs={{0,1},{1,0},{2,3},{3,2},{4,5},{5,4},{6,7},{7,6},{8,9},{9,8},{10,11... | collective-permute-start | bytes 2359304 | tf_op jit(solution)/shard_map/ppermute | solution.py:305
  41.9 4.9 %replicas_both.1 = (bf16[4,8,256,512]{3,2,1,0:T(8,128)(2,1)S(1)}, s32[8,128]{1,0:T(8,128)}) custom-call(s32[6]{0:T(128)S(1)} %stack.27.place, s16[4,256,256]{2,1,0:T(8,128)(2,1)S(1)} %collective-permute-done.8.travel_ref, bf16[32,48,256]{2,1,0:T(8,128)(2,1)S(1)} %join_8.1.source_ref.after_ref), custom_call_target="tpu_custom_call" | custom-call | flops 40000000000 | bytes 1000000 | tf_op jit(solution)/shard_map/replicas_both/pallas_call | solution.py:108
  48.6 2.4 %beams_0.1 = bf16[264,768]{1,0:T(8,128)(2,1)S(1)} custom-call(bf16[4,8,256,512]{3,2,1,0:T(8,128)(2,1)S(1)} %get-tuple-element.45.refs_0_, bf16[4,8,256,512]{3,2,1,0:T(8,128)(2,1)S(1)} %get-tuple-element.46.refs_1_, bf16[4,8,256,512]{3,2,1,0:T(8,128)(2,1)S(1)} %get-tuple-element.47.refs_2_, bf16[4,8,256,512]{3,2,1,0:T(8,128)(2,1)S(1)} %get-tuple-element.49.refs_3_, ...), custom_call_target="tpu_custom_call" | custom-call | flops 3000000000 | bytes 1000000 | tf_op jit(solution)/shard_map/beams_0/pallas_call | solution.py:160
  51.0 3.0 %collective-permute-start.10 = (bf16[264,768]{1,0:T(8,128)(2,1)S(1)}, bf16[264,768]{1,0:T(8,128)(2,1)S(1)}, u32[]{:S(2)}, u32[]{:S(2)}) collective-permute-start(bf16[264,768]{1,0:T(8,128)(2,1)S(1)} %beams_0.1), channel_id=1, source_target_pairs={{0,8},{4,12},{8,0},{12,4},{1,9},{5,13},{9,1},{13,5},{2,10},{6,14},... | collective-permute-start | bytes 1216520 | tf_op jit(solution)/shard_map/ppermute | solution.py:317
  54.1 2.4 %beams_1.1 = bf16[264,768]{1,0:T(8,128)(2,1)S(1)} custom-call(bf16[4,8,256,512]{3,2,1,0:T(8,128)(2,1)S(1)} %get-tuple-element.45.refs_0_, bf16[4,8,256,512]{3,2,1,0:T(8,128)(2,1)S(1)} %get-tuple-element.46.refs_1_, bf16[4,8,256,512]{3,2,1,0:T(8,128)(2,1)S(1)} %get-tuple-element.47.refs_2_, bf16[4,8,256,512]{3,2,1,0:T(8,128)(2,1)S(1)} %get-tuple-element.49.refs_3_, ...), custom_call_target="tpu_custom_call" | custom-call | flops 3000000000 | bytes 1000000 | tf_op jit(solution)/shard_map/beams_1/pallas_call | solution.py:160
  56.4 2.4 %beams_2.1 = bf16[264,768]{1,0:T(8,128)(2,1)S(1)} custom-call(bf16[4,8,256,512]{3,2,1,0:T(8,128)(2,1)S(1)} %get-tuple-element.45.refs_0_, bf16[4,8,256,512]{3,2,1,0:T(8,128)(2,1)S(1)} %get-tuple-element.46.refs_1_, bf16[4,8,256,512]{3,2,1,0:T(8,128)(2,1)S(1)} %get-tuple-element.47.refs_2_, bf16[4,8,256,512]{3,2,1,0:T(8,128)(2,1)S(1)} %get-tuple-element.49.refs_3_, ...), custom_call_target="tpu_custom_call" | custom-call | flops 3000000000 | bytes 1000000 | tf_op jit(solution)/shard_map/beams_2/pallas_call | solution.py:160
  59.2 2.4 %collective-permute-start.12 = (bf16[264,768]{1,0:T(8,128)(2,1)S(1)}, bf16[264,768]{1,0:T(8,128)(2,1)S(1)}, u32[]{:S(2)}, u32[]{:S(2)}) collective-permute-start(bf16[264,768]{1,0:T(8,128)(2,1)S(1)} %beams_2.1), channel_id=1, source_target_pairs={{0,12},{4,0},{8,4},{12,8},{1,13},{5,1},{9,5},{13,9},{2,14},{6,2},{... | collective-permute-start | bytes 1216520 | tf_op jit(solution)/shard_map/ppermute | solution.py:317
  61.6 2.2 %collective-permute-done.10.refs_0_ = bf16[264,768]{1,0:T(8,128)(2,1)S(1)} collective-permute-done((bf16[264,768]{1,0:T(8,128)(2,1)S(1)}, bf16[264,768]{1,0:T(8,128)(2,1)S(1)}, u32[]{:S(2)}, u32[]{:S(2)}) %collective-permute-start.10) | collective-permute-done | bytes 405536 | tf_op jit(solution)/shard_map/ppermute | solution.py:317
  63.8 2.4 %beams_3.1.refs_3_ = f32[256,768]{1,0:T(8,128)S(1)} custom-call(bf16[4,8,256,512]{3,2,1,0:T(8,128)(2,1)S(1)} %get-tuple-element.45.refs_0_, bf16[4,8,256,512]{3,2,1,0:T(8,128)(2,1)S(1)} %get-tuple-element.46.refs_1_, bf16[4,8,256,512]{3,2,1,0:T(8,128)(2,1)S(1)} %get-tuple-element.47.refs_2_, bf16[4,8,256,512]{3,2,1,0:T(8,128)(2,1)S(1)} %get-tuple-element.49.refs_3_, ...), custom_call_target="tpu_custom_call" | custom-call | flops 3000000000 | bytes 1000000 | tf_op jit(solution)/shard_map/beams_3/pallas_call | solution.py:160
  66.2 6.6 %collective-permute-done.11.refs_1_ = bf16[264,768]{1,0:T(8,128)(2,1)S(1)} collective-permute-done((bf16[264,768]{1,0:T(8,128)(2,1)S(1)}, bf16[264,768]{1,0:T(8,128)(2,1)S(1)}, u32[]{:S(2)}, u32[]{:S(2)}) %collective-permute-start.11) | collective-permute-done | bytes 405536 | tf_op jit(solution)/shard_map/ppermute | solution.py:317
  72.8 2.0 %finish.1 = f32[48,256]{1,0:T(8,128)} custom-call(s32[6]{0:T(128)S(1)} %stack.27.place, bf16[264,768]{1,0:T(8,128)(2,1)S(1)} %collective-permute-done.10.refs_0_, bf16[264,768]{1,0:T(8,128)(2,1)S(1)} %collective-permute-done.11.refs_1_, bf16[264,768]{1,0:T(8,128)(2,1)S(1)} %collective-permute-done.12.refs_2_, f32[256,768]{1,0:T(8,128)S(1)} %beams_3.1.refs_3_, ...), custom_call_target="tpu_custom_call" | custom-call | tf_op jit(solution)/shard_map/finish/pallas_call | solution.py:250
  (27 shorter events, 4.4 us)
Async XLA Ops:
  1.5 6.4 %collective-permute-start = (bf16[1,48,256]{2,1,0:T(8,128)(2,1)S(1)}, bf16[1,48,256]{2,1,0:T(8,128)(2,1)S(1)}, u32[]{:S(2)}, u32[]{:S(2)}) collective-permute-start(bf16[1,48,256]{2,1,0:T(8,128)(2,1)S(1)} %reshape.16.refs_0_), channel_id=1, source_target_pairs={{0,2},{2,0},{1,3},{3,1},{4,6},{6,4},{5,7},{7,5},{8,10},{10,8},{9,1... | collective-permute-start | bytes 73736 | tf_op jit(solution)/shard_map/ppermute | solution.py:290
  7.8 5.6 %collective-permute-start.1 = (bf16[2,48,256]{2,1,0:T(8,128)(2,1)S(1)}, bf16[2,48,256]{2,1,0:T(8,128)(2,1)S(1)}, u32[]{:S(2)}, u32[]{:S(2)}) collective-permute-start(bf16[2,48,256]{2,1,0:T(8,128)(2,1)S(1)} %join_1.1.refs_0_), channel_id=1, source_target_pairs={{0,16},{16,0},{1,17},{17,1},{2,18},{18,2},{3,19},{19,3},{4,20},{20... | collective-permute-start | bytes 147464 | tf_op jit(solution)/shard_map/ppermute | solution.py:294
  8.3 16.1 %collective-permute-start.3 = (s16[4,256,256]{2,1,0:T(8,128)(2,1)S(1)}, s16[4,256,256]{2,1,0:T(8,128)(2,1)S(1)}, u32[]{:S(2)}, u32[]{:S(2)}) collective-permute-start(s16[4,256,256]{2,1,0:T(8,128)(2,1)S(1)} %get-tuple-element.38), channel_id=1, source_target_pairs={{0,1},{1,0},{2,3},{3,2},{4,5},{5,4},{6,7},{7,6},{8,9},{9,8},{10,11... | collective-permute-start | bytes 1572872 | tf_op jit(solution)/shard_map/ppermute | solution.py:284
  10.2 21.3 %collective-permute-start.7 = (s16[4,256,256]{2,1,0:T(8,128)(2,1)S(1)}, s16[4,256,256]{2,1,0:T(8,128)(2,1)S(1)}, u32[]{:S(2)}, u32[]{:S(2)}) collective-permute-start(s16[4,256,256]{2,1,0:T(8,128)(2,1)S(1)} %get-tuple-element.42), channel_id=1, source_target_pairs={{0,2},{1,3},{2,0},{3,1},{4,6},{5,7},{6,4},{7,5},{8,10},{9,11},{10,... | collective-permute-start | bytes 1572872 | tf_op jit(solution)/shard_map/ppermute | solution.py:284
  12.6 29.3 %collective-permute-start.8 = (s16[4,256,256]{2,1,0:T(8,128)(2,1)S(1)}, s16[4,256,256]{2,1,0:T(8,128)(2,1)S(1)}, u32[]{:S(2)}, u32[]{:S(2)}) collective-permute-start(s16[4,256,256]{2,1,0:T(8,128)(2,1)S(1)} %get-tuple-element.48), channel_id=1, source_target_pairs={{0,3},{1,2},{2,1},{3,0},{4,7},{5,6},{6,5},{7,4},{8,11},{9,10},{10,... | collective-permute-start | bytes 1572872 | tf_op jit(solution)/shard_map/ppermute | solution.py:284
  13.5 15.3 %collective-permute-start.2 = (bf16[4,48,256]{2,1,0:T(8,128)(2,1)S(1)}, bf16[4,48,256]{2,1,0:T(8,128)(2,1)S(1)}, u32[]{:S(2)}, u32[]{:S(2)}) collective-permute-start(bf16[4,48,256]{2,1,0:T(8,128)(2,1)S(1)} %join_2.1.after_ref.refs_0_), channel_id=1, source_target_pairs={{0,128},{32,160},{64,192},{96,224},{128,0},{160,32},{192,64},{224,... | collective-permute-start | bytes 294920 | tf_op jit(solution)/shard_map/ppermute | solution.py:287
  28.8 7.1 %collective-permute-start.4 = (bf16[8,48,256]{2,1,0:T(8,128)(2,1)S(1)}, bf16[8,48,256]{2,1,0:T(8,128)(2,1)S(1)}, u32[]{:S(2)}, u32[]{:S(2)}) collective-permute-start(bf16[8,48,256]{2,1,0:T(8,128)(2,1)S(1)} %join_4.1.after_ref.refs_0_), channel_id=1, source_target_pairs={{0,224},{32,0},{64,32},{96,64},{128,96},{160,128},{192,160},{224,1... | collective-permute-start | bytes 589832 | tf_op jit(solution)/shard_map/ppermute | solution.py:287
  28.9 8.2 %collective-permute-start.5 = (bf16[8,48,256]{2,1,0:T(8,128)(2,1)S(1)}, bf16[8,48,256]{2,1,0:T(8,128)(2,1)S(1)}, u32[]{:S(2)}, u32[]{:S(2)}) collective-permute-start(bf16[8,48,256]{2,1,0:T(8,128)(2,1)S(1)} %join_4.1.after_ref.refs_0_), channel_id=1, source_target_pairs={{0,32},{32,64},{64,96},{96,128},{128,160},{160,192},{192,224},{224... | collective-permute-start | bytes 589832 | tf_op jit(solution)/shard_map/ppermute | solution.py:287
  30.3 9.1 %collective-permute-start.6 = (bf16[8,48,256]{2,1,0:T(8,128)(2,1)S(1)}, bf16[8,48,256]{2,1,0:T(8,128)(2,1)S(1)}, u32[]{:S(2)}, u32[]{:S(2)}) collective-permute-start(bf16[8,48,256]{2,1,0:T(8,128)(2,1)S(1)} %join_4.1.after_ref.refs_0_), channel_id=1, source_target_pairs={{0,64},{32,224},{64,128},{96,32},{128,192},{160,96},{192,0},{224,1... | collective-permute-start | bytes 589832 | tf_op jit(solution)/shard_map/ppermute | solution.py:287
  39.5 8.2 %collective-permute-start.9 = (bf16[32,48,256]{2,1,0:T(8,128)(2,1)S(1)}, bf16[32,48,256]{2,1,0:T(8,128)(2,1)S(1)}, u32[]{:S(2)}, u32[]{:S(2)}) collective-permute-start(bf16[32,48,256]{2,1,0:T(8,128)(2,1)S(1)} %join_8.1.source_ref.after_ref), channel_id=1, source_target_pairs={{0,1},{1,0},{2,3},{3,2},{4,5},{5,4},{6,7},{7,6},{8,9},{9,8},{10,11... | collective-permute-start | bytes 2359304 | tf_op jit(solution)/shard_map/ppermute | solution.py:305
  51.0 12.8 %collective-permute-start.10 = (bf16[264,768]{1,0:T(8,128)(2,1)S(1)}, bf16[264,768]{1,0:T(8,128)(2,1)S(1)}, u32[]{:S(2)}, u32[]{:S(2)}) collective-permute-start(bf16[264,768]{1,0:T(8,128)(2,1)S(1)} %beams_0.1), channel_id=1, source_target_pairs={{0,8},{4,12},{8,0},{12,4},{1,9},{5,13},{9,1},{13,5},{2,10},{6,14},... | collective-permute-start | bytes 1216520 | tf_op jit(solution)/shard_map/ppermute | solution.py:317
  58.8 14.0 %copy-start = (s32[4,768]{1,0:T(4,128)S(1)}, s32[4,768]{1,0:T(4,128)}, u32[]{:S(2)}) copy-start(s32[4,768]{1,0:T(4,128)} %constant.54.clone.refs_8_) | copy-start | bytes 36868
  58.9 14.0 %collective-permute-start.11 = (bf16[264,768]{1,0:T(8,128)(2,1)S(1)}, bf16[264,768]{1,0:T(8,128)(2,1)S(1)}, u32[]{:S(2)}, u32[]{:S(2)}) collective-permute-start(bf16[264,768]{1,0:T(8,128)(2,1)S(1)} %beams_1.1), channel_id=1, source_target_pairs={{0,4},{4,8},{8,12},{12,0},{1,5},{5,9},{9,13},{13,1},{2,6},{6,10},{... | collective-permute-start | bytes 1216520 | tf_op jit(solution)/shard_map/ppermute | solution.py:317
  59.2 13.6 %collective-permute-start.12 = (bf16[264,768]{1,0:T(8,128)(2,1)S(1)}, bf16[264,768]{1,0:T(8,128)(2,1)S(1)}, u32[]{:S(2)}, u32[]{:S(2)}) collective-permute-start(bf16[264,768]{1,0:T(8,128)(2,1)S(1)} %beams_2.1), channel_id=1, source_target_pairs={{0,12},{4,0},{8,4},{12,8},{1,13},{5,1},{9,5},{13,9},{2,14},{6,2},{... | collective-permute-start | bytes 1216520 | tf_op jit(solution)/shard_map/ppermute | solution.py:317

commit v10 on v9

--- a/solution.py
+++ b/solution.py
@@ -101,20 +101,22 @@
     lax.fori_loop(0, ROWS // TILE, body, 0)
 
 
-def replicas(place, travel, after, name):
+def replicas(place, travel, after, name, slots=(0, 4)):
+    first, stop = slots
+
     def index(i, p):
-        return (p[i], 0, 0)
+        return (p[first + i], 0, 0)
 
     return pl.pallas_call(
         replicas_kernel,
         grid_spec=pltpu.PrefetchScalarGridSpec(
             num_scalar_prefetch=1,
-            grid=(4,),
+            grid=(stop - first,),
             in_specs=[pl.BlockSpec((1, ROWS, CH), index), VMEM],
             out_specs=[VMEM, VMEM],
         ),
         out_shape=[
-            jax.ShapeDtypeStruct((4, NF, ROWS, 2 * CH), bf16),
+            jax.ShapeDtypeStruct((stop - first, NF, ROWS, 2 * CH), bf16),
             jax.ShapeDtypeStruct((8, 128), jnp.int32),
         ],
         cost_estimate=pl.CostEstimate(flops=40_000_000_000, bytes_accessed=1_000_000, transcendentals=0),
@@ -143,22 +145,22 @@
     )(*arrays, token)
 
 
-def beams_kernel(*refs, slot):
+def beams_kernel(*refs, slots):
     reps, weights, norms, out_ref = refs[0:4], refs[4:8], refs[8:12], refs[12]
     columns = []
     for f in range(NF):
-        parts = [product(rep[slot, f], w_ref[f]) for rep, w_ref in zip(reps, weights)]
+        parts = [product(rep[slot, f], w_ref[f]) for rep, slot, w_ref in zip(reps, slots, weights)]
         columns.append((parts[0] + parts[1]) + (parts[2] + parts[3]))
     out_ref[0:ROWS] = jnp.concatenate(columns, axis=1).astype(out_ref.dtype)
     if out_ref.shape[0] > ROWS:
         out_ref[ROWS : ROWS + NORM_ROWS] = (norms[0][...] + norms[1][...]) + (norms[2][...] + norms[3][...])
 
 
-def beams_block(reps, weights, norms, step):
+def beams_block(reps, slots, weights, norms, step):
     own = STEPS[step] == 0
     rows = ROWS if own else ROWS + NORM_ROWS
     return pl.pallas_call(
-        functools.partial(beams_kernel, slot=step),
+        functools.partial(beams_kernel, slots=slots),
         in_specs=[VMEM] * 12,
         out_specs=VMEM,
         out_shape=jax.ShapeDtypeStruct((rows, NF * COLS), f32 if own else bf16),
@@ -303,16 +305,18 @@
     rep_far, token = replicas(place, far, held, "far")
     held = join(token, held, above, below, two_away)
     swapped = lax.ppermute(held, "c", SWAP)
-    rep_both, _ = replicas(place, both, held, "both")
+    rep_both, _ = replicas(place, both, held, "both_first", (0, 1))
     halves = ((held, 0), (swapped, 0), (held, 1), (swapped, 1))
     prepared = [prepare(*half, 2 * index) for index, half in enumerate(halves)]
     weights, norms = [w for w, _ in prepared], [n for _, n in prepared]
-    reps = (rep_own, rep_near, rep_far, rep_both)
     received = []
     for step, dx in enumerate(STEPS):
         if step == 3:
             norms[0], received[0] = tie(norms[0], received[0])
-        beams = beams_block(reps, weights, norms, step)
+        if step == 1:
+            rep_both, _ = replicas(place, both, beams, "both_rest", (1, 4))
+        slots = (step, step, step, step - min(step, 1))
+        beams = beams_block((rep_own, rep_near, rep_far, rep_both), slots, weights, norms, step)
         if dx:
             received.append(lax.ppermute(beams, "x", [(i, (i + dx) % 4) for i in range(4)]))
     return finish(place, received, beams, norms, float(NF * CH * 16))

time: 75 us -> 74.8 us (level)
  Pallas kernels: 31.2 us -> 32.3 us
    ppermute x3, waiting for transfers between devices: 8.84 us -> 6.81 us  [per_device(): lax.ppermute(beams, 'x', [(i, (i + dx) % 4) for i in range(4)])]
    ppermute x1, starting transfers between devices: 2.35 us -> 0.58 us  [per_device(): swapped = lax.ppermute(held, 'c', SWAP)]
    ppermute x4, waiting for transfers between devices: 3.59 us -> 4.96 us  [along_z(): return lax.ppermute(values, 'z', [(i, target(i) % 8) for i in range(8)])]
    ppermute x4, starting transfers between devices: 9.38 us -> 10.6 us  [along_z(): return lax.ppermute(values, 'z', [(i, target(i) % 8) for i in range(8)])]
    pallas_call x4 -> x5, Pallas kernels: 17.8 us -> 18.8 us  [replicas(): pl.pallas_call(replicas_kernel, grid_spec=pltpu.PrefetchScalarGridSpec(nu...]
  transfers between devices with their start and end apart: 13 -> 13, of which waited for: 4 -> 2; matrix products, arithmetic and copies ran while one was open for 3% -> 3% of each run, Pallas kernels for 35% -> 36%
where the time goes in v10:
time: 74.8 us; the launch traced here: 74.6 us
  Pallas kernels  32.3 us (43%)
  starting transfers between devices  26.4 us (35%)
  waiting for transfers between devices  11.8 us (16%)
  other arithmetic  3.82 us (5%)
    pallas_call x5, Pallas kernels, replicas(): pl.pallas_call(replicas_kernel, grid_spec=pltpu.PrefetchScalarGridSpec(nu...  18.8 us
    ppermute x4, starting transfers between devices, along_z(): return lax.ppermute(values, 'z', [(i, target(i) % 8) for i in range(8)])  10.6 us
    pallas_call x4, Pallas kernels, beams_block(): pl.pallas_call(functools.partial(beams_kernel, slots=slots), in_specs=[VM...  9.59 us
    ppermute x3, waiting for transfers between devices, per_device(): lax.ppermute(beams, 'x', [(i, (i + dx) % 4) for i in range(4)])  6.81 us
    ppermute x3, starting transfers between devices, per_device(): lax.ppermute(beams, 'x', [(i, (i + dx) % 4) for i in range(4)])  5.77 us
    ppermute x3, starting transfers between devices, moved(): lax.ppermute(parts[flip], ('yh', 'c'), [(i, i ^ flip) for i in range(4)])  5.14 us
    ppermute x4, waiting for transfers between devices, along_z(): return lax.ppermute(values, 'z', [(i, target(i) % 8) for i in range(8)])  4.96 us
    ppermute x1, starting transfers between devices, per_device(): other = lax.ppermute(held, 'yh', SWAP)  3.83 us
  transfers between devices with their start and end apart: 13, of which 2 were waited for; matrix products, arithmetic and copies ran while one was open for 3% of the time, Pallas kernels for 36%

profile of v10, /device:TPU:1, one launch (start us, length us, event | category | flops | bytes accessed | tf_op | source)
XLA Modules:
  0.0 74.6 jit_solution(9710245625675954157)
XLA Ops:
  0.0 0.7 convert_element_type.35
  0.7 0.7 broadcast_multiply_fusion
  1.5 3.8 %collective-permute-start = (bf16[1,48,256]{2,1,0:T(8,128)(2,1)S(1)}, bf16[1,48,256]{2,1,0:T(8,128)(2,1)S(1)}, u32[]{:S(2)}, u32[]{:S(2)}) collective-permute-start(bf16[1,48,256]{2,1,0:T(8,128)(2,1)S(1)} %reshape.16.refs_0_), channel_id=1, source_target_pairs={{0,2},{2,0},{1,3},{3,1},{4,6},{6,4},{5,7},{7,5},{8,10},{10,8},{9,1... | collective-permute-start | bytes 73736 | tf_op jit(solution)/shard_map/ppermute | solution.py:292
  5.3 2.4 %fusion.3 = (s16[4,256,256]{2,1,0:T(8,128)(2,1)S(1)}, s16[4,256,256]{2,1,0:T(8,128)(2,1)S(1)}, s16[4,256,256]{2,1,0:T(8,128)(2,1)S(1)}, s16[4,256,256]{2,1,0:T(8,128)(2,1)S(1)}) fusion(s32[4,2,2,256,256]{4,3,2,1,0:T(8,128)} %bitcast.31, s32[]{:T(128)S(6)} %select_n.42, s32[]{:T(128)S(6)} %select_n.41, s32[]{:T(128)S(6)} %select_n.40, s32[]{:T(128)S(6)} %select_n.39), kind=kLoop, calls=%fused_computation.7 | loop fusion | flops 1048576 | bytes 6291472 | tf_op jit(solution)/shard_map/convert_element_type | solution.py:279
  8.3 1.9 %collective-permute-start.3 = (s16[4,256,256]{2,1,0:T(8,128)(2,1)S(1)}, s16[4,256,256]{2,1,0:T(8,128)(2,1)S(1)}, u32[]{:S(2)}, u32[]{:S(2)}) collective-permute-start(s16[4,256,256]{2,1,0:T(8,128)(2,1)S(1)} %get-tuple-element.39), channel_id=1, source_target_pairs={{0,1},{1,0},{2,3},{3,2},{4,5},{5,4},{6,7},{7,6},{8,9},{9,8},{10,11... | collective-permute-start | bytes 1572872 | tf_op jit(solution)/shard_map/ppermute | solution.py:286
  10.2 2.4 %collective-permute-start.7 = (s16[4,256,256]{2,1,0:T(8,128)(2,1)S(1)}, s16[4,256,256]{2,1,0:T(8,128)(2,1)S(1)}, u32[]{:S(2)}, u32[]{:S(2)}) collective-permute-start(s16[4,256,256]{2,1,0:T(8,128)(2,1)S(1)} %get-tuple-element.43), channel_id=1, source_target_pairs={{0,2},{1,3},{2,0},{3,1},{4,6},{5,7},{6,4},{7,5},{8,10},{9,11},{10,... | collective-permute-start | bytes 1572872 | tf_op jit(solution)/shard_map/ppermute | solution.py:286
  12.6 0.9 %collective-permute-start.8 = (s16[4,256,256]{2,1,0:T(8,128)(2,1)S(1)}, s16[4,256,256]{2,1,0:T(8,128)(2,1)S(1)}, u32[]{:S(2)}, u32[]{:S(2)}) collective-permute-start(s16[4,256,256]{2,1,0:T(8,128)(2,1)S(1)} %get-tuple-element.49), channel_id=1, source_target_pairs={{0,3},{1,2},{2,1},{3,0},{4,7},{5,6},{6,5},{7,4},{8,11},{9,10},{10,... | collective-permute-start | bytes 1572872 | tf_op jit(solution)/shard_map/ppermute | solution.py:286
  13.5 6.6 %collective-permute-start.2 = (bf16[4,48,256]{2,1,0:T(8,128)(2,1)S(1)}, bf16[4,48,256]{2,1,0:T(8,128)(2,1)S(1)}, u32[]{:S(2)}, u32[]{:S(2)}) collective-permute-start(bf16[4,48,256]{2,1,0:T(8,128)(2,1)S(1)} %join_2.1.after_ref.refs_0_), channel_id=1, source_target_pairs={{0,128},{32,160},{64,192},{96,224},{128,0},{160,32},{192,64},{224,... | collective-permute-start | bytes 294920 | tf_op jit(solution)/shard_map/ppermute | solution.py:289
  20.1 4.3 %replicas_own.1 = (bf16[4,8,256,512]{3,2,1,0:T(8,128)(2,1)S(1)}, s32[8,128]{1,0:T(8,128)S(1)}) custom-call(s32[6]{0:T(128)S(1)} %stack.27.place, s16[4,256,256]{2,1,0:T(8,128)(2,1)S(1)} %get-tuple-element.40.travel_ref, bf16[4,48,256]{2,1,0:T(8,128)(2,1)S(1)} %join_2.1.after_ref.refs_0_), custom_call_target="tpu_custom_call" | custom-call | flops 40000000000 | bytes 1000000 | tf_op jit(solution)/shard_map/replicas_own/pallas_call | solution.py:110
  24.5 4.3 %replicas_near.1 = (bf16[4,8,256,512]{3,2,1,0:T(8,128)(2,1)S(1)}, s32[8,128]{1,0:T(8,128)S(1)}) custom-call(s32[6]{0:T(128)S(1)} %stack.27.place, s16[4,256,256]{2,1,0:T(8,128)(2,1)S(1)} %collective-permute-done.3.travel_ref, s32[8,128]{1,0:T(8,128)S(1)} %get-tuple-element.41.after_ref), custom_call_target="tpu_custom_call" | custom-call | flops 40000000000 | bytes 1000000 | tf_op jit(solution)/shard_map/replicas_near/pallas_call | solution.py:110
  28.8 1.3 %collective-permute-start.6 = (bf16[8,48,256]{2,1,0:T(8,128)(2,1)S(1)}, bf16[8,48,256]{2,1,0:T(8,128)(2,1)S(1)}, u32[]{:S(2)}, u32[]{:S(2)}) collective-permute-start(bf16[8,48,256]{2,1,0:T(8,128)(2,1)S(1)} %join_4.1.after_ref.refs_0_), channel_id=1, source_target_pairs={{0,64},{32,224},{64,128},{96,32},{128,192},{160,96},{192,0},{224,1... | collective-permute-start | bytes 589832 | tf_op jit(solution)/shard_map/ppermute | solution.py:289
  30.1 2.7 %collective-permute-start.4 = (bf16[8,48,256]{2,1,0:T(8,128)(2,1)S(1)}, bf16[8,48,256]{2,1,0:T(8,128)(2,1)S(1)}, u32[]{:S(2)}, u32[]{:S(2)}) collective-permute-start(bf16[8,48,256]{2,1,0:T(8,128)(2,1)S(1)} %join_4.1.after_ref.refs_0_), channel_id=1, source_target_pairs={{0,224},{32,0},{64,32},{96,64},{128,96},{160,128},{192,160},{224,1... | collective-permute-start | bytes 589832 | tf_op jit(solution)/shard_map/ppermute | solution.py:289
  32.8 4.3 %replicas_far.1 = (bf16[4,8,256,512]{3,2,1,0:T(8,128)(2,1)S(1)}, s32[8,128]{1,0:T(8,128)S(1)}) custom-call(s32[6]{0:T(128)S(1)} %stack.27.place, s16[4,256,256]{2,1,0:T(8,128)(2,1)S(1)} %collective-permute-done.7.travel_ref, bf16[8,48,256]{2,1,0:T(8,128)(2,1)S(1)} %join_4.1.after_ref.refs_0_), custom_call_target="tpu_custom_call" | custom-call | flops 40000000000 | bytes 1000000 | tf_op jit(solution)/shard_map/replicas_far/pallas_call | solution.py:110
  37.1 5.0 %collective-permute-done.5.refs_2_ = bf16[8,48,256]{2,1,0:T(8,128)(2,1)S(1)} collective-permute-done((bf16[8,48,256]{2,1,0:T(8,128)(2,1)S(1)}, bf16[8,48,256]{2,1,0:T(8,128)(2,1)S(1)}, u32[]{:S(2)}, u32[]{:S(2)}) %collective-permute-start.5) | collective-permute-done | bytes 196640 | tf_op jit(solution)/shard_map/ppermute | solution.py:289
  42.7 2.0 %replicas_both_first.1 = (bf16[1,8,256,512]{3,2,1,0:T(8,128)(2,1)S(1)}, s32[8,128]{1,0:T(8,128)}) custom-call(s32[6]{0:T(128)S(1)} %stack.27.place, s16[4,256,256]{2,1,0:T(8,128)(2,1)S(1)} %collective-permute-done.8.travel_ref, bf16[32,48,256]{2,1,0:T(8,128)(2,1)S(1)} %join_8.1.source_ref.after_ref), custom_call_target="tpu_custom_call" | custom-call | flops 40000000000 | bytes 1000000 | tf_op jit(solution)/shard_map/replicas_both_first/pallas_call | solution.py:110
  46.5 2.4 %beams_0.1.after_ref = bf16[264,768]{1,0:T(8,128)(2,1)S(1)} custom-call(bf16[4,8,256,512]{3,2,1,0:T(8,128)(2,1)S(1)} %get-tuple-element.46.refs_0_, bf16[4,8,256,512]{3,2,1,0:T(8,128)(2,1)S(1)} %get-tuple-element.47.refs_1_, bf16[4,8,256,512]{3,2,1,0:T(8,128)(2,1)S(1)} %get-tuple-element.48.refs_2_, bf16[1,8,256,512]{3,2,1,0:T(8,128)(2,1)S(1)} %get-tuple-element.50.refs_3_, ...), custom_call_target="tpu_custom_call" | custom-call | flops 3000000000 | bytes 1000000 | tf_op jit(solution)/shard_map/beams_0/pallas_call | solution.py:162
  48.9 3.0 %collective-permute-start.10 = (bf16[264,768]{1,0:T(8,128)(2,1)S(1)}, bf16[264,768]{1,0:T(8,128)(2,1)S(1)}, u32[]{:S(2)}, u32[]{:S(2)}) collective-permute-start(bf16[264,768]{1,0:T(8,128)(2,1)S(1)} %beams_0.1.after_ref), channel_id=1, source_target_pairs={{0,8},{4,12},{8,0},{12,4},{1,9},{5,13},{9,1},{13,5},{2,10},{6,14},... | collective-permute-start | bytes 1216520 | tf_op jit(solution)/shard_map/ppermute | solution.py:321
  51.9 4.0 %replicas_both_rest.1 = (bf16[3,8,256,512]{3,2,1,0:T(8,128)(2,1)S(1)}, s32[8,128]{1,0:T(8,128)}) custom-call(s32[6]{0:T(128)S(1)} %stack.27.place, s16[4,256,256]{2,1,0:T(8,128)(2,1)S(1)} %collective-permute-done.8.travel_ref, bf16[264,768]{1,0:T(8,128)(2,1)S(1)} %beams_0.1.after_ref), custom_call_target="tpu_custom_call" | custom-call | flops 40000000000 | bytes 1000000 | tf_op jit(solution)/shard_map/replicas_both_rest/pallas_call | solution.py:110
  55.9 2.4 %beams_2.1 = bf16[264,768]{1,0:T(8,128)(2,1)S(1)} custom-call(bf16[4,8,256,512]{3,2,1,0:T(8,128)(2,1)S(1)} %get-tuple-element.46.refs_0_, bf16[4,8,256,512]{3,2,1,0:T(8,128)(2,1)S(1)} %get-tuple-element.47.refs_1_, bf16[4,8,256,512]{3,2,1,0:T(8,128)(2,1)S(1)} %get-tuple-element.48.refs_2_, bf16[3,8,256,512]{3,2,1,0:T(8,128)(2,1)S(1)} %get-tuple-element.59.refs_3_, ...), custom_call_target="tpu_custom_call" | custom-call | flops 3000000000 | bytes 1000000 | tf_op jit(solution)/shard_map/beams_2/pallas_call | solution.py:162
  58.3 2.4 %beams_1.1 = bf16[264,768]{1,0:T(8,128)(2,1)S(1)} custom-call(bf16[4,8,256,512]{3,2,1,0:T(8,128)(2,1)S(1)} %get-tuple-element.46.refs_0_, bf16[4,8,256,512]{3,2,1,0:T(8,128)(2,1)S(1)} %get-tuple-element.47.refs_1_, bf16[4,8,256,512]{3,2,1,0:T(8,128)(2,1)S(1)} %get-tuple-element.48.refs_2_, bf16[3,8,256,512]{3,2,1,0:T(8,128)(2,1)S(1)} %get-tuple-element.59.refs_3_, ...), custom_call_target="tpu_custom_call" | custom-call | flops 3000000000 | bytes 1000000 | tf_op jit(solution)/shard_map/beams_1/pallas_call | solution.py:162
  61.1 2.4 %collective-permute-start.12 = (bf16[264,768]{1,0:T(8,128)(2,1)S(1)}, bf16[264,768]{1,0:T(8,128)(2,1)S(1)}, u32[]{:S(2)}, u32[]{:S(2)}) collective-permute-start(bf16[264,768]{1,0:T(8,128)(2,1)S(1)} %beams_2.1), channel_id=1, source_target_pairs={{0,12},{4,0},{8,4},{12,8},{1,13},{5,1},{9,5},{13,9},{2,14},{6,2},{... | collective-permute-start | bytes 1216520 | tf_op jit(solution)/shard_map/ppermute | solution.py:321
  63.4 2.4 %beams_3.1.refs_3_ = f32[256,768]{1,0:T(8,128)S(1)} custom-call(bf16[4,8,256,512]{3,2,1,0:T(8,128)(2,1)S(1)} %get-tuple-element.46.refs_0_, bf16[4,8,256,512]{3,2,1,0:T(8,128)(2,1)S(1)} %get-tuple-element.47.refs_1_, bf16[4,8,256,512]{3,2,1,0:T(8,128)(2,1)S(1)} %get-tuple-element.48.refs_2_, bf16[3,8,256,512]{3,2,1,0:T(8,128)(2,1)S(1)} %get-tuple-element.59.refs_3_, ...), custom_call_target="tpu_custom_call" | custom-call | flops 3000000000 | bytes 1000000 | tf_op jit(solution)/shard_map/beams_3/pallas_call | solution.py:162
  65.8 6.8 %collective-permute-done.11.refs_1_ = bf16[264,768]{1,0:T(8,128)(2,1)S(1)} collective-permute-done((bf16[264,768]{1,0:T(8,128)(2,1)S(1)}, bf16[264,768]{1,0:T(8,128)(2,1)S(1)}, u32[]{:S(2)}, u32[]{:S(2)}) %collective-permute-start.11) | collective-permute-done | bytes 405536 | tf_op jit(solution)/shard_map/ppermute | solution.py:321
  72.7 2.0 %finish.1 = f32[48,256]{1,0:T(8,128)} custom-call(s32[6]{0:T(128)S(1)} %stack.27.place, bf16[264,768]{1,0:T(8,128)(2,1)S(1)} %collective-permute-done.10.refs_0_, bf16[264,768]{1,0:T(8,128)(2,1)S(1)} %collective-permute-done.11.refs_1_, bf16[264,768]{1,0:T(8,128)(2,1)S(1)} %collective-permute-done.12.refs_2_, f32[256,768]{1,0:T(8,128)S(1)} %beams_3.1.refs_3_, ...), custom_call_target="tpu_custom_call" | custom-call | tf_op jit(solution)/shard_map/finish/pallas_call | solution.py:252
  (28 shorter events, 3.5 us)
Async XLA Ops:
  1.5 6.4 %collective-permute-start = (bf16[1,48,256]{2,1,0:T(8,128)(2,1)S(1)}, bf16[1,48,256]{2,1,0:T(8,128)(2,1)S(1)}, u32[]{:S(2)}, u32[]{:S(2)}) collective-permute-start(bf16[1,48,256]{2,1,0:T(8,128)(2,1)S(1)} %reshape.16.refs_0_), channel_id=1, source_target_pairs={{0,2},{2,0},{1,3},{3,1},{4,6},{6,4},{5,7},{7,5},{8,10},{10,8},{9,1... | collective-permute-start | bytes 73736 | tf_op jit(solution)/shard_map/ppermute | solution.py:292
  7.8 5.6 %collective-permute-start.1 = (bf16[2,48,256]{2,1,0:T(8,128)(2,1)S(1)}, bf16[2,48,256]{2,1,0:T(8,128)(2,1)S(1)}, u32[]{:S(2)}, u32[]{:S(2)}) collective-permute-start(bf16[2,48,256]{2,1,0:T(8,128)(2,1)S(1)} %join_1.1.refs_0_), channel_id=1, source_target_pairs={{0,16},{16,0},{1,17},{17,1},{2,18},{18,2},{3,19},{19,3},{4,20},{20... | collective-permute-start | bytes 147464 | tf_op jit(solution)/shard_map/ppermute | solution.py:296
  8.3 16.1 %collective-permute-start.3 = (s16[4,256,256]{2,1,0:T(8,128)(2,1)S(1)}, s16[4,256,256]{2,1,0:T(8,128)(2,1)S(1)}, u32[]{:S(2)}, u32[]{:S(2)}) collective-permute-start(s16[4,256,256]{2,1,0:T(8,128)(2,1)S(1)} %get-tuple-element.39), channel_id=1, source_target_pairs={{0,1},{1,0},{2,3},{3,2},{4,5},{5,4},{6,7},{7,6},{8,9},{9,8},{10,11... | collective-permute-start | bytes 1572872 | tf_op jit(solution)/shard_map/ppermute | solution.py:286
  10.2 22.5 %collective-permute-start.7 = (s16[4,256,256]{2,1,0:T(8,128)(2,1)S(1)}, s16[4,256,256]{2,1,0:T(8,128)(2,1)S(1)}, u32[]{:S(2)}, u32[]{:S(2)}) collective-permute-start(s16[4,256,256]{2,1,0:T(8,128)(2,1)S(1)} %get-tuple-element.43), channel_id=1, source_target_pairs={{0,2},{1,3},{2,0},{3,1},{4,6},{5,7},{6,4},{7,5},{8,10},{9,11},{10,... | collective-permute-start | bytes 1572872 | tf_op jit(solution)/shard_map/ppermute | solution.py:286
  12.6 30.1 %collective-permute-start.8 = (s16[4,256,256]{2,1,0:T(8,128)(2,1)S(1)}, s16[4,256,256]{2,1,0:T(8,128)(2,1)S(1)}, u32[]{:S(2)}, u32[]{:S(2)}) collective-permute-start(s16[4,256,256]{2,1,0:T(8,128)(2,1)S(1)} %get-tuple-element.49), channel_id=1, source_target_pairs={{0,3},{1,2},{2,1},{3,0},{4,7},{5,6},{6,5},{7,4},{8,11},{9,10},{10,... | collective-permute-start | bytes 1572872 | tf_op jit(solution)/shard_map/ppermute | solution.py:286
  13.5 15.3 %collective-permute-start.2 = (bf16[4,48,256]{2,1,0:T(8,128)(2,1)S(1)}, bf16[4,48,256]{2,1,0:T(8,128)(2,1)S(1)}, u32[]{:S(2)}, u32[]{:S(2)}) collective-permute-start(bf16[4,48,256]{2,1,0:T(8,128)(2,1)S(1)} %join_2.1.after_ref.refs_0_), channel_id=1, source_target_pairs={{0,128},{32,160},{64,192},{96,224},{128,0},{160,32},{192,64},{224,... | collective-permute-start | bytes 294920 | tf_op jit(solution)/shard_map/ppermute | solution.py:289
  28.8 8.3 %collective-permute-start.6 = (bf16[8,48,256]{2,1,0:T(8,128)(2,1)S(1)}, bf16[8,48,256]{2,1,0:T(8,128)(2,1)S(1)}, u32[]{:S(2)}, u32[]{:S(2)}) collective-permute-start(bf16[8,48,256]{2,1,0:T(8,128)(2,1)S(1)} %join_4.1.after_ref.refs_0_), channel_id=1, source_target_pairs={{0,64},{32,224},{64,128},{96,32},{128,192},{160,96},{192,0},{224,1... | collective-permute-start | bytes 589832 | tf_op jit(solution)/shard_map/ppermute | solution.py:289
  30.1 12.0 %collective-permute-start.5 = (bf16[8,48,256]{2,1,0:T(8,128)(2,1)S(1)}, bf16[8,48,256]{2,1,0:T(8,128)(2,1)S(1)}, u32[]{:S(2)}, u32[]{:S(2)}) collective-permute-start(bf16[8,48,256]{2,1,0:T(8,128)(2,1)S(1)} %join_4.1.after_ref.refs_0_), channel_id=1, source_target_pairs={{0,32},{32,64},{64,96},{96,128},{128,160},{160,192},{192,224},{224... | collective-permute-start | bytes 589832 | tf_op jit(solution)/shard_map/ppermute | solution.py:289
  30.1 12.0 %collective-permute-start.4 = (bf16[8,48,256]{2,1,0:T(8,128)(2,1)S(1)}, bf16[8,48,256]{2,1,0:T(8,128)(2,1)S(1)}, u32[]{:S(2)}, u32[]{:S(2)}) collective-permute-start(bf16[8,48,256]{2,1,0:T(8,128)(2,1)S(1)} %join_4.1.after_ref.refs_0_), channel_id=1, source_target_pairs={{0,224},{32,0},{64,32},{96,64},{128,96},{160,128},{192,160},{224,1... | collective-permute-start | bytes 589832 | tf_op jit(solution)/shard_map/ppermute | solution.py:289
  42.1 3.5 %collective-permute-start.9 = (bf16[32,48,256]{2,1,0:T(8,128)(2,1)S(1)}, bf16[32,48,256]{2,1,0:T(8,128)(2,1)S(1)}, u32[]{:S(2)}, u32[]{:S(2)}) collective-permute-start(bf16[32,48,256]{2,1,0:T(8,128)(2,1)S(1)} %join_8.1.source_ref.after_ref), channel_id=1, source_target_pairs={{0,1},{1,0},{2,3},{3,2},{4,5},{5,4},{6,7},{7,6},{8,9},{9,8},{10,11... | collective-permute-start | bytes 2359304 | tf_op jit(solution)/shard_map/ppermute | solution.py:307
  48.9 14.5 %collective-permute-start.10 = (bf16[264,768]{1,0:T(8,128)(2,1)S(1)}, bf16[264,768]{1,0:T(8,128)(2,1)S(1)}, u32[]{:S(2)}, u32[]{:S(2)}) collective-permute-start(bf16[264,768]{1,0:T(8,128)(2,1)S(1)} %beams_0.1.after_ref), channel_id=1, source_target_pairs={{0,8},{4,12},{8,0},{12,4},{1,9},{5,13},{9,1},{13,5},{2,10},{6,14},... | collective-permute-start | bytes 1216520 | tf_op jit(solution)/shard_map/ppermute | solution.py:321
  60.7 12.0 %copy-start = (s32[4,768]{1,0:T(4,128)S(1)}, s32[4,768]{1,0:T(4,128)}, u32[]{:S(2)}) copy-start(s32[4,768]{1,0:T(4,128)} %constant.54.clone.refs_8_) | copy-start | bytes 36868
  60.7 12.0 %collective-permute-start.11 = (bf16[264,768]{1,0:T(8,128)(2,1)S(1)}, bf16[264,768]{1,0:T(8,128)(2,1)S(1)}, u32[]{:S(2)}, u32[]{:S(2)}) collective-permute-start(bf16[264,768]{1,0:T(8,128)(2,1)S(1)} %beams_1.1), channel_id=1, source_target_pairs={{0,4},{4,8},{8,12},{12,0},{1,5},{5,9},{9,13},{13,1},{2,6},{6,10},{... | collective-permute-start | bytes 1216520 | tf_op jit(solution)/shard_map/ppermute | solution.py:321
  61.1 11.6 %collective-permute-start.12 = (bf16[264,768]{1,0:T(8,128)(2,1)S(1)}, bf16[264,768]{1,0:T(8,128)(2,1)S(1)}, u32[]{:S(2)}, u32[]{:S(2)}) collective-permute-start(bf16[264,768]{1,0:T(8,128)(2,1)S(1)} %beams_2.1), channel_id=1, source_target_pairs={{0,12},{4,0},{8,4},{12,8},{1,13},{5,1},{9,5},{13,9},{2,14},{6,2},{... | collective-permute-start | bytes 1216520 | tf_op jit(solution)/shard_map/ppermute | solution.py:321

commit v11 on v10

--- a/solution.py
+++ b/solution.py
@@ -292,9 +292,11 @@
     other = lax.ppermute(held, "yh", SWAP)
     held = join(other, held, other)
     held, *parts = tie(held, *parts)
-    far, near, both = moved(2), moved(1), moved(3)
+    far, both = moved(2), moved(3)
     other = lax.ppermute(held, "yl", SWAP)
     held = join(other, held, other)
+    held, parts[1] = tie(held, parts[1])
+    near = moved(1)
     other = along_z(held, lambda i: i ^ 4)
     rep_own, token = replicas(place, parts[0], held, "own")
     rep_near, token = replicas(place, near, token, "near")

time: 74.8 us -> 75.3 us (level)
  transfers between devices with their start and end apart: 13 -> 13, of which waited for: 2 -> 3; matrix products, arithmetic and copies ran while one was open for 3% -> 3% of each run, Pallas kernels for 36% -> 36%
where the time goes in v11:
time: 75.3 us; the launch traced here: 75.2 us
  Pallas kernels  32.3 us (43%)
  starting transfers between devices  26.9 us (36%)
  waiting for transfers between devices  11.8 us (16%)
  other arithmetic  3.82 us (5%)
    pallas_call x5, Pallas kernels, replicas(): pl.pallas_call(replicas_kernel, grid_spec=pltpu.PrefetchScalarGridSpec(nu...  18.8 us
    ppermute x4, starting transfers between devices, along_z(): return lax.ppermute(values, 'z', [(i, target(i) % 8) for i in range(8)])  10.7 us
    pallas_call x4, Pallas kernels, beams_block(): pl.pallas_call(functools.partial(beams_kernel, slots=slots), in_specs=[VM...  9.58 us
    ppermute x3, waiting for transfers between devices, per_device(): lax.ppermute(beams, 'x', [(i, (i + dx) % 4) for i in range(4)])  6.78 us
    ppermute x3, starting transfers between devices, per_device(): lax.ppermute(beams, 'x', [(i, (i + dx) % 4) for i in range(4)])  5.77 us
    ppermute x3, starting transfers between devices, moved(): lax.ppermute(parts[flip], ('yh', 'c'), [(i, i ^ flip) for i in range(4)])  5.62 us
    ppermute x4, waiting for transfers between devices, along_z(): return lax.ppermute(values, 'z', [(i, target(i) % 8) for i in range(8)])  4.99 us
    ppermute x1, starting transfers between devices, per_device(): other = lax.ppermute(held, 'yh', SWAP)  3.83 us
  transfers between devices with their start and end apart: 13, of which 3 were waited for; matrix products, arithmetic and copies ran while one was open for 3% of the time, Pallas kernels for 36%

profile of v11, /device:TPU:1, one launch (start us, length us, event | category | flops | bytes accessed | tf_op | source)
XLA Modules:
  0.0 75.2 jit_solution(10635196171534054012)
XLA Ops:
  0.0 0.7 convert_element_type.35
  0.7 0.7 broadcast_multiply_fusion
  1.5 3.8 %collective-permute-start = (bf16[1,48,256]{2,1,0:T(8,128)(2,1)S(1)}, bf16[1,48,256]{2,1,0:T(8,128)(2,1)S(1)}, u32[]{:S(2)}, u32[]{:S(2)}) collective-permute-start(bf16[1,48,256]{2,1,0:T(8,128)(2,1)S(1)} %reshape.16.refs_0_), channel_id=1, source_target_pairs={{0,2},{2,0},{1,3},{3,1},{4,6},{6,4},{5,7},{7,5},{8,10},{10,8},{9,1... | collective-permute-start | bytes 73736 | tf_op jit(solution)/shard_map/ppermute | solution.py:292
  5.3 2.4 %fusion.3 = (s16[4,256,256]{2,1,0:T(8,128)(2,1)S(1)}, s16[4,256,256]{2,1,0:T(8,128)(2,1)S(1)}, s16[4,256,256]{2,1,0:T(8,128)(2,1)S(1)}, s16[4,256,256]{2,1,0:T(8,128)(2,1)S(1)}) fusion(s32[4,2,2,256,256]{4,3,2,1,0:T(8,128)} %bitcast.31, s32[]{:T(128)S(6)} %select_n.42, s32[]{:T(128)S(6)} %select_n.41, s32[]{:T(128)S(6)} %select_n.40, s32[]{:T(128)S(6)} %select_n.39), kind=kLoop, calls=%fused_computation.7 | loop fusion | flops 1048576 | bytes 6291472 | tf_op jit(solution)/shard_map/convert_element_type | solution.py:279
  8.3 2.2 %collective-permute-start.7 = (s16[4,256,256]{2,1,0:T(8,128)(2,1)S(1)}, s16[4,256,256]{2,1,0:T(8,128)(2,1)S(1)}, u32[]{:S(2)}, u32[]{:S(2)}) collective-permute-start(s16[4,256,256]{2,1,0:T(8,128)(2,1)S(1)} %get-tuple-element.47), channel_id=1, source_target_pairs={{0,2},{1,3},{2,0},{3,1},{4,6},{5,7},{6,4},{7,5},{8,10},{9,11},{10,... | collective-permute-start | bytes 1572872 | tf_op jit(solution)/shard_map/ppermute | solution.py:286
  10.5 2.9 %collective-permute-start.8 = (s16[4,256,256]{2,1,0:T(8,128)(2,1)S(1)}, s16[4,256,256]{2,1,0:T(8,128)(2,1)S(1)}, u32[]{:S(2)}, u32[]{:S(2)}) collective-permute-start(s16[4,256,256]{2,1,0:T(8,128)(2,1)S(1)} %get-tuple-element.53), channel_id=1, source_target_pairs={{0,3},{1,2},{2,1},{3,0},{4,7},{5,6},{6,5},{7,4},{8,11},{9,10},{10,... | collective-permute-start | bytes 1572872 | tf_op jit(solution)/shard_map/ppermute | solution.py:286
  13.4 6.7 %collective-permute-start.2 = (bf16[4,48,256]{2,1,0:T(8,128)(2,1)S(1)}, bf16[4,48,256]{2,1,0:T(8,128)(2,1)S(1)}, u32[]{:S(2)}, u32[]{:S(2)}) collective-permute-start(bf16[4,48,256]{2,1,0:T(8,128)(2,1)S(1)} %join_2.1.after_ref.refs_0_), channel_id=1, source_target_pairs={{0,128},{32,160},{64,192},{96,224},{128,0},{160,32},{192,64},{224,... | collective-permute-start | bytes 294920 | tf_op jit(solution)/shard_map/ppermute | solution.py:289
  20.1 0.6 collective-permute-start.3
  20.7 4.3 %replicas_own.1 = (bf16[4,8,256,512]{3,2,1,0:T(8,128)(2,1)S(1)}, s32[8,128]{1,0:T(8,128)S(1)}) custom-call(s32[6]{0:T(128)S(1)} %stack.27.place, s16[4,256,256]{2,1,0:T(8,128)(2,1)S(1)} %get-tuple-element.44.travel_ref, bf16[4,48,256]{2,1,0:T(8,128)(2,1)S(1)} %join_2.1.after_ref.refs_0_), custom_call_target="tpu_custom_call" | custom-call | flops 40000000000 | bytes 1000000 | tf_op jit(solution)/shard_map/replicas_own/pallas_call | solution.py:110
  25.0 4.3 %replicas_near.1 = (bf16[4,8,256,512]{3,2,1,0:T(8,128)(2,1)S(1)}, s32[8,128]{1,0:T(8,128)S(1)}) custom-call(s32[6]{0:T(128)S(1)} %stack.27.place, s16[4,256,256]{2,1,0:T(8,128)(2,1)S(1)} %collective-permute-done.3.travel_ref, s32[8,128]{1,0:T(8,128)S(1)} %get-tuple-element.45.after_ref), custom_call_target="tpu_custom_call" | custom-call | flops 40000000000 | bytes 1000000 | tf_op jit(solution)/shard_map/replicas_near/pallas_call | solution.py:110
  29.4 1.3 %collective-permute-start.6 = (bf16[8,48,256]{2,1,0:T(8,128)(2,1)S(1)}, bf16[8,48,256]{2,1,0:T(8,128)(2,1)S(1)}, u32[]{:S(2)}, u32[]{:S(2)}) collective-permute-start(bf16[8,48,256]{2,1,0:T(8,128)(2,1)S(1)} %join_4.1.after_ref.refs_0_), channel_id=1, source_target_pairs={{0,64},{32,224},{64,128},{96,32},{128,192},{160,96},{192,0},{224,1... | collective-permute-start | bytes 589832 | tf_op jit(solution)/shard_map/ppermute | solution.py:289
  30.7 2.7 %collective-permute-start.4 = (bf16[8,48,256]{2,1,0:T(8,128)(2,1)S(1)}, bf16[8,48,256]{2,1,0:T(8,128)(2,1)S(1)}, u32[]{:S(2)}, u32[]{:S(2)}) collective-permute-start(bf16[8,48,256]{2,1,0:T(8,128)(2,1)S(1)} %join_4.1.after_ref.refs_0_), channel_id=1, source_target_pairs={{0,224},{32,0},{64,32},{96,64},{128,96},{160,128},{192,160},{224,1... | collective-permute-start | bytes 589832 | tf_op jit(solution)/shard_map/ppermute | solution.py:289
  33.3 4.3 %replicas_far.1 = (bf16[4,8,256,512]{3,2,1,0:T(8,128)(2,1)S(1)}, s32[8,128]{1,0:T(8,128)S(1)}) custom-call(s32[6]{0:T(128)S(1)} %stack.27.place, s16[4,256,256]{2,1,0:T(8,128)(2,1)S(1)} %collective-permute-done.7.travel_ref, bf16[8,48,256]{2,1,0:T(8,128)(2,1)S(1)} %join_4.1.after_ref.refs_0_), custom_call_target="tpu_custom_call" | custom-call | flops 40000000000 | bytes 1000000 | tf_op jit(solution)/shard_map/replicas_far/pallas_call | solution.py:110
  38.1 4.5 %collective-permute-done.5.refs_2_ = bf16[8,48,256]{2,1,0:T(8,128)(2,1)S(1)} collective-permute-done((bf16[8,48,256]{2,1,0:T(8,128)(2,1)S(1)}, bf16[8,48,256]{2,1,0:T(8,128)(2,1)S(1)}, u32[]{:S(2)}, u32[]{:S(2)}) %collective-permute-start.5) | collective-permute-done | bytes 196640 | tf_op jit(solution)/shard_map/ppermute | solution.py:289
  43.2 2.0 %replicas_both_first.1 = (bf16[1,8,256,512]{3,2,1,0:T(8,128)(2,1)S(1)}, s32[8,128]{1,0:T(8,128)}) custom-call(s32[6]{0:T(128)S(1)} %stack.27.place, s16[4,256,256]{2,1,0:T(8,128)(2,1)S(1)} %collective-permute-done.8.travel_ref, bf16[32,48,256]{2,1,0:T(8,128)(2,1)S(1)} %join_8.1.source_ref.after_ref), custom_call_target="tpu_custom_call" | custom-call | flops 40000000000 | bytes 1000000 | tf_op jit(solution)/shard_map/replicas_both_first/pallas_call | solution.py:110
  47.1 2.4 %beams_0.1.after_ref = bf16[264,768]{1,0:T(8,128)(2,1)S(1)} custom-call(bf16[4,8,256,512]{3,2,1,0:T(8,128)(2,1)S(1)} %get-tuple-element.50.refs_0_, bf16[4,8,256,512]{3,2,1,0:T(8,128)(2,1)S(1)} %get-tuple-element.51.refs_1_, bf16[4,8,256,512]{3,2,1,0:T(8,128)(2,1)S(1)} %get-tuple-element.52.refs_2_, bf16[1,8,256,512]{3,2,1,0:T(8,128)(2,1)S(1)} %get-tuple-element.54.refs_3_, ...), custom_call_target="tpu_custom_call" | custom-call | flops 3000000000 | bytes 1000000 | tf_op jit(solution)/shard_map/beams_0/pallas_call | solution.py:162
  49.5 3.0 %collective-permute-start.10 = (bf16[264,768]{1,0:T(8,128)(2,1)S(1)}, bf16[264,768]{1,0:T(8,128)(2,1)S(1)}, u32[]{:S(2)}, u32[]{:S(2)}) collective-permute-start(bf16[264,768]{1,0:T(8,128)(2,1)S(1)} %beams_0.1.after_ref), channel_id=1, source_target_pairs={{0,8},{4,12},{8,0},{12,4},{1,9},{5,13},{9,1},{13,5},{2,10},{6,14},... | collective-permute-start | bytes 1216520 | tf_op jit(solution)/shard_map/ppermute | solution.py:323
  52.5 4.0 %replicas_both_rest.1 = (bf16[3,8,256,512]{3,2,1,0:T(8,128)(2,1)S(1)}, s32[8,128]{1,0:T(8,128)}) custom-call(s32[6]{0:T(128)S(1)} %stack.27.place, s16[4,256,256]{2,1,0:T(8,128)(2,1)S(1)} %collective-permute-done.8.travel_ref, bf16[264,768]{1,0:T(8,128)(2,1)S(1)} %beams_0.1.after_ref), custom_call_target="tpu_custom_call" | custom-call | flops 40000000000 | bytes 1000000 | tf_op jit(solution)/shard_map/replicas_both_rest/pallas_call | solution.py:110
  56.5 2.4 %beams_2.1 = bf16[264,768]{1,0:T(8,128)(2,1)S(1)} custom-call(bf16[4,8,256,512]{3,2,1,0:T(8,128)(2,1)S(1)} %get-tuple-element.50.refs_0_, bf16[4,8,256,512]{3,2,1,0:T(8,128)(2,1)S(1)} %get-tuple-element.51.refs_1_, bf16[4,8,256,512]{3,2,1,0:T(8,128)(2,1)S(1)} %get-tuple-element.52.refs_2_, bf16[3,8,256,512]{3,2,1,0:T(8,128)(2,1)S(1)} %get-tuple-element.63.refs_3_, ...), custom_call_target="tpu_custom_call" | custom-call | flops 3000000000 | bytes 1000000 | tf_op jit(solution)/shard_map/beams_2/pallas_call | solution.py:162
  58.8 2.4 %beams_1.1 = bf16[264,768]{1,0:T(8,128)(2,1)S(1)} custom-call(bf16[4,8,256,512]{3,2,1,0:T(8,128)(2,1)S(1)} %get-tuple-element.50.refs_0_, bf16[4,8,256,512]{3,2,1,0:T(8,128)(2,1)S(1)} %get-tuple-element.51.refs_1_, bf16[4,8,256,512]{3,2,1,0:T(8,128)(2,1)S(1)} %get-tuple-element.52.refs_2_, bf16[3,8,256,512]{3,2,1,0:T(8,128)(2,1)S(1)} %get-tuple-element.63.refs_3_, ...), custom_call_target="tpu_custom_call" | custom-call | flops 3000000000 | bytes 1000000 | tf_op jit(solution)/shard_map/beams_1/pallas_call | solution.py:162
  61.6 2.4 %collective-permute-start.12 = (bf16[264,768]{1,0:T(8,128)(2,1)S(1)}, bf16[264,768]{1,0:T(8,128)(2,1)S(1)}, u32[]{:S(2)}, u32[]{:S(2)}) collective-permute-start(bf16[264,768]{1,0:T(8,128)(2,1)S(1)} %beams_2.1), channel_id=1, source_target_pairs={{0,12},{4,0},{8,4},{12,8},{1,13},{5,1},{9,5},{13,9},{2,14},{6,2},{... | collective-permute-start | bytes 1216520 | tf_op jit(solution)/shard_map/ppermute | solution.py:323
  64.0 2.4 %beams_3.1.refs_3_ = f32[256,768]{1,0:T(8,128)S(1)} custom-call(bf16[4,8,256,512]{3,2,1,0:T(8,128)(2,1)S(1)} %get-tuple-element.50.refs_0_, bf16[4,8,256,512]{3,2,1,0:T(8,128)(2,1)S(1)} %get-tuple-element.51.refs_1_, bf16[4,8,256,512]{3,2,1,0:T(8,128)(2,1)S(1)} %get-tuple-element.52.refs_2_, bf16[3,8,256,512]{3,2,1,0:T(8,128)(2,1)S(1)} %get-tuple-element.63.refs_3_, ...), custom_call_target="tpu_custom_call" | custom-call | flops 3000000000 | bytes 1000000 | tf_op jit(solution)/shard_map/beams_3/pallas_call | solution.py:162
  66.4 6.8 %collective-permute-done.11.refs_1_ = bf16[264,768]{1,0:T(8,128)(2,1)S(1)} collective-permute-done((bf16[264,768]{1,0:T(8,128)(2,1)S(1)}, bf16[264,768]{1,0:T(8,128)(2,1)S(1)}, u32[]{:S(2)}, u32[]{:S(2)}) %collective-permute-start.11) | collective-permute-done | bytes 405536 | tf_op jit(solution)/shard_map/ppermute | solution.py:323
  73.2 2.0 %finish.1 = f32[48,256]{1,0:T(8,128)} custom-call(s32[6]{0:T(128)S(1)} %stack.27.place, bf16[264,768]{1,0:T(8,128)(2,1)S(1)} %collective-permute-done.10.refs_0_, bf16[264,768]{1,0:T(8,128)(2,1)S(1)} %collective-permute-done.11.refs_1_, bf16[264,768]{1,0:T(8,128)(2,1)S(1)} %collective-permute-done.12.refs_2_, f32[256,768]{1,0:T(8,128)S(1)} %beams_3.1.refs_3_, ...), custom_call_target="tpu_custom_call" | custom-call | tf_op jit(solution)/shard_map/finish/pallas_call | solution.py:252
  (28 shorter events, 4.0 us)
Async XLA Ops:
  1.5 6.4 %collective-permute-start = (bf16[1,48,256]{2,1,0:T(8,128)(2,1)S(1)}, bf16[1,48,256]{2,1,0:T(8,128)(2,1)S(1)}, u32[]{:S(2)}, u32[]{:S(2)}) collective-permute-start(bf16[1,48,256]{2,1,0:T(8,128)(2,1)S(1)} %reshape.16.refs_0_), channel_id=1, source_target_pairs={{0,2},{2,0},{1,3},{3,1},{4,6},{6,4},{5,7},{7,5},{8,10},{10,8},{9,1... | collective-permute-start | bytes 73736 | tf_op jit(solution)/shard_map/ppermute | solution.py:292
  7.8 5.5 %collective-permute-start.1 = (bf16[2,48,256]{2,1,0:T(8,128)(2,1)S(1)}, bf16[2,48,256]{2,1,0:T(8,128)(2,1)S(1)}, u32[]{:S(2)}, u32[]{:S(2)}) collective-permute-start(bf16[2,48,256]{2,1,0:T(8,128)(2,1)S(1)} %join_1.1.refs_0_), channel_id=1, source_target_pairs={{0,16},{16,0},{1,17},{17,1},{2,18},{18,2},{3,19},{19,3},{4,20},{20... | collective-permute-start | bytes 147464 | tf_op jit(solution)/shard_map/ppermute | solution.py:296
  8.3 25.0 %collective-permute-start.7 = (s16[4,256,256]{2,1,0:T(8,128)(2,1)S(1)}, s16[4,256,256]{2,1,0:T(8,128)(2,1)S(1)}, u32[]{:S(2)}, u32[]{:S(2)}) collective-permute-start(s16[4,256,256]{2,1,0:T(8,128)(2,1)S(1)} %get-tuple-element.47), channel_id=1, source_target_pairs={{0,2},{1,3},{2,0},{3,1},{4,6},{5,7},{6,4},{7,5},{8,10},{9,11},{10,... | collective-permute-start | bytes 1572872 | tf_op jit(solution)/shard_map/ppermute | solution.py:286
  10.5 32.7 %collective-permute-start.8 = (s16[4,256,256]{2,1,0:T(8,128)(2,1)S(1)}, s16[4,256,256]{2,1,0:T(8,128)(2,1)S(1)}, u32[]{:S(2)}, u32[]{:S(2)}) collective-permute-start(s16[4,256,256]{2,1,0:T(8,128)(2,1)S(1)} %get-tuple-element.53), channel_id=1, source_target_pairs={{0,3},{1,2},{2,1},{3,0},{4,7},{5,6},{6,5},{7,4},{8,11},{9,10},{10,... | collective-permute-start | bytes 1572872 | tf_op jit(solution)/shard_map/ppermute | solution.py:286
  13.4 16.0 %collective-permute-start.2 = (bf16[4,48,256]{2,1,0:T(8,128)(2,1)S(1)}, bf16[4,48,256]{2,1,0:T(8,128)(2,1)S(1)}, u32[]{:S(2)}, u32[]{:S(2)}) collective-permute-start(bf16[4,48,256]{2,1,0:T(8,128)(2,1)S(1)} %join_2.1.after_ref.refs_0_), channel_id=1, source_target_pairs={{0,128},{32,160},{64,192},{96,224},{128,0},{160,32},{192,64},{224,... | collective-permute-start | bytes 294920 | tf_op jit(solution)/shard_map/ppermute | solution.py:289
  20.1 4.9 %collective-permute-start.3 = (s16[4,256,256]{2,1,0:T(8,128)(2,1)S(1)}, s16[4,256,256]{2,1,0:T(8,128)(2,1)S(1)}, u32[]{:S(2)}, u32[]{:S(2)}) collective-permute-start(s16[4,256,256]{2,1,0:T(8,128)(2,1)S(1)} %get-tuple-element.43), channel_id=1, source_target_pairs={{0,1},{1,0},{2,3},{3,2},{4,5},{5,4},{6,7},{7,6},{8,9},{9,8},{10,11... | collective-permute-start | bytes 1572872 | tf_op jit(solution)/shard_map/ppermute | solution.py:286
  29.4 8.8 %collective-permute-start.6 = (bf16[8,48,256]{2,1,0:T(8,128)(2,1)S(1)}, bf16[8,48,256]{2,1,0:T(8,128)(2,1)S(1)}, u32[]{:S(2)}, u32[]{:S(2)}) collective-permute-start(bf16[8,48,256]{2,1,0:T(8,128)(2,1)S(1)} %join_4.1.after_ref.refs_0_), channel_id=1, source_target_pairs={{0,64},{32,224},{64,128},{96,32},{128,192},{160,96},{192,0},{224,1... | collective-permute-start | bytes 589832 | tf_op jit(solution)/shard_map/ppermute | solution.py:289
  30.6 12.0 %collective-permute-start.5 = (bf16[8,48,256]{2,1,0:T(8,128)(2,1)S(1)}, bf16[8,48,256]{2,1,0:T(8,128)(2,1)S(1)}, u32[]{:S(2)}, u32[]{:S(2)}) collective-permute-start(bf16[8,48,256]{2,1,0:T(8,128)(2,1)S(1)} %join_4.1.after_ref.refs_0_), channel_id=1, source_target_pairs={{0,32},{32,64},{64,96},{96,128},{128,160},{160,192},{192,224},{224... | collective-permute-start | bytes 589832 | tf_op jit(solution)/shard_map/ppermute | solution.py:289
  30.7 12.0 %collective-permute-start.4 = (bf16[8,48,256]{2,1,0:T(8,128)(2,1)S(1)}, bf16[8,48,256]{2,1,0:T(8,128)(2,1)S(1)}, u32[]{:S(2)}, u32[]{:S(2)}) collective-permute-start(bf16[8,48,256]{2,1,0:T(8,128)(2,1)S(1)} %join_4.1.after_ref.refs_0_), channel_id=1, source_target_pairs={{0,224},{32,0},{64,32},{96,64},{128,96},{160,128},{192,160},{224,1... | collective-permute-start | bytes 589832 | tf_op jit(solution)/shard_map/ppermute | solution.py:289
  42.7 3.4 %collective-permute-start.9 = (bf16[32,48,256]{2,1,0:T(8,128)(2,1)S(1)}, bf16[32,48,256]{2,1,0:T(8,128)(2,1)S(1)}, u32[]{:S(2)}, u32[]{:S(2)}) collective-permute-start(bf16[32,48,256]{2,1,0:T(8,128)(2,1)S(1)} %join_8.1.source_ref.after_ref), channel_id=1, source_target_pairs={{0,1},{1,0},{2,3},{3,2},{4,5},{5,4},{6,7},{7,6},{8,9},{9,8},{10,11... | collective-permute-start | bytes 2359304 | tf_op jit(solution)/shard_map/ppermute | solution.py:309
  49.5 14.5 %collective-permute-start.10 = (bf16[264,768]{1,0:T(8,128)(2,1)S(1)}, bf16[264,768]{1,0:T(8,128)(2,1)S(1)}, u32[]{:S(2)}, u32[]{:S(2)}) collective-permute-start(bf16[264,768]{1,0:T(8,128)(2,1)S(1)} %beams_0.1.after_ref), channel_id=1, source_target_pairs={{0,8},{4,12},{8,0},{12,4},{1,9},{5,13},{9,1},{13,5},{2,10},{6,14},... | collective-permute-start | bytes 1216520 | tf_op jit(solution)/shard_map/ppermute | solution.py:323
  61.2 12.0 %copy-start = (s32[4,768]{1,0:T(4,128)S(1)}, s32[4,768]{1,0:T(4,128)}, u32[]{:S(2)}) copy-start(s32[4,768]{1,0:T(4,128)} %constant.54.clone.refs_8_) | copy-start | bytes 36868
  61.3 11.9 %collective-permute-start.11 = (bf16[264,768]{1,0:T(8,128)(2,1)S(1)}, bf16[264,768]{1,0:T(8,128)(2,1)S(1)}, u32[]{:S(2)}, u32[]{:S(2)}) collective-permute-start(bf16[264,768]{1,0:T(8,128)(2,1)S(1)} %beams_1.1), channel_id=1, source_target_pairs={{0,4},{4,8},{8,12},{12,0},{1,5},{5,9},{9,13},{13,1},{2,6},{6,10},{... | collective-permute-start | bytes 1216520 | tf_op jit(solution)/shard_map/ppermute | solution.py:323
  61.6 11.6 %collective-permute-start.12 = (bf16[264,768]{1,0:T(8,128)(2,1)S(1)}, bf16[264,768]{1,0:T(8,128)(2,1)S(1)}, u32[]{:S(2)}, u32[]{:S(2)}) collective-permute-start(bf16[264,768]{1,0:T(8,128)(2,1)S(1)} %beams_2.1), channel_id=1, source_target_pairs={{0,12},{4,0},{8,4},{12,8},{1,13},{5,1},{9,5},{13,9},{2,14},{6,2},{... | collective-permute-start | bytes 1216520 | tf_op jit(solution)/shard_map/ppermute | solution.py:323
